TPU v7x, 1024 devices: a whole 4x8x16 slice. The times are simulated.
1024 devices in a mesh: group: 4 (over x), tile: 256 (over z, y, core).
Axes of the slice: x: 4, y: 8, z: 16, core: 2. Of those that a mesh axis runs over, the one named last changes fastest.
Arguments:
- facies: int32 [256, 2048, 256], P('group', 'tile'), may hold values from 0 to 7
- perm_table: float32 [8], replicated, may hold values from 0.05 to 10
- source: float32 [256, 2048, 256], P('group', 'tile'), may hold values from -6 to 6
Outputs:
- head: float32 [256, 2048, 256], P('group', 'tile')
All inputs are finite; a program needn't handle non-finite values.
Results may differ from a plain program's by a relative error of at most 0.0003.
Values sent between devices are 32-bit elements; how exact they have to be, the bound alone decides.
No kernel may reach another device: no remote copies, remote signals or barrier semaphores. Data moves between devices by JAX's collectives and lax.ppermute only.
A program may use at most 32 MiB of HBM per device.

v0:
```python
import jax
import jax.numpy as jnp
from jax import lax
from jax.sharding import PartitionSpec as P

COARSE_ITERS = 3


relax_weight = 0.8


def padded(cells, sides, width):
    for axis, dim in sides:
        count = lax.axis_size(axis)
        ends = count - 1
        head = lax.slice_in_dim(cells, 0, width, axis=dim)
        tail = lax.slice_in_dim(cells, cells.shape[dim] - width, cells.shape[dim], axis=dim)
        cells = jnp.concatenate(
            [
                lax.ppermute(tail, axis, [(i, (i + 1) % count) for i in range(ends)]),
                cells,
                lax.ppermute(head, axis, [((i + 1) % count, i) for i in range(ends)]),
            ],
            axis=dim,
        )
    return cells


def swapped(block, axis, apart):
    count = lax.axis_size(axis)
    route = []
    for low in range(count):
        high = low | 1 << apart
        if high != low and high < count:
            route += [(low, high), (high, low)]
    return lax.ppermute(block, axis, route)


def harmonic(left_perm, right_perm):
    pair_sum = left_perm + right_perm
    positive = pair_sum > 0.0
    return jnp.where(
        positive, 2.0 * left_perm * right_perm / jnp.where(positive, pair_sum, 1.0), 0.0
    )


def face_fields(perm_ext, storage):
    perm_mid = perm_ext[1:-1, 1:-1]
    perm_z = jnp.pad(perm_mid, ((0, 0), (0, 0), (1, 1)))
    neighbours = [
        perm_ext[2:, 1:-1],
        perm_ext[:-2, 1:-1],
        perm_ext[1:-1, 2:],
        perm_ext[1:-1, :-2],
        perm_z[:, :, 2:],
        perm_z[:, :, :-2],
    ]
    faces = tuple((harmonic(perm_mid, nb) for nb in neighbours))
    diagonal = storage + jnp.zeros_like(perm_mid)
    for trans in faces:
        diagonal = diagonal + trans
    return (faces, diagonal)


def operator(head_ext, faces, storage):
    head_mid = head_ext[1:-1, 1:-1]
    head_z = jnp.pad(head_mid, ((0, 0), (0, 0), (1, 1)))
    neighbours = [
        head_ext[2:, 1:-1],
        head_ext[:-2, 1:-1],
        head_ext[1:-1, 2:],
        head_ext[1:-1, :-2],
        head_z[:, :, 2:],
        head_z[:, :, :-2],
    ]
    flux_sum = storage * head_mid
    for trans, head_nb in zip(faces, neighbours):
        flux_sum = flux_sum + trans * (head_mid - head_nb)
    return flux_sum


def sweep(head_ext, faces, diagonal, rhs_mid, storage):
    flux_sum = operator(head_ext, faces, storage)
    return head_ext[1:-1, 1:-1] + relax_weight * (rhs_mid - flux_sum) / diagonal


def shifted(values, stride, fill):
    length = values.shape[1]
    if stride > 0:
        pad_block = jnp.full_like(values[:, :stride], fill)
        return jnp.concatenate([pad_block, values[:, : length - stride]], axis=1)
    stride = -stride
    pad_block = jnp.full_like(values[:, :stride], fill)
    return jnp.concatenate([values[:, stride:], pad_block], axis=1)


def line_solve(lower, diagonal, upper, rhs_now):
    length = rhs_now.shape[1]
    stride = 1
    while stride < length:
        low_prev = shifted(lower, stride, 0.0)
        diag_prev = shifted(diagonal, stride, 1.0)
        up_prev = shifted(upper, stride, 0.0)
        rhs_prev = shifted(rhs_now, stride, 0.0)
        low_next = shifted(lower, -stride, 0.0)
        diag_next = shifted(diagonal, -stride, 1.0)
        up_next = shifted(upper, -stride, 0.0)
        rhs_next = shifted(rhs_now, -stride, 0.0)
        alpha = -lower / diag_prev
        gamma = -upper / diag_next
        diagonal = diagonal + alpha * up_prev + gamma * low_next
        rhs_now = rhs_now + alpha * rhs_prev + gamma * rhs_next
        lower = alpha * low_prev
        upper = gamma * up_next
        stride = stride * 2
    return rhs_now / diagonal


def coarse_solve(coarse_rhs, link_x, link_y, store_brick):
    zero_row = jnp.zeros_like(coarse_rhs[:1])
    zero_col = jnp.zeros_like(coarse_rhs[:, :1])
    link_x_prev = jnp.concatenate([zero_row, link_x[:-1]], axis=0)
    link_y_prev = jnp.concatenate([zero_col, link_y[:, :-1]], axis=1)
    diagonal = store_brick + link_x + link_x_prev + link_y + link_y_prev
    lower = -link_y_prev
    upper = -link_y
    correction = jnp.zeros_like(coarse_rhs)
    for sweep_no in range(COARSE_ITERS):
        before = jnp.concatenate([zero_row, correction[:-1]], axis=0)
        after = jnp.concatenate([correction[1:], zero_row], axis=0)
        rhs_now = coarse_rhs + link_x_prev * before + link_x * after
        correction = line_solve(lower, diagonal, upper, rhs_now)
    return correction


def rim(field):
    return padded(field, (("group", 0), ("tile", 1)), 1)


def brick_links(perm_ext, width, cells_x, cells_y):
    link_x = jnp.sum(
        harmonic(
            perm_ext[width + cells_x - 1, width : width + cells_y],
            perm_ext[width + cells_x, width : width + cells_y],
        )
    )
    link_y = jnp.sum(
        harmonic(
            perm_ext[width : width + cells_x, width + cells_y - 1],
            perm_ext[width : width + cells_x, width + cells_y],
        )
    )
    return (link_x, link_y)


def merge_bits(merged, axis_bits, position, dim, swap_fn):
    for bit in range(axis_bits):
        partner = swap_fn(merged, bit)
        low_side = position // (1 << bit) % 2 == 0
        merged = jnp.where(
            low_side,
            jnp.concatenate([merged, partner], axis=dim),
            jnp.concatenate([partner, merged], axis=dim),
        )
    return merged


def on_device(facies, perm_table, source):
    cells_x, cells_y, cells_z = source.shape
    storage = 0.01 / cells_y
    perm = jnp.zeros(source.shape, jnp.float32)
    for facies_id in range(perm_table.shape[0]):
        perm = jnp.where(facies == facies_id, perm_table[facies_id], perm)
    group_pos = lax.axis_index("group")
    tile_pos = lax.axis_index("tile")
    perm_ext = padded(perm, (("group", 0), ("tile", 1)), 1)
    faces_all, diag_all = face_fields(perm_ext, storage)
    head_one = sweep(jnp.zeros_like(perm_ext), faces_all, diag_all, source, storage)
    head_two = sweep(rim(head_one), faces_all, diag_all, source, storage)
    flux_sum = operator(rim(head_two), faces_all, storage)
    link_x, link_y = brick_links(perm_ext, 1, cells_x, cells_y)
    resid = source - flux_sum
    own_sums = jnp.stack([jnp.sum(resid), link_x, link_y]).reshape(3, 1, 1)
    groups = lax.axis_size("group")
    tiles = lax.axis_size("tile")

    def tile_swap(merged, bit):
        return swapped(merged, "tile", bit)

    def group_swap(merged, bit):
        return swapped(merged, "group", bit)

    whole = merge_bits(own_sums, tiles.bit_length() - 1, tile_pos, 2, tile_swap)
    whole = merge_bits(whole, groups.bit_length() - 1, group_pos, 1, group_swap)
    correction = coarse_solve(whole[0], whole[1], whole[2], storage * cells_x * cells_y * cells_z)
    own_shift = lax.dynamic_slice(correction, (group_pos, tile_pos), (1, 1))[0, 0]
    head_three = head_two + own_shift
    head_four = sweep(rim(head_three), faces_all, diag_all, source, storage)
    return sweep(rim(head_four), faces_all, diag_all, source, storage)


def solution(mesh):
    placed = (P("group", "tile", None), P(), P("group", "tile", None))
    return jax.shard_map(
        on_device, mesh=mesh, in_specs=placed, out_specs=P("group", "tile", None), check_vma=False
    )
```

profile of v0, /device:TPU:1, one launch (start us, length us, event | category | flops | bytes accessed | tf_op | source)
XLA Modules:
  0.0 208.3 jit_solution(1963238975387554599)
XLA Ops:
  0.0 1.6 fusion.164
  1.6 6.3 %select_select_fusion = f32[64,8,256]{2,0,1:T(8,128)S(1)} fusion(s32[64,8,256]{2,1,0:T(8,128)} %param.3, f32[]{:T(128)} %bitcast.7, f32[]{:T(128)} %bitcast.6, f32[]{:T(128)} %bitcast.5, f32[]{:T(128)} %bitcast.4, f32[]{:T(128)} %bitcast.3, f32[]{:T(128)} %bitcast.2, f32[]{:T(128)} %bitcast.1, f32[]{:T(128)} %bitcast), kind=kLoop, calls=%fused_computation.170 | loop fusion | flops 2097152 | bytes 1048608 | tf_op jit(solution)/shard_map/jit(_where)/select_n | solution.py:173
  7.9 1.3 collective-permute-start
  9.2 4.6 %collective-permute-start.1 = (f32[1,8,256]{2,0,1:T(1,128)S(1)}, f32[1,8,256]{2,0,1:T(1,128)S(1)}, u32[]{:S(2)}, u32[]{:S(2)}) collective-permute-start(f32[1,8,256]{2,0,1:T(1,128)S(1)} %get-tuple-element.63), channel_id=1, source_target_pairs={{0,256},{256,512},{512,768},{1,257},{257,513},{513,769},{2,258},{2... | collective-permute-start | bytes 24584 | tf_op jit(solution)/shard_map/ppermute | solution.py:20
  14.6 5.1 %collective-permute-start.3 = (f32[66,1,256]{2,0,1:T(8,128)S(1)}, f32[66,1,256]{2,0,1:T(8,128)S(1)}, u32[]{:S(2)}, u32[]{:S(2)}) collective-permute-start(f32[66,1,256]{2,0,1:T(8,128)S(1)} %get-tuple-element.53), channel_id=1, source_target_pairs={{0,1},{1,2},{2,3},{3,4},{4,5},{5,6},{6,7},{7,8},{8,9},{9,10},{10,1... | collective-permute-start | bytes 202760 | tf_op jit(solution)/shard_map/ppermute | solution.py:20
  19.7 12.8 %collective-permute-start.2 = (f32[66,1,256]{2,0,1:T(8,128)S(1)}, f32[66,1,256]{2,0,1:T(8,128)S(1)}, u32[]{:S(2)}, u32[]{:S(2)}) collective-permute-start(f32[66,1,256]{2,0,1:T(8,128)S(1)} %get-tuple-element.54), channel_id=1, source_target_pairs={{1,0},{2,1},{3,2},{4,3},{5,4},{6,5},{7,6},{8,7},{9,8},{10,9},{11,1... | collective-permute-start | bytes 202760 | tf_op jit(solution)/shard_map/ppermute | solution.py:22
  33.4 1.4 fusion.50
  34.9 3.9 %collective-permute-start.5 = (f32[1,8,256]{2,0,1:T(1,128)S(1)}, f32[1,8,256]{2,0,1:T(1,128)S(1)}, u32[]{:S(2)}, u32[]{:S(2)}) collective-permute-start(f32[1,8,256]{2,0,1:T(1,128)S(1)} %get-tuple-element.61), channel_id=1, source_target_pairs={{0,256},{256,512},{512,768},{1,257},{257,513},{513,769},{2,258},{2... | collective-permute-start | bytes 24584 | tf_op jit(solution)/shard_map/ppermute | solution.py:20
  38.8 1.3 collective-permute-start.4
  40.1 3.1 %collective-permute-done.4 = f32[1,8,256]{2,0,1:T(1,128)S(1)} collective-permute-done((f32[1,8,256]{2,0,1:T(1,128)S(1)}, f32[1,8,256]{2,0,1:T(1,128)S(1)}, u32[]{:S(2)}, u32[]{:S(2)}) %collective-permute-start.4) | collective-permute-done | bytes 8224 | tf_op jit(solution)/shard_map/ppermute | solution.py:22
  43.2 3.7 %collective-permute-start.6 = (f32[66,1,256]{2,0,1:T(8,128)S(1)}, f32[66,1,256]{2,0,1:T(8,128)S(1)}, u32[]{:S(2)}, u32[]{:S(2)}) collective-permute-start(f32[66,1,256]{2,0,1:T(8,128)S(1)} %get-tuple-element.51), channel_id=1, source_target_pairs={{1,0},{2,1},{3,2},{4,3},{5,4},{6,5},{7,6},{8,7},{9,8},{10,9},{11,1... | collective-permute-start | bytes 202760 | tf_op jit(solution)/shard_map/ppermute | solution.py:22
  46.9 1.9 collective-permute-start.7
  50.2 1.9 fusion.13
  52.1 1.9 collective-permute-start.9
  54.0 1.3 collective-permute-start.8
  56.0 2.4 %collective-permute-done.8 = f32[1,8,256]{2,0,1:T(1,128)S(1)} collective-permute-done((f32[1,8,256]{2,0,1:T(1,128)S(1)}, f32[1,8,256]{2,0,1:T(1,128)S(1)}, u32[]{:S(2)}, u32[]{:S(2)}) %collective-permute-start.8) | collective-permute-done | bytes 8224 | tf_op jit(solution)/shard_map/ppermute | solution.py:22
  58.4 3.1 %collective-permute-start.10 = (f32[66,1,256]{2,0,1:T(8,128)S(1)}, f32[66,1,256]{2,0,1:T(8,128)S(1)}, u32[]{:S(2)}, u32[]{:S(2)}) collective-permute-start(f32[66,1,256]{2,0,1:T(8,128)S(1)} %get-tuple-element.49), channel_id=1, source_target_pairs={{1,0},{2,1},{3,2},{4,3},{5,4},{6,5},{7,6},{8,7},{9,8},{10,9},{11,1... | collective-permute-start | bytes 202760 | tf_op jit(solution)/shard_map/ppermute | solution.py:22
  61.6 4.5 %collective-permute-start.11 = (f32[66,1,256]{2,0,1:T(8,128)S(1)}, f32[66,1,256]{2,0,1:T(8,128)S(1)}, u32[]{:S(2)}, u32[]{:S(2)}) collective-permute-start(f32[66,1,256]{2,0,1:T(8,128)S(1)} %get-tuple-element.50), channel_id=1, source_target_pairs={{0,1},{1,2},{2,3},{3,4},{4,5},{5,6},{6,7},{7,8},{8,9},{9,10},{10,1... | collective-permute-start | bytes 202760 | tf_op jit(solution)/shard_map/ppermute | solution.py:20
  67.5 2.3 %fusion.21 = f32[]{:T(128)} fusion(f32[64,8,256]{2,0,1:T(8,128)S(1)} %get-tuple-element.44, f32[64,8,256]{2,0,1:T(8,128)S(1)} %fusion.13, f32[64,8,256]{2,0,1:T(8,128)S(1)} %get-tuple-element.43, f32[66,1,256]{2,0,1:T(8,128)S(1)} %collective-permute-done.11, f32[1,8,256]{2,0,1:T(1,128)S(1)} %collective-permute-done.8, ...), kind=kLoop, calls=%fused_computation.45 | loop fusion | flops 8126463 | bytes 2924548 | tf_op jit(solution)/shard_map/reduce_sum | solution.py:183
  69.8 2.0 fusion.168
  71.8 2.0 fusion.169
  73.8 1.9 collective-permute-start.12
  76.8 4.1 %collective-permute-start.13 = (f32[3,1,2]{0,2,1:T(2,128)S(1)}, f32[3,1,2]{0,2,1:T(2,128)S(1)}, u32[]{:S(2)}, u32[]{:S(2)}) collective-permute-start(f32[3,1,2]{0,2,1:T(2,128)S(1)} %maximum_select_fusion.10), channel_id=1, source_target_pairs={{0,2},{2,0},{1,3},{3,1},{4,6},{6,4},{5,7},{7,5},{8,10},{10,8},{9,1... | collective-permute-start | bytes 80 | tf_op jit(solution)/shard_map/ppermute | solution.py:36
  82.0 3.2 %collective-permute-start.14 = (f32[3,1,4]{0,2,1:T(4,128)S(1)}, f32[3,1,4]{0,2,1:T(4,128)S(1)}, u32[]{:S(2)}, u32[]{:S(2)}) collective-permute-start(f32[3,1,4]{0,2,1:T(4,128)S(1)} %maximum_select_fusion.4), channel_id=1, source_target_pairs={{0,4},{4,0},{1,5},{5,1},{2,6},{6,2},{3,7},{7,3},{8,12},{12,8},{9,1... | collective-permute-start | bytes 152 | tf_op jit(solution)/shard_map/ppermute | solution.py:36
  85.2 2.0 collective-permute-done.14
  87.5 5.7 %collective-permute-start.15 = (f32[3,1,8]{2,1,0:T(1,128)S(1)}, f32[3,1,8]{2,1,0:T(1,128)S(1)}, u32[]{:S(2)}, u32[]{:S(2)}) collective-permute-start(f32[3,1,8]{2,1,0:T(1,128)S(1)} %broadcast_select_fusion.5), channel_id=1, source_target_pairs={{0,8},{8,0},{1,9},{9,1},{2,10},{10,2},{3,11},{11,3},{4,12},{12,4},... | collective-permute-start | bytes 296 | tf_op jit(solution)/shard_map/ppermute | solution.py:36
  93.1 2.5 %collective-permute-done.15 = f32[3,1,8]{2,1,0:T(1,128)S(1)} collective-permute-done((f32[3,1,8]{2,1,0:T(1,128)S(1)}, f32[3,1,8]{2,1,0:T(1,128)S(1)}, u32[]{:S(2)}, u32[]{:S(2)}) %collective-permute-start.15) | collective-permute-done | bytes 128 | tf_op jit(solution)/shard_map/ppermute | solution.py:36
  95.8 5.8 %collective-permute-start.16 = (f32[3,1,16]{2,1,0:T(1,128)S(1)}, f32[3,1,16]{2,1,0:T(1,128)S(1)}, u32[]{:S(2)}, u32[]{:S(2)}) collective-permute-start(f32[3,1,16]{2,1,0:T(1,128)S(1)} %broadcast_select_fusion.4), channel_id=1, source_target_pairs={{0,16},{16,0},{1,17},{17,1},{2,18},{18,2},{3,19},{19,3},{4,20},{20... | collective-permute-start | bytes 584 | tf_op jit(solution)/shard_map/ppermute | solution.py:36
  102.6 5.8 %collective-permute-start.17 = (f32[3,1,32]{2,1,0:T(1,128)S(1)}, f32[3,1,32]{2,1,0:T(1,128)S(1)}, u32[]{:S(2)}, u32[]{:S(2)}) collective-permute-start(f32[3,1,32]{2,1,0:T(1,128)S(1)} %broadcast_select_fusion.3), channel_id=1, source_target_pairs={{0,32},{32,0},{1,33},{33,1},{2,34},{34,2},{3,35},{35,3},{4,36},{36... | collective-permute-start | bytes 1160 | tf_op jit(solution)/shard_map/ppermute | solution.py:36
  109.4 13.3 %collective-permute-start.18 = (f32[3,1,64]{2,1,0:T(1,128)S(1)}, f32[3,1,64]{2,1,0:T(1,128)S(1)}, u32[]{:S(2)}, u32[]{:S(2)}) collective-permute-start(f32[3,1,64]{2,1,0:T(1,128)S(1)} %broadcast_select_fusion.2), channel_id=1, source_target_pairs={{0,64},{64,0},{1,65},{65,1},{2,66},{66,2},{3,67},{67,3},{4,68},{68... | collective-permute-start | bytes 2312 | tf_op jit(solution)/shard_map/ppermute | solution.py:36
  123.8 15.7 %collective-permute-start.19 = (f32[3,1,128]{2,1,0:T(1,128)S(1)}, f32[3,1,128]{2,1,0:T(1,128)S(1)}, u32[]{:S(2)}, u32[]{:S(2)}) collective-permute-start(f32[3,1,128]{2,1,0:T(1,128)S(1)} %broadcast_select_fusion.1), channel_id=1, source_target_pairs={{0,128},{128,0},{1,129},{129,1},{2,130},{130,2},{3,131},{131,3},{4... | collective-permute-start | bytes 4616 | tf_op jit(solution)/shard_map/ppermute | solution.py:36
  140.4 3.1 %collective-permute-start.20 = (f32[3,1,256]{2,1,0:T(1,128)S(1)}, f32[3,1,256]{2,1,0:T(1,128)S(1)}, u32[]{:S(2)}, u32[]{:S(2)}) collective-permute-start(f32[3,1,256]{2,1,0:T(1,128)S(1)} %broadcast_select_fusion), channel_id=1, source_target_pairs={{0,256},{256,0},{512,768},{768,512},{1,257},{257,1},{513,769},{769... | collective-permute-start | bytes 9224 | tf_op jit(solution)/shard_map/ppermute | solution.py:36
  143.6 1.5 collective-permute-done.20
  145.1 3.2 %collective-permute-start.21 = (f32[3,2,256]{2,1,0:T(2,128)S(1)}, f32[3,2,256]{2,1,0:T(2,128)S(1)}, u32[]{:S(2)}, u32[]{:S(2)}) collective-permute-start(f32[3,2,256]{2,1,0:T(2,128)S(1)} %maximum_select_fusion.1), channel_id=1, source_target_pairs={{0,512},{512,0},{256,768},{768,256},{1,513},{513,1},{257,769},{769... | collective-permute-start | bytes 18440 | tf_op jit(solution)/shard_map/ppermute | solution.py:36
  148.3 2.6 %collective-permute-done.21 = f32[3,2,256]{2,1,0:T(2,128)S(1)} collective-permute-done((f32[3,2,256]{2,1,0:T(2,128)S(1)}, f32[3,2,256]{2,1,0:T(2,128)S(1)}, u32[]{:S(2)}, u32[]{:S(2)}) %collective-permute-start.21) | collective-permute-done | bytes 6176 | tf_op jit(solution)/shard_map/ppermute | solution.py:36
  163.9 3.1 %collective-permute-start.23 = (f32[1,8,256]{2,0,1:T(1,128)S(1)}, f32[1,8,256]{2,0,1:T(1,128)S(1)}, u32[]{:S(2)}, u32[]{:S(2)}) collective-permute-start(f32[1,8,256]{2,0,1:T(1,128)S(1)} %get-tuple-element.57), channel_id=1, source_target_pairs={{0,256},{256,512},{512,768},{1,257},{257,513},{513,769},{2,258},{2... | collective-permute-start | bytes 24584 | tf_op jit(solution)/shard_map/ppermute | solution.py:20
  167.0 1.3 collective-permute-start.22
  168.4 3.1 %collective-permute-done.22 = f32[1,8,256]{2,0,1:T(1,128)S(1)} collective-permute-done((f32[1,8,256]{2,0,1:T(1,128)S(1)}, f32[1,8,256]{2,0,1:T(1,128)S(1)}, u32[]{:S(2)}, u32[]{:S(2)}) %collective-permute-start.22) | collective-permute-done | bytes 8224 | tf_op jit(solution)/shard_map/ppermute | solution.py:22
  171.5 13.4 %collective-permute-start.24 = (f32[66,1,256]{2,0,1:T(8,128)S(1)}, f32[66,1,256]{2,0,1:T(8,128)S(1)}, u32[]{:S(2)}, u32[]{:S(2)}) collective-permute-start(f32[66,1,256]{2,0,1:T(8,128)S(1)} %get-tuple-element.47), channel_id=1, source_target_pairs={{1,0},{2,1},{3,2},{4,3},{5,4},{6,5},{7,6},{8,7},{9,8},{10,9},{11,1... | collective-permute-start | bytes 202760 | tf_op jit(solution)/shard_map/ppermute | solution.py:22
  184.9 1.9 collective-permute-start.25
  186.8 1.4 collective-permute-done.25
  188.2 1.9 fusion.31
  190.2 1.7 collective-permute-start.27
  193.1 3.1 %collective-permute-done.26 = f32[1,8,256]{2,0,1:T(1,128)S(1)} collective-permute-done((f32[1,8,256]{2,0,1:T(1,128)S(1)}, f32[1,8,256]{2,0,1:T(1,128)S(1)}, u32[]{:S(2)}, u32[]{:S(2)}) %collective-permute-start.26) | collective-permute-done | bytes 8224 | tf_op jit(solution)/shard_map/ppermute | solution.py:22
  196.2 3.3 %collective-permute-start.28 = (f32[66,1,256]{2,0,1:T(8,128)S(1)}, f32[66,1,256]{2,0,1:T(8,128)S(1)}, u32[]{:S(2)}, u32[]{:S(2)}) collective-permute-start(f32[66,1,256]{2,0,1:T(8,128)S(1)} %get-tuple-element.45), channel_id=1, source_target_pairs={{1,0},{2,1},{3,2},{4,3},{5,4},{6,5},{7,6},{8,7},{9,8},{10,9},{11,1... | collective-permute-start | bytes 202760 | tf_op jit(solution)/shard_map/ppermute | solution.py:22
  199.6 4.3 %collective-permute-start.29 = (f32[66,1,256]{2,0,1:T(8,128)S(1)}, f32[66,1,256]{2,0,1:T(8,128)S(1)}, u32[]{:S(2)}, u32[]{:S(2)}) collective-permute-start(f32[66,1,256]{2,0,1:T(8,128)S(1)} %get-tuple-element.46), channel_id=1, source_target_pairs={{0,1},{1,2},{2,3},{3,4},{4,5},{5,6},{6,7},{7,8},{8,9},{9,10},{10,1... | collective-permute-start | bytes 202760 | tf_op jit(solution)/shard_map/ppermute | solution.py:20
  204.0 1.3 collective-permute-done.29
  205.3 1.9 fusion.41
  (160 shorter events, 24.4 us)
Async XLA Ops:
  7.9 5.9 %collective-permute-start = (f32[1,8,256]{2,1,0:T(8,128)S(1)}, f32[1,8,256]{2,1,0:T(8,128)S(1)}, u32[]{:S(2)}, u32[]{:S(2)}) collective-permute-start(f32[1,8,256]{2,1,0:T(8,128)S(1)} %copy.280), channel_id=1, source_target_pairs={{256,0},{512,256},{768,512},{257,1},{513,257},{769,513},{258,2},{5... | collective-permute-start | bytes 24584 | tf_op jit(solution)/shard_map/ppermute | solution.py:22
  9.2 5.4 %collective-permute-start.1 = (f32[1,8,256]{2,0,1:T(1,128)S(1)}, f32[1,8,256]{2,0,1:T(1,128)S(1)}, u32[]{:S(2)}, u32[]{:S(2)}) collective-permute-start(f32[1,8,256]{2,0,1:T(1,128)S(1)} %get-tuple-element.63), channel_id=1, source_target_pairs={{0,256},{256,512},{512,768},{1,257},{257,513},{513,769},{2,258},{2... | collective-permute-start | bytes 24584 | tf_op jit(solution)/shard_map/ppermute | solution.py:20
  13.8 19.6 %copy-start = (f32[64,8,256]{2,1,0:T(8,128)S(1)}, f32[64,8,256]{2,1,0:T(8,128)}, u32[]{:S(2)}) copy-start(f32[64,8,256]{2,1,0:T(8,128)} %param.5) | copy-start | bytes 1572868
  14.6 17.9 %collective-permute-start.3 = (f32[66,1,256]{2,0,1:T(8,128)S(1)}, f32[66,1,256]{2,0,1:T(8,128)S(1)}, u32[]{:S(2)}, u32[]{:S(2)}) collective-permute-start(f32[66,1,256]{2,0,1:T(8,128)S(1)} %get-tuple-element.53), channel_id=1, source_target_pairs={{0,1},{1,2},{2,3},{3,4},{4,5},{5,6},{6,7},{7,8},{8,9},{9,10},{10,1... | collective-permute-start | bytes 202760 | tf_op jit(solution)/shard_map/ppermute | solution.py:20
  19.7 13.7 %collective-permute-start.2 = (f32[66,1,256]{2,0,1:T(8,128)S(1)}, f32[66,1,256]{2,0,1:T(8,128)S(1)}, u32[]{:S(2)}, u32[]{:S(2)}) collective-permute-start(f32[66,1,256]{2,0,1:T(8,128)S(1)} %get-tuple-element.54), channel_id=1, source_target_pairs={{1,0},{2,1},{3,2},{4,3},{5,4},{6,5},{7,6},{8,7},{9,8},{10,9},{11,1... | collective-permute-start | bytes 202760 | tf_op jit(solution)/shard_map/ppermute | solution.py:22
  34.9 5.2 %collective-permute-start.5 = (f32[1,8,256]{2,0,1:T(1,128)S(1)}, f32[1,8,256]{2,0,1:T(1,128)S(1)}, u32[]{:S(2)}, u32[]{:S(2)}) collective-permute-start(f32[1,8,256]{2,0,1:T(1,128)S(1)} %get-tuple-element.61), channel_id=1, source_target_pairs={{0,256},{256,512},{512,768},{1,257},{257,513},{513,769},{2,258},{2... | collective-permute-start | bytes 24584 | tf_op jit(solution)/shard_map/ppermute | solution.py:20
  38.8 4.4 %collective-permute-start.4 = (f32[1,8,256]{2,0,1:T(1,128)S(1)}, f32[1,8,256]{2,0,1:T(1,128)S(1)}, u32[]{:S(2)}, u32[]{:S(2)}) collective-permute-start(f32[1,8,256]{2,0,1:T(1,128)S(1)} %get-tuple-element.62), channel_id=1, source_target_pairs={{256,0},{512,256},{768,512},{257,1},{513,257},{769,513},{258,2},{5... | collective-permute-start | bytes 24584 | tf_op jit(solution)/shard_map/ppermute | solution.py:22
  43.2 5.8 %collective-permute-start.6 = (f32[66,1,256]{2,0,1:T(8,128)S(1)}, f32[66,1,256]{2,0,1:T(8,128)S(1)}, u32[]{:S(2)}, u32[]{:S(2)}) collective-permute-start(f32[66,1,256]{2,0,1:T(8,128)S(1)} %get-tuple-element.51), channel_id=1, source_target_pairs={{1,0},{2,1},{3,2},{4,3},{5,4},{6,5},{7,6},{8,7},{9,8},{10,9},{11,1... | collective-permute-start | bytes 202760 | tf_op jit(solution)/shard_map/ppermute | solution.py:22
  46.9 3.3 %collective-permute-start.7 = (f32[66,1,256]{2,0,1:T(8,128)S(1)}, f32[66,1,256]{2,0,1:T(8,128)S(1)}, u32[]{:S(2)}, u32[]{:S(2)}) collective-permute-start(f32[66,1,256]{2,0,1:T(8,128)S(1)} %get-tuple-element.52), channel_id=1, source_target_pairs={{0,1},{1,2},{2,3},{3,4},{4,5},{5,6},{6,7},{7,8},{8,9},{9,10},{10,1... | collective-permute-start | bytes 202760 | tf_op jit(solution)/shard_map/ppermute | solution.py:20
  52.1 3.9 %collective-permute-start.9 = (f32[1,8,256]{2,0,1:T(1,128)S(1)}, f32[1,8,256]{2,0,1:T(1,128)S(1)}, u32[]{:S(2)}, u32[]{:S(2)}) collective-permute-start(f32[1,8,256]{2,0,1:T(1,128)S(1)} %get-tuple-element.59), channel_id=1, source_target_pairs={{0,256},{256,512},{512,768},{1,257},{257,513},{513,769},{2,258},{2... | collective-permute-start | bytes 24584 | tf_op jit(solution)/shard_map/ppermute | solution.py:20
  54.0 4.4 %collective-permute-start.8 = (f32[1,8,256]{2,0,1:T(1,128)S(1)}, f32[1,8,256]{2,0,1:T(1,128)S(1)}, u32[]{:S(2)}, u32[]{:S(2)}) collective-permute-start(f32[1,8,256]{2,0,1:T(1,128)S(1)} %get-tuple-element.60), channel_id=1, source_target_pairs={{256,0},{512,256},{768,512},{257,1},{513,257},{769,513},{258,2},{5... | collective-permute-start | bytes 24584 | tf_op jit(solution)/shard_map/ppermute | solution.py:22
  58.4 8.3 %collective-permute-start.10 = (f32[66,1,256]{2,0,1:T(8,128)S(1)}, f32[66,1,256]{2,0,1:T(8,128)S(1)}, u32[]{:S(2)}, u32[]{:S(2)}) collective-permute-start(f32[66,1,256]{2,0,1:T(8,128)S(1)} %get-tuple-element.49), channel_id=1, source_target_pairs={{1,0},{2,1},{3,2},{4,3},{5,4},{6,5},{7,6},{8,7},{9,8},{10,9},{11,1... | collective-permute-start | bytes 202760 | tf_op jit(solution)/shard_map/ppermute | solution.py:22
  61.6 5.9 %collective-permute-start.11 = (f32[66,1,256]{2,0,1:T(8,128)S(1)}, f32[66,1,256]{2,0,1:T(8,128)S(1)}, u32[]{:S(2)}, u32[]{:S(2)}) collective-permute-start(f32[66,1,256]{2,0,1:T(8,128)S(1)} %get-tuple-element.50), channel_id=1, source_target_pairs={{0,1},{1,2},{2,3},{3,4},{4,5},{5,6},{6,7},{7,8},{8,9},{9,10},{10,1... | collective-permute-start | bytes 202760 | tf_op jit(solution)/shard_map/ppermute | solution.py:20
  73.8 3.0 %collective-permute-start.12 = (f32[3,1,1]{0,2,1:T(1,128)S(1)}, f32[3,1,1]{0,2,1:T(1,128)S(1)}, u32[]{:S(2)}, u32[]{:S(2)}) collective-permute-start(f32[3,1,1]{0,2,1:T(1,128)S(1)} %fusion.169), channel_id=1, source_target_pairs={{0,1},{1,0},{2,3},{3,2},{4,5},{5,4},{6,7},{7,6},{8,9},{9,8},{10,11... | collective-permute-start | bytes 44 | tf_op jit(solution)/shard_map/ppermute | solution.py:36
  76.8 5.0 %collective-permute-start.13 = (f32[3,1,2]{0,2,1:T(2,128)S(1)}, f32[3,1,2]{0,2,1:T(2,128)S(1)}, u32[]{:S(2)}, u32[]{:S(2)}) collective-permute-start(f32[3,1,2]{0,2,1:T(2,128)S(1)} %maximum_select_fusion.10), channel_id=1, source_target_pairs={{0,2},{2,0},{1,3},{3,1},{4,6},{6,4},{5,7},{7,5},{8,10},{10,8},{9,1... | collective-permute-start | bytes 80 | tf_op jit(solution)/shard_map/ppermute | solution.py:36
  82.0 5.2 %collective-permute-start.14 = (f32[3,1,4]{0,2,1:T(4,128)S(1)}, f32[3,1,4]{0,2,1:T(4,128)S(1)}, u32[]{:S(2)}, u32[]{:S(2)}) collective-permute-start(f32[3,1,4]{0,2,1:T(4,128)S(1)} %maximum_select_fusion.4), channel_id=1, source_target_pairs={{0,4},{4,0},{1,5},{5,1},{2,6},{6,2},{3,7},{7,3},{8,12},{12,8},{9,1... | collective-permute-start | bytes 152 | tf_op jit(solution)/shard_map/ppermute | solution.py:36
  87.5 8.2 %collective-permute-start.15 = (f32[3,1,8]{2,1,0:T(1,128)S(1)}, f32[3,1,8]{2,1,0:T(1,128)S(1)}, u32[]{:S(2)}, u32[]{:S(2)}) collective-permute-start(f32[3,1,8]{2,1,0:T(1,128)S(1)} %broadcast_select_fusion.5), channel_id=1, source_target_pairs={{0,8},{8,0},{1,9},{9,1},{2,10},{10,2},{3,11},{11,3},{4,12},{12,4},... | collective-permute-start | bytes 296 | tf_op jit(solution)/shard_map/ppermute | solution.py:36
  95.8 6.8 %collective-permute-start.16 = (f32[3,1,16]{2,1,0:T(1,128)S(1)}, f32[3,1,16]{2,1,0:T(1,128)S(1)}, u32[]{:S(2)}, u32[]{:S(2)}) collective-permute-start(f32[3,1,16]{2,1,0:T(1,128)S(1)} %broadcast_select_fusion.4), channel_id=1, source_target_pairs={{0,16},{16,0},{1,17},{17,1},{2,18},{18,2},{3,19},{19,3},{4,20},{20... | collective-permute-start | bytes 584 | tf_op jit(solution)/shard_map/ppermute | solution.py:36
  102.6 6.8 %collective-permute-start.17 = (f32[3,1,32]{2,1,0:T(1,128)S(1)}, f32[3,1,32]{2,1,0:T(1,128)S(1)}, u32[]{:S(2)}, u32[]{:S(2)}) collective-permute-start(f32[3,1,32]{2,1,0:T(1,128)S(1)} %broadcast_select_fusion.3), channel_id=1, source_target_pairs={{0,32},{32,0},{1,33},{33,1},{2,34},{34,2},{3,35},{35,3},{4,36},{36... | collective-permute-start | bytes 1160 | tf_op jit(solution)/shard_map/ppermute | solution.py:36
  109.4 14.2 %collective-permute-start.18 = (f32[3,1,64]{2,1,0:T(1,128)S(1)}, f32[3,1,64]{2,1,0:T(1,128)S(1)}, u32[]{:S(2)}, u32[]{:S(2)}) collective-permute-start(f32[3,1,64]{2,1,0:T(1,128)S(1)} %broadcast_select_fusion.2), channel_id=1, source_target_pairs={{0,64},{64,0},{1,65},{65,1},{2,66},{66,2},{3,67},{67,3},{4,68},{68... | collective-permute-start | bytes 2312 | tf_op jit(solution)/shard_map/ppermute | solution.py:36
  123.8 16.7 %collective-permute-start.19 = (f32[3,1,128]{2,1,0:T(1,128)S(1)}, f32[3,1,128]{2,1,0:T(1,128)S(1)}, u32[]{:S(2)}, u32[]{:S(2)}) collective-permute-start(f32[3,1,128]{2,1,0:T(1,128)S(1)} %broadcast_select_fusion.1), channel_id=1, source_target_pairs={{0,128},{128,0},{1,129},{129,1},{2,130},{130,2},{3,131},{131,3},{4... | collective-permute-start | bytes 4616 | tf_op jit(solution)/shard_map/ppermute | solution.py:36
  140.4 4.6 %collective-permute-start.20 = (f32[3,1,256]{2,1,0:T(1,128)S(1)}, f32[3,1,256]{2,1,0:T(1,128)S(1)}, u32[]{:S(2)}, u32[]{:S(2)}) collective-permute-start(f32[3,1,256]{2,1,0:T(1,128)S(1)} %broadcast_select_fusion), channel_id=1, source_target_pairs={{0,256},{256,0},{512,768},{768,512},{1,257},{257,1},{513,769},{769... | collective-permute-start | bytes 9224 | tf_op jit(solution)/shard_map/ppermute | solution.py:36
  145.1 5.9 %collective-permute-start.21 = (f32[3,2,256]{2,1,0:T(2,128)S(1)}, f32[3,2,256]{2,1,0:T(2,128)S(1)}, u32[]{:S(2)}, u32[]{:S(2)}) collective-permute-start(f32[3,2,256]{2,1,0:T(2,128)S(1)} %maximum_select_fusion.1), channel_id=1, source_target_pairs={{0,512},{512,0},{256,768},{768,256},{1,513},{513,1},{257,769},{769... | collective-permute-start | bytes 18440 | tf_op jit(solution)/shard_map/ppermute | solution.py:36
  163.9 4.4 %collective-permute-start.23 = (f32[1,8,256]{2,0,1:T(1,128)S(1)}, f32[1,8,256]{2,0,1:T(1,128)S(1)}, u32[]{:S(2)}, u32[]{:S(2)}) collective-permute-start(f32[1,8,256]{2,0,1:T(1,128)S(1)} %get-tuple-element.57), channel_id=1, source_target_pairs={{0,256},{256,512},{512,768},{1,257},{257,513},{513,769},{2,258},{2... | collective-permute-start | bytes 24584 | tf_op jit(solution)/shard_map/ppermute | solution.py:20
  167.0 4.4 %collective-permute-start.22 = (f32[1,8,256]{2,0,1:T(1,128)S(1)}, f32[1,8,256]{2,0,1:T(1,128)S(1)}, u32[]{:S(2)}, u32[]{:S(2)}) collective-permute-start(f32[1,8,256]{2,0,1:T(1,128)S(1)} %get-tuple-element.58), channel_id=1, source_target_pairs={{256,0},{512,256},{768,512},{257,1},{513,257},{769,513},{258,2},{5... | collective-permute-start | bytes 24584 | tf_op jit(solution)/shard_map/ppermute | solution.py:22
  171.5 15.4 %collective-permute-start.24 = (f32[66,1,256]{2,0,1:T(8,128)S(1)}, f32[66,1,256]{2,0,1:T(8,128)S(1)}, u32[]{:S(2)}, u32[]{:S(2)}) collective-permute-start(f32[66,1,256]{2,0,1:T(8,128)S(1)} %get-tuple-element.47), channel_id=1, source_target_pairs={{1,0},{2,1},{3,2},{4,3},{5,4},{6,5},{7,6},{8,7},{9,8},{10,9},{11,1... | collective-permute-start | bytes 202760 | tf_op jit(solution)/shard_map/ppermute | solution.py:22
  184.9 3.3 %collective-permute-start.25 = (f32[66,1,256]{2,0,1:T(8,128)S(1)}, f32[66,1,256]{2,0,1:T(8,128)S(1)}, u32[]{:S(2)}, u32[]{:S(2)}) collective-permute-start(f32[66,1,256]{2,0,1:T(8,128)S(1)} %get-tuple-element.48), channel_id=1, source_target_pairs={{0,1},{1,2},{2,3},{3,4},{4,5},{5,6},{6,7},{7,8},{8,9},{9,10},{10,1... | collective-permute-start | bytes 202760 | tf_op jit(solution)/shard_map/ppermute | solution.py:20
  190.2 3.0 %collective-permute-start.27 = (f32[1,8,256]{2,0,1:T(1,128)S(1)}, f32[1,8,256]{2,0,1:T(1,128)S(1)}, u32[]{:S(2)}, u32[]{:S(2)}) collective-permute-start(f32[1,8,256]{2,0,1:T(1,128)S(1)} %get-tuple-element.55), channel_id=1, source_target_pairs={{0,256},{256,512},{512,768},{1,257},{257,513},{513,769},{2,258},{2... | collective-permute-start | bytes 24584 | tf_op jit(solution)/shard_map/ppermute | solution.py:20
  191.8 4.4 %collective-permute-start.26 = (f32[1,8,256]{2,0,1:T(1,128)S(1)}, f32[1,8,256]{2,0,1:T(1,128)S(1)}, u32[]{:S(2)}, u32[]{:S(2)}) collective-permute-start(f32[1,8,256]{2,0,1:T(1,128)S(1)} %get-tuple-element.56), channel_id=1, source_target_pairs={{256,0},{512,256},{768,512},{257,1},{513,257},{769,513},{258,2},{5... | collective-permute-start | bytes 24584 | tf_op jit(solution)/shard_map/ppermute | solution.py:22
  196.2 7.7 %collective-permute-start.28 = (f32[66,1,256]{2,0,1:T(8,128)S(1)}, f32[66,1,256]{2,0,1:T(8,128)S(1)}, u32[]{:S(2)}, u32[]{:S(2)}) collective-permute-start(f32[66,1,256]{2,0,1:T(8,128)S(1)} %get-tuple-element.45), channel_id=1, source_target_pairs={{1,0},{2,1},{3,2},{4,3},{5,4},{6,5},{7,6},{8,7},{9,8},{10,9},{11,1... | collective-permute-start | bytes 202760 | tf_op jit(solution)/shard_map/ppermute | solution.py:22
  199.6 5.7 %collective-permute-start.29 = (f32[66,1,256]{2,0,1:T(8,128)S(1)}, f32[66,1,256]{2,0,1:T(8,128)S(1)}, u32[]{:S(2)}, u32[]{:S(2)}) collective-permute-start(f32[66,1,256]{2,0,1:T(8,128)S(1)} %get-tuple-element.46), channel_id=1, source_target_pairs={{0,1},{1,2},{2,3},{3,4},{4,5},{5,6},{6,7},{7,8},{8,9},{9,10},{10,1... | collective-permute-start | bytes 202760 | tf_op jit(solution)/shard_map/ppermute | solution.py:20
where the time goes:
time: 212 us; the launch traced here: 208 us
  starting transfers between devices  137 us (65%)
  waiting for transfers between devices  32.2 us (15%)
  other arithmetic  26.7 us (13%)
  local copies, waits for them, and re-layouts  8.57 us (4%)
  between operations  3.41 us (2%)
    ppermute x10, starting transfers between devices, swapped(): return lax.ppermute(block, axis, route)  61.7 us
    ppermute x10, starting transfers between devices, padded(): lax.ppermute(head, axis, [((i + 1) % count, i) for i in range(ends)])  42.8 us
    ppermute x10, starting transfers between devices, padded(): lax.ppermute(tail, axis, [(i, (i + 1) % count) for i in range(ends)])  32.9 us
    ppermute x10, waiting for transfers between devices, swapped(): return lax.ppermute(block, axis, route)  14.2 us
    ppermute x10, waiting for transfers between devices, padded(): lax.ppermute(head, axis, [((i + 1) % count, i) for i in range(ends)])  12.7 us
    select_n x1, other arithmetic, on_device(): perm = jnp.where(facies == facies_id, perm_table[facies_id], perm)  6.26 us
    add x3, other arithmetic, sweep(): return head_ext[1:-1, 1:-1] + relax_weight * (rhs_mid - flux_sum) / diagonal  5.74 us
    ppermute x10, waiting for transfers between devices, padded(): lax.ppermute(tail, axis, [(i, (i + 1) % count) for i in range(ends)])  5.36 us
  transfers between devices with their start and end apart: 30, of which 21 were waited for; matrix products, arithmetic and copies ran while one was open for 1% of the time, Pallas kernels for 0%

commit v1 on v0

v1 whole, which is shorter than its diff:
```python
import functools

import jax
import jax.numpy as jnp
from jax import lax
from jax.experimental import pallas as pl
from jax.experimental.pallas import tpu as pltpu
from jax.sharding import Mesh
from jax.sharding import PartitionSpec as P

COARSE_ITERS = 3
RELAX = 0.8
HALO = 4
TILE_AXES = ("z", "y", "core")
ROWS = 16
VMEM = pl.BlockSpec(memory_space=pltpu.VMEM)
SMEM = pl.BlockSpec(memory_space=pltpu.SMEM)


def position():
    z, y, core = (lax.axis_index(a) for a in TILE_AXES)
    tile = (z * lax.axis_size("y") + y) * lax.axis_size("core") + core
    return lax.axis_index("group"), tile, core, y


def call(kernel, out_shape, in_specs, scratch=(), name=None, cost=None):
    outs = jax.tree.map(lambda _: VMEM, out_shape)
    return pl.pallas_call(
        kernel,
        out_shape=out_shape,
        in_specs=in_specs,
        out_specs=outs,
        scratch_shapes=list(scratch),
        name=name,
        cost_estimate=cost,
        compiler_params=pltpu.CompilerParams(vmem_limit_bytes=48 * 1024 * 1024),
    )


def f32(*shape):
    return jax.ShapeDtypeStruct(shape, jnp.float32)


def rows_kernel(table_ref, facies_ref, source_ref, r_ref, near_ref, far_ref):
    core = position()[2]
    planes, rows, depth = facies_ref.shape
    low = lax.broadcasted_iota(jnp.int32, (rows, depth), 0) < rows // 2
    kinds = table_ref.shape[0]
    first = core == 0

    def body(x, carry):
        facies = facies_ref[x]
        perm = jnp.full((rows, depth), table_ref[0], jnp.float32)
        for kind in range(1, kinds):
            perm = jnp.where(facies == kind, table_ref[kind], perm)
        r = 1.0 / perm
        source = source_ref[x]
        r_ref[x] = r
        begin = jnp.where(low, r, pltpu.roll(source, rows // 2, 0))
        end = jnp.where(low, pltpu.roll(r, rows // 2, 0), source)
        near_ref[x] = jnp.where(first, end, begin)
        far_ref[x] = jnp.where(first, begin, end)
        return carry

    lax.fori_loop(0, planes, body, 0, unroll=4)


def halo_rows(near_ref, far_ref, x, core, tile, tiles):
    rows = far_ref.shape[1]
    depth = far_ref.shape[2]
    low = lax.broadcasted_iota(jnp.int32, (rows, depth), 0) < rows // 2
    near = near_ref[1 - core, x]
    far = far_ref[x]
    first = core == 0
    after = jnp.where(first, near, far)
    before = jnp.where(first, far, near)
    r = jnp.where(low, after, pltpu.roll(before, rows // 2, 0))
    source = jnp.where(low, pltpu.roll(after, rows // 2, 0), before)
    absent = (low & (tile == tiles - 1)) | (~low & (tile == 0))
    return jnp.where(absent, 1.0, r), jnp.where(absent, 0.0, source)


def planes_kernel(r_ref, source_ref, near_ref, far_ref, begin_ref, end_ref):
    _, tile, core, _ = position()
    tiles = lax.axis_size("z") * lax.axis_size("y") * lax.axis_size("core")
    planes = r_ref.shape[0]
    for d in range(HALO):
        for out, x in ((begin_ref, d), (end_ref, planes - 1 - d)):
            out[d] = r_ref[x]
            if d < HALO - 1:
                side_r, side_source = halo_rows(near_ref, far_ref, x, core, tile, tiles)
                out[4 + d] = side_r
                out[7 + d] = source_ref[x]
                if d < HALO - 2:
                    out[10 + d] = side_source


def fine_kernel(
    storage,
    r_ref, source_ref, near_ref, far_ref, begin_ref, end_ref,
    sums_ref, v_ref, tx_ref, ty_ref, tz_ref, w_ref, ws_ref,
    rr_ref, ss_ref, h_ref,
):
    group, tile, core, y_pos = position()
    groups = lax.axis_size("group")
    tiles = lax.axis_size("z") * lax.axis_size("y") * lax.axis_size("core")
    planes, rows, depth = r_ref.shape
    wide = planes + 2 * HALO
    ones = jnp.ones((rows, depth), jnp.float32)
    zeros = jnp.zeros((rows, depth), jnp.float32)
    for d in range(HALO):
        for recv, x, there in (
            (end_ref, HALO - 1 - d, group > 0),
            (begin_ref, HALO + planes + d, group < groups - 1),
        ):
            rr_ref[x, 0:rows] = jnp.where(there, recv[d], 1.0)
            rr_ref[x, rows:ROWS] = jnp.where(there, recv[4 + d], 1.0) if d < HALO - 1 else ones
            ss_ref[x, 0:rows] = jnp.where(there, recv[7 + d], 0.0) if d < HALO - 1 else zeros
            ss_ref[x, rows:ROWS] = jnp.where(there, recv[10 + d], 0.0) if d < HALO - 2 else zeros

    def gather_rows(x, carry):
        side_r, side_source = halo_rows(near_ref, far_ref, x, core, tile, tiles)
        rr_ref[HALO + x, 0:rows] = r_ref[x]
        rr_ref[HALO + x, rows:ROWS] = side_r
        ss_ref[HALO + x, 0:rows] = source_ref[x]
        ss_ref[HALO + x, rows:ROWS] = side_source
        return carry

    lax.fori_loop(0, planes, gather_rows, 0, unroll=2)

    row = lax.broadcasted_iota(jnp.int32, (ROWS, depth), 0)
    column = lax.broadcasted_iota(jnp.int32, (ROWS, depth), 1)
    y_wall = ((row == ROWS - 1) & (tile == 0)) | ((row == rows - 1) & (tile == tiles - 1))
    z_wall = column == depth - 1

    def faces(x, before):
        r = rr_ref[x]
        x_wall = ((x == HALO - 1) & (group == 0)) | ((x == HALO + planes - 1) & (group == groups - 1))
        tx = jnp.where(x_wall, 0.0, 2.0 / (r + rr_ref[x + 1]))
        ty = jnp.where(y_wall, 0.0, 2.0 / (r + pltpu.roll(r, ROWS - 1, 0)))
        tz = jnp.where(z_wall, 0.0, 2.0 / (r + pltpu.roll(r, depth - 1, 1)))
        diagonal = storage + tx + before + ty + pltpu.roll(ty, 1, 0) + tz + pltpu.roll(tz, 1, 1)
        w = RELAX / diagonal
        ws = w * ss_ref[x]
        tx_ref[x] = tx
        ty_ref[x] = ty
        tz_ref[x] = tz
        w_ref[x] = w
        ws_ref[x] = ws
        h_ref[x] = ws
        return tx

    start = 2.0 / (rr_ref[0] + rr_ref[1])
    lax.fori_loop(1, wide - 1, faces, start, unroll=2)

    def second(x, carry):
        total, y_flux, before = carry
        h = h_ref[x]
        tx = tx_ref[x]
        v, ahead = relax(h, h_ref[x + 1], before, tx, ty_ref[x], tz_ref[x], w_ref[x], ws_ref[x], depth)
        v_ref[x] = v
        inside = (x >= HALO) & (x < HALO + planes)
        total = total + jnp.where(inside, ss_ref[x, 0:rows] - storage * v[0:rows], 0.0)
        flux = ty_ref[x] * (v - pltpu.roll(v, ROWS - 1, 0))
        y_flux = y_flux + jnp.where(inside, flux, 0.0)
        return total, y_flux, ahead

    wide_zeros = jnp.zeros((ROWS, depth), jnp.float32)
    first_flow = tx_ref[1] * h_ref[1]
    total, y_flux, _ = lax.fori_loop(
        2, wide - 2, second, (zeros, wide_zeros, first_flow), unroll=2
    )
    left, right = HALO - 1, HALO + planes - 1
    out_left = tx_ref[left, 0:rows] * (v_ref[left + 1, 0:rows] - v_ref[left, 0:rows])
    out_right = tx_ref[right, 0:rows] * (v_ref[right, 0:rows] - v_ref[right + 1, 0:rows])
    side = jnp.where(row == ROWS - 1, y_flux, jnp.where(row == rows - 1, -y_flux, 0.0))
    rhs = total - out_left - out_right + side[0:rows] + side[rows:ROWS]
    rhs = jnp.sum(rhs, keepdims=True)
    link_x = jnp.sum(tx_ref[right, 0:rows], keepdims=True)

    def y_links(x, acc):
        return acc + ty_ref[HALO + x, 0:rows]

    link_y = lax.fori_loop(0, planes, y_links, zeros, unroll=8)
    link_y = jnp.sum(jnp.where(row[0:rows] == rows - 1, link_y, 0.0), keepdims=True)
    lane = lax.broadcasted_iota(jnp.int32, (8, 128), 1) - 8 * group
    mine = lax.broadcasted_iota(jnp.int32, (8, 128), 0) == y_pos
    packed = jnp.where(lane == 0, rhs, 0.0) + jnp.where(lane == 1, link_x, 0.0)
    packed = jnp.where(mine, packed + jnp.where(lane == 2, link_y, 0.0), 0.0)
    for peer in range(sums_ref.shape[0]):
        sums_ref[peer] = packed


def relax(h, h_next, before, tx, ty, tz, w, ws, depth):
    ahead = tx * h
    flow = before + tx * h_next
    flow = flow + ty * pltpu.roll(h, h.shape[0] - 1, 0) + pltpu.roll(ty * h, 1, 0)
    flow = flow + tz * pltpu.roll(h, depth - 1, 1) + pltpu.roll(tz * h, 1, 1)
    return (1.0 - RELAX) * h + ws + w * flow, ahead


def merge_kernel(part_ref, out_ref):
    total = part_ref[0]
    for peer in range(1, part_ref.shape[0]):
        total = total + part_ref[peer]
    for peer in range(out_ref.shape[0]):
        out_ref[peer] = total


def before_by(pair, stride):
    even, odd = pair
    length = even.shape[0]
    if stride == 1:
        return pltpu.roll(odd, 1, 0), even
    shift = stride // 2
    return pltpu.roll(even, shift, 0), pltpu.roll(odd, shift, 0)


def after_by(pair, stride):
    even, odd = pair
    length = even.shape[0]
    if stride == 1:
        return odd, pltpu.roll(even, length - 1, 0)
    shift = length - stride // 2
    return pltpu.roll(even, shift, 0), pltpu.roll(odd, shift, 0)


def each(fn, *pairs):
    return tuple(fn(*values) for values in zip(*pairs, strict=True))


def coarse_solve(sums_ref, store_brick, levels):
    lines = sums_ref.shape[0] // 2
    rhs = tuple(
        jnp.concatenate([sums_ref[2 * z + core] for z in range(lines)], axis=0) for core in range(2)
    )
    lanes = rhs[0].shape[1]
    link_x = each(lambda a: pltpu.roll(a, lanes - 1, 1), rhs)
    link_y = each(lambda a: pltpu.roll(a, lanes - 2, 1), rhs)
    link_x_before = each(lambda a: pltpu.roll(a, 8, 1), link_x)
    link_y_before = before_by(link_y, 1)
    diagonal = each(lambda a, b, c, d: store_brick + a + b + c + d, link_x, link_x_before, link_y, link_y_before)
    upper = each(lambda a: -a, link_y)
    alphas, gammas = [], []
    for level in range(levels):
        stride = 1 << level
        inverse = each(lambda d: 1.0 / d, diagonal)
        ratio = each(lambda u, i: -u * i, upper, inverse)
        alpha = before_by(ratio, stride)
        gamma = each(lambda u, i: -u * i, upper, after_by(inverse, stride))
        low = before_by(each(lambda q, u: q * u, ratio, upper), stride)
        diagonal = each(lambda d, a, g, u: d + a + g * u, diagonal, low, gamma, upper)
        upper = each(lambda g, u: g * u, gamma, after_by(upper, stride))
        alphas.append(alpha)
        gammas.append(gamma)
    inverse = each(lambda d: 1.0 / d, diagonal)
    correction = None
    for sweep_no in range(COARSE_ITERS):
        now = rhs
        if sweep_no:
            now = each(
                lambda r, a, b, c: r + a * pltpu.roll(c, 8, 1) + b * pltpu.roll(c, lanes - 8, 1),
                rhs, link_x_before, link_x, correction,
            )
        for level in range(levels):
            stride = 1 << level
            now = each(
                lambda n, a, p, g, q: n + a * p + g * q,
                now, alphas[level], before_by(now, stride), gammas[level], after_by(now, stride),
            )
        correction = each(lambda n, i: n * i, now, inverse)
    return correction


def last_kernel(
    store_brick, levels,
    sums_ref, v_ref, tx_ref, ty_ref, tz_ref, w_ref, ws_ref,
    out_ref,
    lines_ref, h_ref, g_ref,
):
    group, tile, core, _ = position()
    planes, rows, depth = out_ref.shape
    even, odd = coarse_solve(sums_ref, store_brick, levels)
    length = even.shape[0]
    for parity, line in ((0, even), (1, odd)):
        lines_ref[parity, 0:8] = jnp.zeros((8, line.shape[1]), jnp.float32)
        lines_ref[parity, 8 : 8 + length] = line
        lines_ref[parity, 8 + length : 16 + length] = jnp.zeros((8, line.shape[1]), jnp.float32)
    half = tile // 2
    here = lines_ref[core, pl.ds(8 + half, 1), :]
    ahead = lines_ref[1 - core, pl.ds(8 + half + core, 1), :]
    behind = lines_ref[1 - core, pl.ds(7 + half + core, 1), :]
    lane = lax.broadcasted_iota(jnp.int32, here.shape, 1)
    row = lax.broadcasted_iota(jnp.int32, (ROWS, depth), 0)

    def shift_of(offset):
        own, up, down = (
            jnp.sum(jnp.where(lane == 8 * (group + offset), line, 0.0), keepdims=True)
            for line in (here, ahead, behind)
        )
        return jnp.where(row < rows, own, jnp.where(row < rows + HALO, up, down))

    shifts = [shift_of(offset) for offset in (-1, 0, 1)]
    for x in (2, 3):
        h_ref[x] = v_ref[x] + shifts[0]
        h_ref[HALO + planes + x - 2] = v_ref[HALO + planes + x - 2] + shifts[2]
    middle = shifts[1]

    def lift(x, carry):
        h_ref[x] = v_ref[x] + middle
        return carry

    lax.fori_loop(HALO, HALO + planes, lift, 0, unroll=4)

    def third(x, before):
        v, ahead = relax(
            h_ref[x], h_ref[x + 1], before, tx_ref[x], ty_ref[x], tz_ref[x], w_ref[x], ws_ref[x], depth
        )
        g_ref[x] = v
        return ahead

    lax.fori_loop(HALO - 1, HALO + planes + 1, third, tx_ref[HALO - 2] * h_ref[HALO - 2], unroll=2)

    def fourth(x, before):
        h = g_ref[x]
        h_own = h[0:rows]
        tx = tx_ref[x, 0:rows]
        tz = tz_ref[x, 0:rows]
        ty = ty_ref[x]
        ahead = tx * h_own
        flow = before + tx * g_ref[x + 1, 0:rows]
        flow = flow + (ty * pltpu.roll(h, ROWS - 1, 0) + pltpu.roll(ty * h, 1, 0))[0:rows]
        flow = flow + tz * pltpu.roll(h_own, depth - 1, 1) + pltpu.roll(tz * h_own, 1, 1)
        out_ref[x - HALO] = (1.0 - RELAX) * h_own + ws_ref[x, 0:rows] + w_ref[x, 0:rows] * flow
        return ahead

    first = tx_ref[HALO - 1, 0:rows] * g_ref[HALO - 1, 0:rows]
    lax.fori_loop(HALO, HALO + planes, fourth, first, unroll=2)


def spread(block, axes):
    return lax.all_to_all(block, axes, 0, 0)


def on_device(facies, perm_table, source):
    planes, rows, depth = source.shape
    storage = 0.01 / rows
    groups = lax.axis_size("group")
    z_size, y_size, cores = (lax.axis_size(a) for a in TILE_AXES)
    tiles = z_size * y_size * cores
    brick = f32(planes, rows, depth)
    r, near, far = call(rows_kernel, (brick, brick, brick), [SMEM, VMEM, VMEM], name="rows")(
        perm_table, facies, source
    )
    pairs = [p for i in range(1, tiles - 1, 2) for p in ((i, i + 1), (i + 1, i))]
    far = lax.ppermute(far, TILE_AXES, pairs)
    near = lax.all_gather(near, "core")
    slab = f32(12, rows, depth)
    begin, end = call(planes_kernel, (slab, slab), [VMEM] * 4, name="planes")(r, source, near, far)
    end = lax.ppermute(end, "group", [(i, i + 1) for i in range(groups - 1)])
    begin = lax.ppermute(begin, "group", [(i + 1, i) for i in range(groups - 1)])
    wide = f32(planes + 2 * HALO, ROWS, depth)
    scratch = [pltpu.VMEM(wide.shape, jnp.float32)]
    sums, *fields = call(
        functools.partial(fine_kernel, storage),
        (f32(groups * y_size, 8, 128),) + (wide,) * 6,
        [VMEM] * 6,
        scratch * 3,
        name="fine",
    )(r, source, near, far, begin, end)
    sums = spread(sums, ("group", "y"))
    sums = call(merge_kernel, f32(z_size * cores, 8, 128), [VMEM], name="merge")(sums)
    sums = spread(sums, ("z", "core"))
    length = z_size * y_size
    return call(
        functools.partial(last_kernel, storage * planes * rows * depth, tiles.bit_length() - 1),
        brick,
        [VMEM] * 7,
        [pltpu.VMEM((2, length + 16, 128), jnp.float32)] + scratch * 2,
        name="last",
    )(sums, *fields)


def solution(mesh):
    groups, tiles = mesh.shape["group"], mesh.shape["tile"]
    chips = Mesh(mesh.devices.reshape(groups, tiles // 16, 8, 2), ("group",) + TILE_AXES)
    cells = P("group", TILE_AXES, None)
    return jax.shard_map(
        on_device, mesh=chips, in_specs=(cells, P(), cells), out_specs=cells, check_vma=False
    )
```

time: 212 us -> 134 us (0.63); the launches traced: 208 us -> 134 us
  starting transfers between devices: 137 us -> 9.88 us
  blocking collectives: 0 us -> 48.4 us
  other arithmetic: 26.7 us -> 0 us
  Pallas kernels: 0 us -> 23.1 us
  between operations: 3.41 us -> 13.4 us
    ppermute x30 -> x3, starting transfers between devices: 137 us -> 9.88 us  [the longest x1 4.59 us: on_device(): far = lax.ppermute(far, TILE_AXES, pairs)]
    all_to_all x0 -> x2, blocking collectives: none -> 48.4 us  [spread(): return lax.all_to_all(block, axes, 0, 0)]
    ppermute x30 -> x3, waiting for transfers between devices: 32.2 us -> 8.47 us  [the longest x1 6.85 us: on_device(): far = lax.ppermute(far, TILE_AXES, pairs)]
    pallas_call x0 -> x5, Pallas kernels: none -> 23.1 us  [the longest x1 11.9 us: on_device(): call(functools.partial(fine_kernel, storage), (f32(groups * y_size, 8, 12...]
    all_gather x0 -> x1, waiting for transfers between devices: none -> 22.7 us  [on_device(): near = lax.all_gather(near, 'core')]
    add x34 -> x0, other arithmetic: 8.03 us -> none  [the longest x3 5.74 us: sweep(): return head_ext[1:-1, 1:-1] + relax_weight * (rhs_mid - flux_sum) / diagonal]
    unnamed x7 -> x16, local copies, waits for them, and re-layouts: 0.02 us -> 7.78 us
    select_n x17 -> x0, other arithmetic: 6.96 us -> none  [the longest x1 6.26 us: on_device(): perm = jnp.where(facies == facies_id, perm_table[facies_id], perm)]
  transfers between devices with their start and end apart: 30 -> 4, of which waited for: 21 -> 4; matrix products, arithmetic and copies ran while one was open for 1% -> 0% of each run, Pallas kernels for 0% -> 0%
where the time goes in v1:
time: 134 us
  blocking collectives  48.4 us (36%)
  waiting for transfers between devices  31.2 us (23%)
  Pallas kernels  23.1 us (17%)
  between operations  13.4 us (10%)
  starting transfers between devices  9.88 us (7%)
  local copies, waits for them, and re-layouts  7.78 us (6%)
    all_to_all x2, blocking collectives, spread(): return lax.all_to_all(block, axes, 0, 0)  48.4 us
    all_gather x1, waiting for transfers between devices, on_device(): near = lax.all_gather(near, 'core')  22.7 us
    pallas_call x1, Pallas kernels, on_device(): call(functools.partial(fine_kernel, storage), (f32(groups * y_size, 8, 12...  11.9 us
    pallas_call x1, Pallas kernels, on_device(): call(functools.partial(last_kernel, storage * planes * rows * depth, tile...  9.21 us
    unnamed x16, local copies, waits for them, and re-layouts  7.78 us
    ppermute x1, waiting for transfers between devices, on_device(): far = lax.ppermute(far, TILE_AXES, pairs)  6.85 us
    ppermute x1, starting transfers between devices, on_device(): far = lax.ppermute(far, TILE_AXES, pairs)  4.59 us
    ppermute x1, starting transfers between devices, on_device(): end = lax.ppermute(end, 'group', [(i, i + 1) for i in range(groups - 1)])  3.99 us
  transfers between devices with their start and end apart: 4, of which 4 were waited for; matrix products, arithmetic and copies ran while one was open for 0% of the time, Pallas kernels for 0%

profile of v1, /device:TPU:1, one launch (start us, length us, event | category | flops | bytes accessed | tf_op | source)
XLA Modules:
  0.0 133.8 jit_solution(12601994095094043895)
XLA Ops:
  6.5 0.0 all-gather.3.cloned.1.call-start
  6.5 0.0 copy-start
  6.5 1.0 copy-done
  7.6 0.0 copy-start.6
  7.6 1.0 copy-done.6
  8.6 0.0 copy-start.7
  8.6 0.7 copy-done.7
  9.3 0.0 copy-start.1
  9.3 1.9 %rows.1 = (f32[64,8,256]{2,1,0:T(8,128)S(1)}, f32[64,8,256]{2,1,0:T(8,128)}, f32[64,8,256]{2,1,0:T(8,128)S(1)}) custom-call(f32[8]{0:T(128)S(1)} %copy-done.7, s32[64,8,256]{2,1,0:T(8,128)S(1)} %copy-done.6, f32[64,8,256]{2,1,0:T(8,128)S(1)} %copy-done), custom_call_target="tpu_custom_call" | custom-call | tf_op jit(solution)/shard_map/rows/pallas_call | solution.py:352
  11.1 0.0 all-gather.3.cloned.1.call-update
  11.2 4.6 %collective-permute-start = (f32[64,8,256]{2,1,0:T(8,128)S(1)}, f32[64,8,256]{2,1,0:T(8,128)S(1)}, u32[]{:S(2)}, u32[]{:S(2)}) collective-permute-start(f32[64,8,256]{2,1,0:T(8,128)S(1)} %get-tuple-element.19), channel_id=1, source_target_pairs={{1,2},{2,1},{3,4},{4,3},{5,6},{6,5},{7,8},{8,7},{9,10},{10,9},{11,... | collective-permute-start | bytes 1572872 | tf_op jit(solution)/shard_map/ppermute | solution.py:356
  15.8 6.8 %collective-permute-done.far_ref = f32[64,8,256]{2,1,0:T(8,128)S(1)} collective-permute-done((f32[64,8,256]{2,1,0:T(8,128)S(1)}, f32[64,8,256]{2,1,0:T(8,128)S(1)}, u32[]{:S(2)}, u32[]{:S(2)}) %collective-permute-start) | collective-permute-done | bytes 524320 | tf_op jit(solution)/shard_map/ppermute | solution.py:356
  22.6 22.7 %all-gather.3.cloned.1.call-done = f32[128,8,256]{2,1,0:T(8,128)} async-done(((f32[64,8,256]{2,1,0:T(8,128)}), f32[128,8,256]{2,1,0:T(8,128)}) %all-gather.3.cloned.1.call-update) | async-done | bytes 1048592 | tf_op jit(solution)/shard_map/all_gather | solution.py:357
  45.3 0.0 copy-done.1
  45.3 0.0 copy-start.2
  45.3 1.2 copy-done.2
  46.6 1.3 collective-permute-start.1
  47.9 4.0 %collective-permute-start.2 = (f32[12,8,256]{2,1,0:T(8,128)S(1)}, f32[12,8,256]{2,1,0:T(8,128)S(1)}, u32[]{:S(2)}, u32[]{:S(2)}) collective-permute-start(f32[12,8,256]{2,1,0:T(8,128)S(1)} %get-tuple-element.21), channel_id=1, source_target_pairs={{0,256},{256,512},{512,768},{1,257},{257,513},{513,769},{2,258},{2... | collective-permute-start | bytes 294920 | tf_op jit(solution)/shard_map/ppermute | solution.py:360
  51.9 0.8 collective-permute-done.1.begin_ref
  52.7 0.8 collective-permute-done.2.end_ref
  53.5 11.9 %fine.1 = (f32[32,8,128]{2,1,0:T(8,128)S(1)}, f32[72,16,256]{2,1,0:T(8,128)S(1)}, f32[72,16,256]{2,1,0:T(8,128)S(1)}, f32[72,16,256]{2,1,0:T(8,128)}, f32[72,16,...) custom-call(f32[64,8,256]{2,1,0:T(8,128)S(1)} %get-tuple-element.17.r_ref, ...), custom_call_target="tpu_custom_call" | custom-call | tf_op jit(solution)/shard_map/fine/pallas_call | solution.py:364
  65.4 16.8 %all_to_all.10.part_ref = f32[32,8,128]{2,1,0:T(8,128)S(1)} all-to-all(f32[32,8,128]{2,1,0:T(8,128)S(1)} %get-tuple-element.22), channel_id=1, replica_groups=mesh['group'=4,'z'=16,'y'=8,'core'=2] {'group','y'}, dimensions={0} | all-to-all | bytes 262144 | tf_op jit(solution)/shard_map/all_to_all | solution.py:342
  82.3 31.6 %all_to_all.11.sums_ref = f32[32,8,128]{2,1,0:T(8,128)S(1)} all-to-all(f32[32,8,128]{2,1,0:T(8,128)S(1)} %merge.1), channel_id=1, replica_groups=mesh['group'=4,'z'=16,'y'=8,'core'=2] {'z','core'}, dimensions={0} | all-to-all | bytes 262144 | tf_op jit(solution)/shard_map/all_to_all | solution.py:342
  113.9 0.0 copy-start.3
  113.9 1.3 copy-done.3
  115.2 0.0 copy-start.4
  115.2 1.3 copy-done.4
  116.5 0.0 copy-start.5
  116.5 1.3 copy-done.5
  117.7 9.2 %last.1 = f32[64,8,256]{2,1,0:T(8,128)} custom-call(f32[32,8,128]{2,1,0:T(8,128)S(1)} %all_to_all.11.sums_ref, f32[72,16,256]{2,1,0:T(8,128)S(1)} %get-tuple-element.23.v_ref, f32[72,16,256]{2,1,0:T(8,128)S(1)} %get-tuple-element.24.tx_ref, f32[72,16,256]{2,1,0:T(8,128)S(1)} %copy-done.3, f32[72,16,256]{2,1,0:T(8,128)S(1)} %copy-done.4, ...), custom_call_target="tpu_custom_call" | custom-call | tf_op jit(solution)/shard_map/last/pallas_call | solution.py:375
  (2 shorter events, 0.1 us)
Async XLA Ops:
  6.5 38.8 %all-gather.3.cloned.1.call-start = ((), (), s32[]{:S(2)}) async-start(), calls=%async_computation.2 | async-start | bytes 1572864 | tf_op jit(solution)/shard_map/all_gather | solution.py:357
  6.5 1.0 copy-start
  7.6 1.0 copy-start.6
  8.6 0.7 copy-start.7
  9.3 36.1 %copy-start.1 = (f32[64,8,256]{2,1,0:T(8,128)S(1)}, f32[64,8,256]{2,1,0:T(8,128)}, u32[]{:S(2)}) copy-start(f32[64,8,256]{2,1,0:T(8,128)} %source_ref.5) | copy-start | bytes 1572868
  11.2 11.5 %collective-permute-start = (f32[64,8,256]{2,1,0:T(8,128)S(1)}, f32[64,8,256]{2,1,0:T(8,128)S(1)}, u32[]{:S(2)}, u32[]{:S(2)}) collective-permute-start(f32[64,8,256]{2,1,0:T(8,128)S(1)} %get-tuple-element.19), channel_id=1, source_target_pairs={{1,2},{2,1},{3,4},{4,3},{5,6},{6,5},{7,8},{8,7},{9,10},{10,9},{11,... | collective-permute-start | bytes 1572872 | tf_op jit(solution)/shard_map/ppermute | solution.py:356
  45.3 1.2 copy-start.2
  46.6 6.1 %collective-permute-start.1 = (f32[12,8,256]{2,1,0:T(8,128)S(1)}, f32[12,8,256]{2,1,0:T(8,128)S(1)}, u32[]{:S(2)}, u32[]{:S(2)}) collective-permute-start(f32[12,8,256]{2,1,0:T(8,128)S(1)} %get-tuple-element.20), channel_id=1, source_target_pairs={{256,0},{512,256},{768,512},{257,1},{513,257},{769,513},{258,2},{5... | collective-permute-start | bytes 294920 | tf_op jit(solution)/shard_map/ppermute | solution.py:361
  47.9 5.6 %collective-permute-start.2 = (f32[12,8,256]{2,1,0:T(8,128)S(1)}, f32[12,8,256]{2,1,0:T(8,128)S(1)}, u32[]{:S(2)}, u32[]{:S(2)}) collective-permute-start(f32[12,8,256]{2,1,0:T(8,128)S(1)} %get-tuple-element.21), channel_id=1, source_target_pairs={{0,256},{256,512},{512,768},{1,257},{257,513},{513,769},{2,258},{2... | collective-permute-start | bytes 294920 | tf_op jit(solution)/shard_map/ppermute | solution.py:360
  113.9 1.3 copy-start.3
  115.2 1.3 copy-start.4
  116.5 1.3 copy-start.5
Sparse Core Ops, SparseCore 0:
  11.3 34.0 all-gather.2

commit v2 on v1

--- a/solution.py
+++ b/solution.py
@@ -33,7 +33,7 @@
         scratch_shapes=list(scratch),
         name=name,
         cost_estimate=cost,
-        compiler_params=pltpu.CompilerParams(vmem_limit_bytes=48 * 1024 * 1024),
+        compiler_params=pltpu.CompilerParams(vmem_limit_bytes=24 * 1024 * 1024),
     )
 
 
@@ -69,7 +69,7 @@
     rows = far_ref.shape[1]
     depth = far_ref.shape[2]
     low = lax.broadcasted_iota(jnp.int32, (rows, depth), 0) < rows // 2
-    near = near_ref[1 - core, x]
+    near = near_ref[x]
     far = far_ref[x]
     first = core == 0
     after = jnp.where(first, near, far)
@@ -183,10 +183,9 @@
 
     link_y = lax.fori_loop(0, planes, y_links, zeros, unroll=8)
     link_y = jnp.sum(jnp.where(row[0:rows] == rows - 1, link_y, 0.0), keepdims=True)
-    lane = lax.broadcasted_iota(jnp.int32, (8, 128), 1) - 8 * group
-    mine = lax.broadcasted_iota(jnp.int32, (8, 128), 0) == y_pos
+    lane = lax.broadcasted_iota(jnp.int32, (1, 128), 1) - (32 * group + 4 * y_pos)
     packed = jnp.where(lane == 0, rhs, 0.0) + jnp.where(lane == 1, link_x, 0.0)
-    packed = jnp.where(mine, packed + jnp.where(lane == 2, link_y, 0.0), 0.0)
+    packed = packed + jnp.where(lane == 2, link_y, 0.0)
     for peer in range(sums_ref.shape[0]):
         sums_ref[peer] = packed
 
@@ -231,13 +230,23 @@
 
 def coarse_solve(sums_ref, store_brick, levels):
     lines = sums_ref.shape[0] // 2
+    lanes = sums_ref.shape[2]
+    y_lane = lax.broadcasted_iota(jnp.int32, (8, lanes), 1) // 4 % 8
+    own_y = y_lane == lax.broadcasted_iota(jnp.int32, (8, lanes), 0)
+
+    def unpack(line):
+        line = jnp.where(own_y, jnp.broadcast_to(line, (8, lanes)), 0.0)
+        for shift in (16, 8, 4):
+            line = line + pltpu.roll(line, lanes - shift, 1)
+        return line
+
     rhs = tuple(
-        jnp.concatenate([sums_ref[2 * z + core] for z in range(lines)], axis=0) for core in range(2)
-    )
-    lanes = rhs[0].shape[1]
+        jnp.concatenate([unpack(sums_ref[2 * z + core]) for z in range(lines)], axis=0)
+        for core in range(2)
+    )
     link_x = each(lambda a: pltpu.roll(a, lanes - 1, 1), rhs)
     link_y = each(lambda a: pltpu.roll(a, lanes - 2, 1), rhs)
-    link_x_before = each(lambda a: pltpu.roll(a, 8, 1), link_x)
+    link_x_before = each(lambda a: pltpu.roll(a, 32, 1), link_x)
     link_y_before = before_by(link_y, 1)
     diagonal = each(lambda a, b, c, d: store_brick + a + b + c + d, link_x, link_x_before, link_y, link_y_before)
     upper = each(lambda a: -a, link_y)
@@ -259,7 +268,7 @@
         now = rhs
         if sweep_no:
             now = each(
-                lambda r, a, b, c: r + a * pltpu.roll(c, 8, 1) + b * pltpu.roll(c, lanes - 8, 1),
+                lambda r, a, b, c: r + a * pltpu.roll(c, 32, 1) + b * pltpu.roll(c, lanes - 32, 1),
                 rhs, link_x_before, link_x, correction,
             )
         for level in range(levels):
@@ -295,7 +304,7 @@
 
     def shift_of(offset):
         own, up, down = (
-            jnp.sum(jnp.where(lane == 8 * (group + offset), line, 0.0), keepdims=True)
+            jnp.sum(jnp.where(lane == 32 * (group + offset), line, 0.0), keepdims=True)
             for line in (here, ahead, behind)
         )
         return jnp.where(row < rows, own, jnp.where(row < rows + HALO, up, down))
@@ -354,7 +363,7 @@
     )
     pairs = [p for i in range(1, tiles - 1, 2) for p in ((i, i + 1), (i + 1, i))]
     far = lax.ppermute(far, TILE_AXES, pairs)
-    near = lax.all_gather(near, "core")
+    near = lax.ppermute(near, "core", [(0, 1), (1, 0)])
     slab = f32(12, rows, depth)
     begin, end = call(planes_kernel, (slab, slab), [VMEM] * 4, name="planes")(r, source, near, far)
     end = lax.ppermute(end, "group", [(i, i + 1) for i in range(groups - 1)])
@@ -363,13 +372,13 @@
     scratch = [pltpu.VMEM(wide.shape, jnp.float32)]
     sums, *fields = call(
         functools.partial(fine_kernel, storage),
-        (f32(groups * y_size, 8, 128),) + (wide,) * 6,
+        (f32(groups * y_size, 1, 128),) + (wide,) * 6,
         [VMEM] * 6,
         scratch * 3,
         name="fine",
     )(r, source, near, far, begin, end)
     sums = spread(sums, ("group", "y"))
-    sums = call(merge_kernel, f32(z_size * cores, 8, 128), [VMEM], name="merge")(sums)
+    sums = call(merge_kernel, f32(z_size * cores, 1, 128), [VMEM], name="merge")(sums)
     sums = spread(sums, ("z", "core"))
     length = z_size * y_size
     return call(

time: 134 us -> 96.4 us (0.72)
  waiting for transfers between devices: 31.2 us -> 10.2 us
  starting transfers between devices: 9.88 us -> 23.3 us
  between operations: 13.4 us -> 0.07 us
  blocking collectives: 48.4 us -> 40.7 us
  local copies, waits for them, and re-layouts: 7.78 us -> 2.74 us
  Pallas kernels: 23.1 us -> 19.1 us
    all_gather x1 -> x0, waiting for transfers between devices: 22.7 us -> none  [on_device(): near = lax.all_gather(near, 'core')]
    ppermute x0 -> x1, starting transfers between devices: none -> 16.1 us  [on_device(): near = lax.ppermute(near, 'core', [(0, 1), (1, 0)])]
    all_to_all x2, blocking collectives: 48.4 us -> 40.7 us  [spread(): return lax.all_to_all(block, axes, 0, 0)]
    unnamed x16 -> x8, local copies, waits for them, and re-layouts: 7.78 us -> 2.74 us
    ppermute x1, starting transfers between devices: 4.59 us -> 1.92 us  [on_device(): far = lax.ppermute(far, TILE_AXES, pairs)]
    pallas_call x2, Pallas kernels: 12 us -> 9.94 us  [the longest x1 9.9 us: on_device(): call(functools.partial(fine_kernel, storage), (f32(groups * y_size, 1, 12...]
    ppermute x1, waiting for transfers between devices: 6.85 us -> 8.56 us  [on_device(): far = lax.ppermute(far, TILE_AXES, pairs)]
  transfers between devices with their start and end apart: 4 -> 4, of which waited for: 4 -> 3; matrix products, arithmetic and copies ran while one was open for 0% -> 0% of each run, Pallas kernels for 0% -> 0%
where the time goes in v2:
time: 96.4 us; the launch traced here: 96.1 us
  blocking collectives  40.7 us (42%)
  starting transfers between devices  23.3 us (24%)
  Pallas kernels  19.1 us (20%)
  waiting for transfers between devices  10.2 us (11%)
  local copies, waits for them, and re-layouts  2.74 us (3%)
    all_to_all x2, blocking collectives, spread(): return lax.all_to_all(block, axes, 0, 0)  40.7 us
    ppermute x1, starting transfers between devices, on_device(): near = lax.ppermute(near, 'core', [(0, 1), (1, 0)])  16.1 us
    pallas_call x1, Pallas kernels, on_device(): call(functools.partial(fine_kernel, storage), (f32(groups * y_size, 1, 12...  9.9 us
    ppermute x1, waiting for transfers between devices, on_device(): far = lax.ppermute(far, TILE_AXES, pairs)  8.56 us
    pallas_call x1, Pallas kernels, on_device(): call(functools.partial(last_kernel, storage * planes * rows * depth, tile...  8.11 us
    ppermute x1, starting transfers between devices, on_device(): end = lax.ppermute(end, 'group', [(i, i + 1) for i in range(groups - 1)])  3.99 us
    unnamed x8, local copies, waits for them, and re-layouts  2.74 us
  transfers between devices with their start and end apart: 4, of which 3 were waited for; matrix products, arithmetic and copies ran while one was open for 0% of the time, Pallas kernels for 0%

profile of v2, /device:TPU:1, one launch (start us, length us, event | category | flops | bytes accessed | tf_op | source)
XLA Modules:
  0.0 96.1 jit_solution(10064774219243302131)
XLA Ops:
  0.0 0.0 copy-start
  0.0 1.0 %copy-done = f32[64,8,256]{2,1,0:T(8,128)S(1)} copy-done((f32[64,8,256]{2,1,0:T(8,128)S(1)}, f32[64,8,256]{2,1,0:T(8,128)}, u32[]{:S(2)}) %copy-start) | copy-done | bytes 524312
  1.0 0.0 copy-start.2
  1.0 1.0 %copy-done.2 = s32[64,8,256]{2,1,0:T(8,128)S(1)} copy-done((s32[64,8,256]{2,1,0:T(8,128)S(1)}, s32[64,8,256]{2,1,0:T(8,128)}, u32[]{:S(2)}) %copy-start.2) | copy-done | bytes 524312
  2.1 0.0 copy-start.3
  2.1 0.7 copy-done.3
  2.7 0.0 copy-start.1
  2.7 1.1 %rows.1 = (f32[64,8,256]{2,1,0:T(8,128)S(1)}, f32[64,8,256]{2,1,0:T(8,128)S(1)}, f32[64,8,256]{2,1,0:T(8,128)S(1)}) custom-call(f32[8]{0:T(128)S(1)} %copy-done.3, s32[64,8,256]{2,1,0:T(8,128)S(1)} %copy-done.2, f32[64,8,256]{2,1,0:T(8,128)S(1)} %copy-done), custom_call_target="tpu_custom_call" | custom-call | tf_op jit(solution)/shard_map/rows/pallas_call | solution.py:361
  3.8 16.1 %collective-permute-start = (f32[64,8,256]{2,1,0:T(8,128)S(1)}, f32[64,8,256]{2,1,0:T(8,128)S(1)}, u32[]{:S(2)}, u32[]{:S(2)}) collective-permute-start(f32[64,8,256]{2,1,0:T(8,128)S(1)} %get-tuple-element.18), channel_id=1, source_target_pairs={{0,1},{1,0},{2,3},{3,2},{4,5},{5,4},{6,7},{7,6},{8,9},{9,8},{10,11... | collective-permute-start | bytes 1572872 | tf_op jit(solution)/shard_map/ppermute | solution.py:366
  19.9 1.9 %collective-permute-start.1 = (f32[64,8,256]{2,1,0:T(8,128)S(1)}, f32[64,8,256]{2,1,0:T(8,128)S(1)}, u32[]{:S(2)}, u32[]{:S(2)}) collective-permute-start(f32[64,8,256]{2,1,0:T(8,128)S(1)} %get-tuple-element.19), channel_id=1, source_target_pairs={{1,2},{2,1},{3,4},{4,3},{5,6},{6,5},{7,8},{8,7},{9,10},{10,9},{11,... | collective-permute-start | bytes 1572872 | tf_op jit(solution)/shard_map/ppermute | solution.py:365
  21.8 0.0 collective-permute-done.near_ref
  21.8 8.6 %collective-permute-done.1.far_ref = f32[64,8,256]{2,1,0:T(8,128)S(1)} collective-permute-done((f32[64,8,256]{2,1,0:T(8,128)S(1)}, f32[64,8,256]{2,1,0:T(8,128)S(1)}, u32[]{:S(2)}, u32[]{:S(2)}) %collective-permute-start.1) | collective-permute-done | bytes 524320 | tf_op jit(solution)/shard_map/ppermute | solution.py:365
  30.4 0.0 copy-done.1
  30.4 1.3 %collective-permute-start.2 = (f32[12,8,256]{2,1,0:T(8,128)S(1)}, f32[12,8,256]{2,1,0:T(8,128)S(1)}, u32[]{:S(2)}, u32[]{:S(2)}) collective-permute-start(f32[12,8,256]{2,1,0:T(8,128)S(1)} %get-tuple-element.20), channel_id=1, source_target_pairs={{256,0},{512,256},{768,512},{257,1},{513,257},{769,513},{258,2},{5... | collective-permute-start | bytes 294920 | tf_op jit(solution)/shard_map/ppermute | solution.py:370
  31.7 4.0 %collective-permute-start.3 = (f32[12,8,256]{2,1,0:T(8,128)S(1)}, f32[12,8,256]{2,1,0:T(8,128)S(1)}, u32[]{:S(2)}, u32[]{:S(2)}) collective-permute-start(f32[12,8,256]{2,1,0:T(8,128)S(1)} %get-tuple-element.21), channel_id=1, source_target_pairs={{0,256},{256,512},{512,768},{1,257},{257,513},{513,769},{2,258},{2... | collective-permute-start | bytes 294920 | tf_op jit(solution)/shard_map/ppermute | solution.py:369
  35.7 0.1 collective-permute-done.2.begin_ref
  35.8 1.6 %collective-permute-done.3.end_ref = f32[12,8,256]{2,1,0:T(8,128)S(1)} collective-permute-done((f32[12,8,256]{2,1,0:T(8,128)S(1)}, f32[12,8,256]{2,1,0:T(8,128)S(1)}, u32[]{:S(2)}, u32[]{:S(2)}) %collective-permute-start.3) | collective-permute-done | bytes 98336 | tf_op jit(solution)/shard_map/ppermute | solution.py:369
  37.3 9.9 %fine.1 = (f32[32,1,128]{2,1,0:T(1,128)S(1)}, f32[72,16,256]{2,1,0:T(8,128)S(1)}, f32[72,16,256]{2,1,0:T(8,128)S(1)}, f32[72,16,256]{2,1,0:T(8,128)S(1)}, f32[72...) custom-call(f32[64,8,256]{2,1,0:T(8,128)S(1)} %get-tuple-element.17.r_ref, ...), custom_call_target="tpu_custom_call" | custom-call | tf_op jit(solution)/shard_map/fine/pallas_call | solution.py:373
  47.2 12.3 %all_to_all.10.part_ref = f32[32,1,128]{2,1,0:T(1,128)S(1)} all-to-all(f32[32,1,128]{2,1,0:T(1,128)S(1)} %get-tuple-element.22), channel_id=1, replica_groups=mesh['group'=4,'z'=16,'y'=8,'core'=2] {'group','y'}, dimensions={0} | all-to-all | bytes 32768 | tf_op jit(solution)/shard_map/all_to_all | solution.py:351
  59.5 28.4 %all_to_all.11.sums_ref = f32[32,1,128]{2,1,0:T(1,128)S(1)} all-to-all(f32[32,1,128]{2,1,0:T(1,128)S(1)} %merge.1), channel_id=1, replica_groups=mesh['group'=4,'z'=16,'y'=8,'core'=2] {'z','core'}, dimensions={0} | all-to-all | bytes 32768 | tf_op jit(solution)/shard_map/all_to_all | solution.py:351
  88.0 8.1 %last.1 = f32[64,8,256]{2,1,0:T(8,128)} custom-call(f32[32,1,128]{2,1,0:T(1,128)S(1)} %all_to_all.11.sums_ref, f32[72,16,256]{2,1,0:T(8,128)S(1)} %get-tuple-element.23.v_ref, f32[72,16,256]{2,1,0:T(8,128)S(1)} %get-tuple-element.24.tx_ref, f32[72,16,256]{2,1,0:T(8,128)S(1)} %get-tuple-element.25.ty_ref, f32[72,16,256]{2,1,0:T(8,128)S(1)} %get-tuple-element.26.tz_ref, ...), custom_call_target="tpu_custom_call" | custom-call | tf_op jit(solution)/shard_map/last/pallas_call | solution.py:384
  (2 shorter events, 0.1 us)
Async XLA Ops:
  0.0 1.0 %copy-start = (f32[64,8,256]{2,1,0:T(8,128)S(1)}, f32[64,8,256]{2,1,0:T(8,128)}, u32[]{:S(2)}) copy-start(f32[64,8,256]{2,1,0:T(8,128)} %source_ref.5) | copy-start | bytes 1572868
  1.0 1.0 %copy-start.2 = (s32[64,8,256]{2,1,0:T(8,128)S(1)}, s32[64,8,256]{2,1,0:T(8,128)}, u32[]{:S(2)}) copy-start(s32[64,8,256]{2,1,0:T(8,128)} %facies_ref.1) | copy-start | bytes 1572868
  2.1 0.7 copy-start.3
  2.7 27.6 %copy-start.1 = (f32[64,8,256]{2,1,0:T(8,128)S(1)}, f32[64,8,256]{2,1,0:T(8,128)}, u32[]{:S(2)}) copy-start(f32[64,8,256]{2,1,0:T(8,128)} %source_ref.5) | copy-start | bytes 1572868
  3.8 18.0 %collective-permute-start = (f32[64,8,256]{2,1,0:T(8,128)S(1)}, f32[64,8,256]{2,1,0:T(8,128)S(1)}, u32[]{:S(2)}, u32[]{:S(2)}) collective-permute-start(f32[64,8,256]{2,1,0:T(8,128)S(1)} %get-tuple-element.18), channel_id=1, source_target_pairs={{0,1},{1,0},{2,3},{3,2},{4,5},{5,4},{6,7},{7,6},{8,9},{9,8},{10,11... | collective-permute-start | bytes 1572872 | tf_op jit(solution)/shard_map/ppermute | solution.py:366
  19.9 10.5 %collective-permute-start.1 = (f32[64,8,256]{2,1,0:T(8,128)S(1)}, f32[64,8,256]{2,1,0:T(8,128)S(1)}, u32[]{:S(2)}, u32[]{:S(2)}) collective-permute-start(f32[64,8,256]{2,1,0:T(8,128)S(1)} %get-tuple-element.19), channel_id=1, source_target_pairs={{1,2},{2,1},{3,4},{4,3},{5,6},{6,5},{7,8},{8,7},{9,10},{10,9},{11,... | collective-permute-start | bytes 1572872 | tf_op jit(solution)/shard_map/ppermute | solution.py:365
  30.4 5.4 %collective-permute-start.2 = (f32[12,8,256]{2,1,0:T(8,128)S(1)}, f32[12,8,256]{2,1,0:T(8,128)S(1)}, u32[]{:S(2)}, u32[]{:S(2)}) collective-permute-start(f32[12,8,256]{2,1,0:T(8,128)S(1)} %get-tuple-element.20), channel_id=1, source_target_pairs={{256,0},{512,256},{768,512},{257,1},{513,257},{769,513},{258,2},{5... | collective-permute-start | bytes 294920 | tf_op jit(solution)/shard_map/ppermute | solution.py:370
  31.7 5.6 %collective-permute-start.3 = (f32[12,8,256]{2,1,0:T(8,128)S(1)}, f32[12,8,256]{2,1,0:T(8,128)S(1)}, u32[]{:S(2)}, u32[]{:S(2)}) collective-permute-start(f32[12,8,256]{2,1,0:T(8,128)S(1)} %get-tuple-element.21), channel_id=1, source_target_pairs={{0,256},{256,512},{512,768},{1,257},{257,513},{513,769},{2,258},{2... | collective-permute-start | bytes 294920 | tf_op jit(solution)/shard_map/ppermute | solution.py:369

commit v3 on v2

--- a/solution.py
+++ b/solution.py
@@ -14,7 +14,7 @@
 TILE_AXES = ("z", "y", "core")
 ROWS = 16
 VMEM = pl.BlockSpec(memory_space=pltpu.VMEM)
-SMEM = pl.BlockSpec(memory_space=pltpu.SMEM)
+HBM = pl.BlockSpec(memory_space=pltpu.HBM)
 
 
 def position():
@@ -41,28 +41,49 @@
     return jax.ShapeDtypeStruct(shape, jnp.float32)
 
 
-def rows_kernel(table_ref, facies_ref, source_ref, r_ref, near_ref, far_ref):
+def rows_kernel(
+    chunks, table_hbm, facies_hbm, source_hbm, r_ref, source_ref, near_ref, far_ref,
+    table_ref, facies_ref, table_sem, sems,
+):
     core = position()[2]
     planes, rows, depth = facies_ref.shape
     low = lax.broadcasted_iota(jnp.int32, (rows, depth), 0) < rows // 2
     kinds = table_ref.shape[0]
     first = core == 0
-
-    def body(x, carry):
-        facies = facies_ref[x]
-        perm = jnp.full((rows, depth), table_ref[0], jnp.float32)
-        for kind in range(1, kinds):
-            perm = jnp.where(facies == kind, table_ref[kind], perm)
-        r = 1.0 / perm
-        source = source_ref[x]
-        r_ref[x] = r
-        begin = jnp.where(low, r, pltpu.roll(source, rows // 2, 0))
-        end = jnp.where(low, pltpu.roll(r, rows // 2, 0), source)
-        near_ref[x] = jnp.where(first, end, begin)
-        far_ref[x] = jnp.where(first, begin, end)
-        return carry
-
-    lax.fori_loop(0, planes, body, 0, unroll=4)
+    step = planes // chunks
+    table = pltpu.make_async_copy(table_hbm, table_ref, table_sem)
+    table.start()
+    copies = []
+    for chunk in range(chunks):
+        part = pl.ds(chunk * step, step)
+        pair = (
+            pltpu.make_async_copy(facies_hbm.at[part], facies_ref.at[part], sems.at[0, chunk]),
+            pltpu.make_async_copy(source_hbm.at[part], source_ref.at[part], sems.at[1, chunk]),
+        )
+        for copy in pair:
+            copy.start()
+        copies.append(pair)
+    table.wait()
+
+    for chunk in range(chunks):
+        for copy in copies[chunk]:
+            copy.wait()
+
+        def body(x, carry):
+            facies = facies_ref[x]
+            perm = jnp.full((rows, depth), table_ref[0], jnp.float32)
+            for kind in range(1, kinds):
+                perm = jnp.where(facies == kind, table_ref[kind], perm)
+            r = 1.0 / perm
+            source = source_ref[x]
+            r_ref[x] = r
+            begin = jnp.where(low, r, pltpu.roll(source, rows // 2, 0))
+            end = jnp.where(low, pltpu.roll(r, rows // 2, 0), source)
+            near_ref[x] = jnp.where(first, end, begin)
+            far_ref[x] = jnp.where(first, begin, end)
+            return carry
+
+        lax.fori_loop(chunk * step, (chunk + 1) * step, body, 0, unroll=8)
 
 
 def halo_rows(near_ref, far_ref, x, core, tile, tiles):
@@ -126,7 +147,7 @@
         ss_ref[HALO + x, rows:ROWS] = side_source
         return carry
 
-    lax.fori_loop(0, planes, gather_rows, 0, unroll=2)
+    lax.fori_loop(0, planes, gather_rows, 0, unroll=16)
 
     row = lax.broadcasted_iota(jnp.int32, (ROWS, depth), 0)
     column = lax.broadcasted_iota(jnp.int32, (ROWS, depth), 1)
@@ -151,7 +172,7 @@
         return tx
 
     start = 2.0 / (rr_ref[0] + rr_ref[1])
-    lax.fori_loop(1, wide - 1, faces, start, unroll=2)
+    lax.fori_loop(1, wide - 1, faces, start, unroll=16)
 
     def second(x, carry):
         total, y_flux, before = carry
@@ -168,7 +189,7 @@
     wide_zeros = jnp.zeros((ROWS, depth), jnp.float32)
     first_flow = tx_ref[1] * h_ref[1]
     total, y_flux, _ = lax.fori_loop(
-        2, wide - 2, second, (zeros, wide_zeros, first_flow), unroll=2
+        2, wide - 2, second, (zeros, wide_zeros, first_flow), unroll=16
     )
     left, right = HALO - 1, HALO + planes - 1
     out_left = tx_ref[left, 0:rows] * (v_ref[left + 1, 0:rows] - v_ref[left, 0:rows])
@@ -328,7 +349,7 @@
         g_ref[x] = v
         return ahead
 
-    lax.fori_loop(HALO - 1, HALO + planes + 1, third, tx_ref[HALO - 2] * h_ref[HALO - 2], unroll=2)
+    lax.fori_loop(HALO - 1, HALO + planes + 1, third, tx_ref[HALO - 2] * h_ref[HALO - 2], unroll=16)
 
     def fourth(x, before):
         h = g_ref[x]
@@ -344,7 +365,7 @@
         return ahead
 
     first = tx_ref[HALO - 1, 0:rows] * g_ref[HALO - 1, 0:rows]
-    lax.fori_loop(HALO, HALO + planes, fourth, first, unroll=2)
+    lax.fori_loop(HALO, HALO + planes, fourth, first, unroll=16)
 
 
 def spread(block, axes):
@@ -358,9 +379,19 @@
     z_size, y_size, cores = (lax.axis_size(a) for a in TILE_AXES)
     tiles = z_size * y_size * cores
     brick = f32(planes, rows, depth)
-    r, near, far = call(rows_kernel, (brick, brick, brick), [SMEM, VMEM, VMEM], name="rows")(
-        perm_table, facies, source
-    )
+    chunks = 4
+    r, source, near, far = call(
+        functools.partial(rows_kernel, chunks),
+        (brick,) * 4,
+        [HBM] * 3,
+        [
+            pltpu.SMEM(perm_table.shape, jnp.float32),
+            pltpu.VMEM(source.shape, jnp.int32),
+            pltpu.SemaphoreType.DMA,
+            pltpu.SemaphoreType.DMA((2, chunks)),
+        ],
+        name="rows",
+    )(*(pltpu.with_memory_space_constraint(a, pltpu.HBM) for a in (perm_table, facies, source)))
     pairs = [p for i in range(1, tiles - 1, 2) for p in ((i, i + 1), (i + 1, i))]
     far = lax.ppermute(far, TILE_AXES, pairs)
     near = lax.ppermute(near, "core", [(0, 1), (1, 0)])

time: 96.4 us -> 84.4 us (0.88)
  Pallas kernels: 19.1 us -> 9.95 us
  local copies, waits for them, and re-layouts: 2.74 us -> 0 us
    pallas_call x1, Pallas kernels: 9.9 us -> 4.13 us  [on_device(): call(functools.partial(fine_kernel, storage), (f32(groups * y_size, 1, 12...]
    pallas_call x1, Pallas kernels: 8.11 us -> 4.26 us  [on_device(): call(functools.partial(last_kernel, storage * planes * rows * depth, tile...]
    unnamed x8 -> x0, local copies, waits for them, and re-layouts: 2.74 us -> none
where the time goes in v3:
time: 84.4 us; the launch traced here: 84.2 us
  blocking collectives  40.7 us (48%)
  starting transfers between devices  23.3 us (28%)
  waiting for transfers between devices  10.2 us (12%)
  Pallas kernels  9.95 us (12%)
    all_to_all x2, blocking collectives, spread(): return lax.all_to_all(block, axes, 0, 0)  40.7 us
    ppermute x1, starting transfers between devices, on_device(): near = lax.ppermute(near, 'core', [(0, 1), (1, 0)])  16.1 us
    ppermute x1, waiting for transfers between devices, on_device(): far = lax.ppermute(far, TILE_AXES, pairs)  8.56 us
    pallas_call x1, Pallas kernels, on_device(): call(functools.partial(last_kernel, storage * planes * rows * depth, tile...  4.26 us
    pallas_call x1, Pallas kernels, on_device(): call(functools.partial(fine_kernel, storage), (f32(groups * y_size, 1, 12...  4.13 us
    ppermute x1, starting transfers between devices, on_device(): end = lax.ppermute(end, 'group', [(i, i + 1) for i in range(groups - 1)])  3.99 us
    ppermute x1, starting transfers between devices, on_device(): far = lax.ppermute(far, TILE_AXES, pairs)  1.92 us
  transfers between devices with their start and end apart: 4, of which 3 were waited for; matrix products, arithmetic and copies ran while one was open for 0% of the time, Pallas kernels for 0%

profile of v3, /device:TPU:1, one launch (start us, length us, event | category | flops | bytes accessed | tf_op | source)
XLA Modules:
  0.0 84.2 jit_solution(17594425135664046926)
XLA Ops:
  0.0 1.5 %rows.1 = (f32[64,8,256]{2,1,0:T(8,128)S(1)}, f32[64,8,256]{2,1,0:T(8,128)S(1)}, f32[64,8,256]{2,1,0:T(8,128)S(1)}, f32[64,8,256]{2,1,0:T(8,128)S(1)}) custom-call(f32[8]{0:T(128)} %table_hbm.1, s32[64,8,256]{2,1,0:T(8,128)} %facies_hbm.1, f32[64,8,256]{2,1,0:T(8,128)} %source_hbm.1), custom_call_target="tpu_custom_call" | custom-call | tf_op jit(solution)/shard_map/rows/pallas_call | solution.py:383
  1.5 16.1 %collective-permute-start = (f32[64,8,256]{2,1,0:T(8,128)S(1)}, f32[64,8,256]{2,1,0:T(8,128)S(1)}, u32[]{:S(2)}, u32[]{:S(2)}) collective-permute-start(f32[64,8,256]{2,1,0:T(8,128)S(1)} %get-tuple-element.20), channel_id=1, source_target_pairs={{0,1},{1,0},{2,3},{3,2},{4,5},{5,4},{6,7},{7,6},{8,9},{9,8},{10,11... | collective-permute-start | bytes 1572872 | tf_op jit(solution)/shard_map/ppermute | solution.py:397
  17.6 1.9 %collective-permute-start.1 = (f32[64,8,256]{2,1,0:T(8,128)S(1)}, f32[64,8,256]{2,1,0:T(8,128)S(1)}, u32[]{:S(2)}, u32[]{:S(2)}) collective-permute-start(f32[64,8,256]{2,1,0:T(8,128)S(1)} %get-tuple-element.21), channel_id=1, source_target_pairs={{1,2},{2,1},{3,4},{4,3},{5,6},{6,5},{7,8},{8,7},{9,10},{10,9},{11,... | collective-permute-start | bytes 1572872 | tf_op jit(solution)/shard_map/ppermute | solution.py:396
  19.5 0.0 collective-permute-done.near_ref
  19.5 8.6 %collective-permute-done.1.far_ref = f32[64,8,256]{2,1,0:T(8,128)S(1)} collective-permute-done((f32[64,8,256]{2,1,0:T(8,128)S(1)}, f32[64,8,256]{2,1,0:T(8,128)S(1)}, u32[]{:S(2)}, u32[]{:S(2)}) %collective-permute-start.1) | collective-permute-done | bytes 524320 | tf_op jit(solution)/shard_map/ppermute | solution.py:396
  28.1 1.3 %collective-permute-start.2 = (f32[12,8,256]{2,1,0:T(8,128)S(1)}, f32[12,8,256]{2,1,0:T(8,128)S(1)}, u32[]{:S(2)}, u32[]{:S(2)}) collective-permute-start(f32[12,8,256]{2,1,0:T(8,128)S(1)} %get-tuple-element.22), channel_id=1, source_target_pairs={{256,0},{512,256},{768,512},{257,1},{513,257},{769,513},{258,2},{5... | collective-permute-start | bytes 294920 | tf_op jit(solution)/shard_map/ppermute | solution.py:401
  29.4 4.0 %collective-permute-start.3 = (f32[12,8,256]{2,1,0:T(8,128)S(1)}, f32[12,8,256]{2,1,0:T(8,128)S(1)}, u32[]{:S(2)}, u32[]{:S(2)}) collective-permute-start(f32[12,8,256]{2,1,0:T(8,128)S(1)} %get-tuple-element.23), channel_id=1, source_target_pairs={{0,256},{256,512},{512,768},{1,257},{257,513},{513,769},{2,258},{2... | collective-permute-start | bytes 294920 | tf_op jit(solution)/shard_map/ppermute | solution.py:400
  33.4 0.1 collective-permute-done.2.begin_ref
  33.5 1.6 %collective-permute-done.3.end_ref = f32[12,8,256]{2,1,0:T(8,128)S(1)} collective-permute-done((f32[12,8,256]{2,1,0:T(8,128)S(1)}, f32[12,8,256]{2,1,0:T(8,128)S(1)}, u32[]{:S(2)}, u32[]{:S(2)}) %collective-permute-start.3) | collective-permute-done | bytes 98336 | tf_op jit(solution)/shard_map/ppermute | solution.py:400
  35.0 4.1 %fine.1 = (f32[32,1,128]{2,1,0:T(1,128)S(1)}, f32[72,16,256]{2,1,0:T(8,128)S(1)}, f32[72,16,256]{2,1,0:T(8,128)S(1)}, f32[72,16,256]{2,1,0:T(8,128)S(1)}, f32[72...) custom-call(f32[64,8,256]{2,1,0:T(8,128)S(1)} %get-tuple-element.18.r_ref, ...), custom_call_target="tpu_custom_call" | custom-call | tf_op jit(solution)/shard_map/fine/pallas_call | solution.py:404
  39.2 12.3 %all_to_all.10.part_ref = f32[32,1,128]{2,1,0:T(1,128)S(1)} all-to-all(f32[32,1,128]{2,1,0:T(1,128)S(1)} %get-tuple-element.24), channel_id=1, replica_groups=mesh['group'=4,'z'=16,'y'=8,'core'=2] {'group','y'}, dimensions={0} | all-to-all | bytes 32768 | tf_op jit(solution)/shard_map/all_to_all | solution.py:372
  51.5 28.4 %all_to_all.11.sums_ref = f32[32,1,128]{2,1,0:T(1,128)S(1)} all-to-all(f32[32,1,128]{2,1,0:T(1,128)S(1)} %merge.1), channel_id=1, replica_groups=mesh['group'=4,'z'=16,'y'=8,'core'=2] {'z','core'}, dimensions={0} | all-to-all | bytes 32768 | tf_op jit(solution)/shard_map/all_to_all | solution.py:372
  79.9 4.3 %last.1 = f32[64,8,256]{2,1,0:T(8,128)} custom-call(f32[32,1,128]{2,1,0:T(1,128)S(1)} %all_to_all.11.sums_ref, f32[72,16,256]{2,1,0:T(8,128)S(1)} %get-tuple-element.25.v_ref, f32[72,16,256]{2,1,0:T(8,128)S(1)} %get-tuple-element.26.tx_ref, f32[72,16,256]{2,1,0:T(8,128)S(1)} %get-tuple-element.27.ty_ref, f32[72,16,256]{2,1,0:T(8,128)S(1)} %get-tuple-element.28.tz_ref, ...), custom_call_target="tpu_custom_call" | custom-call | tf_op jit(solution)/shard_map/last/pallas_call | solution.py:415
  (2 shorter events, 0.1 us)
Async XLA Ops:
  1.5 18.0 %collective-permute-start = (f32[64,8,256]{2,1,0:T(8,128)S(1)}, f32[64,8,256]{2,1,0:T(8,128)S(1)}, u32[]{:S(2)}, u32[]{:S(2)}) collective-permute-start(f32[64,8,256]{2,1,0:T(8,128)S(1)} %get-tuple-element.20), channel_id=1, source_target_pairs={{0,1},{1,0},{2,3},{3,2},{4,5},{5,4},{6,7},{7,6},{8,9},{9,8},{10,11... | collective-permute-start | bytes 1572872 | tf_op jit(solution)/shard_map/ppermute | solution.py:397
  17.6 10.5 %collective-permute-start.1 = (f32[64,8,256]{2,1,0:T(8,128)S(1)}, f32[64,8,256]{2,1,0:T(8,128)S(1)}, u32[]{:S(2)}, u32[]{:S(2)}) collective-permute-start(f32[64,8,256]{2,1,0:T(8,128)S(1)} %get-tuple-element.21), channel_id=1, source_target_pairs={{1,2},{2,1},{3,4},{4,3},{5,6},{6,5},{7,8},{8,7},{9,10},{10,9},{11,... | collective-permute-start | bytes 1572872 | tf_op jit(solution)/shard_map/ppermute | solution.py:396
  28.1 5.4 %collective-permute-start.2 = (f32[12,8,256]{2,1,0:T(8,128)S(1)}, f32[12,8,256]{2,1,0:T(8,128)S(1)}, u32[]{:S(2)}, u32[]{:S(2)}) collective-permute-start(f32[12,8,256]{2,1,0:T(8,128)S(1)} %get-tuple-element.22), channel_id=1, source_target_pairs={{256,0},{512,256},{768,512},{257,1},{513,257},{769,513},{258,2},{5... | collective-permute-start | bytes 294920 | tf_op jit(solution)/shard_map/ppermute | solution.py:401
  29.4 5.6 %collective-permute-start.3 = (f32[12,8,256]{2,1,0:T(8,128)S(1)}, f32[12,8,256]{2,1,0:T(8,128)S(1)}, u32[]{:S(2)}, u32[]{:S(2)}) collective-permute-start(f32[12,8,256]{2,1,0:T(8,128)S(1)} %get-tuple-element.23), channel_id=1, source_target_pairs={{0,256},{256,512},{512,768},{1,257},{257,513},{513,769},{2,258},{2... | collective-permute-start | bytes 294920 | tf_op jit(solution)/shard_map/ppermute | solution.py:400

commit v4 on v3

--- a/solution.py
+++ b/solution.py
@@ -41,13 +41,22 @@
     return jax.ShapeDtypeStruct(shape, jnp.float32)
 
 
+def low_half(shape):
+    return lax.broadcasted_iota(jnp.int32, shape, 0) < shape[0] // 2
+
+
+def row_tiles(r, source):
+    low = low_half(r.shape)
+    half = r.shape[0] // 2
+    return jnp.where(low, r, pltpu.roll(source, half, 0)), jnp.where(low, pltpu.roll(r, half, 0), source)
+
+
 def rows_kernel(
     chunks, table_hbm, facies_hbm, source_hbm, r_ref, source_ref, near_ref, far_ref,
     table_ref, facies_ref, table_sem, sems,
 ):
     core = position()[2]
     planes, rows, depth = facies_ref.shape
-    low = lax.broadcasted_iota(jnp.int32, (rows, depth), 0) < rows // 2
     kinds = table_ref.shape[0]
     first = core == 0
     step = planes // chunks
@@ -77,8 +86,7 @@
             r = 1.0 / perm
             source = source_ref[x]
             r_ref[x] = r
-            begin = jnp.where(low, r, pltpu.roll(source, rows // 2, 0))
-            end = jnp.where(low, pltpu.roll(r, rows // 2, 0), source)
+            begin, end = row_tiles(r, source)
             near_ref[x] = jnp.where(first, end, begin)
             far_ref[x] = jnp.where(first, begin, end)
             return carry
@@ -86,39 +94,39 @@
         lax.fori_loop(chunk * step, (chunk + 1) * step, body, 0, unroll=8)
 
 
-def halo_rows(near_ref, far_ref, x, core, tile, tiles):
-    rows = far_ref.shape[1]
-    depth = far_ref.shape[2]
-    low = lax.broadcasted_iota(jnp.int32, (rows, depth), 0) < rows // 2
-    near = near_ref[x]
-    far = far_ref[x]
+def halo_rows(near, far, core, tile, tiles):
+    low = low_half(near.shape)
     first = core == 0
     after = jnp.where(first, near, far)
     before = jnp.where(first, far, near)
-    r = jnp.where(low, after, pltpu.roll(before, rows // 2, 0))
-    source = jnp.where(low, pltpu.roll(after, rows // 2, 0), before)
+    half = near.shape[0] // 2
+    r = jnp.where(low, after, pltpu.roll(before, half, 0))
+    source = jnp.where(low, pltpu.roll(after, half, 0), before)
     absent = (low & (tile == tiles - 1)) | (~low & (tile == 0))
     return jnp.where(absent, 1.0, r), jnp.where(absent, 0.0, source)
 
 
-def planes_kernel(r_ref, source_ref, near_ref, far_ref, begin_ref, end_ref):
-    _, tile, core, _ = position()
-    tiles = lax.axis_size("z") * lax.axis_size("y") * lax.axis_size("core")
+def planes_kernel(r_ref, source_ref, near_ref, begin_ref, end_ref):
     planes = r_ref.shape[0]
     for d in range(HALO):
         for out, x in ((begin_ref, d), (end_ref, planes - 1 - d)):
             out[d] = r_ref[x]
             if d < HALO - 1:
-                side_r, side_source = halo_rows(near_ref, far_ref, x, core, tile, tiles)
-                out[4 + d] = side_r
+                out[4 + d] = near_ref[x]
                 out[7 + d] = source_ref[x]
-                if d < HALO - 2:
-                    out[10 + d] = side_source
+
+
+def corners_kernel(begin_ref, end_ref, out_ref):
+    first = position()[2] == 0
+    for side, recv in enumerate((begin_ref, end_ref)):
+        for d in range(HALO - 1):
+            begin, end = row_tiles(recv[d], recv[7 + d])
+            out_ref[3 * side + d] = jnp.where(first, begin, end)
 
 
 def fine_kernel(
     storage,
-    r_ref, source_ref, near_ref, far_ref, begin_ref, end_ref,
+    r_ref, source_ref, near_ref, far_ref, begin_ref, end_ref, corner_ref,
     sums_ref, v_ref, tx_ref, ty_ref, tz_ref, w_ref, ws_ref,
     rr_ref, ss_ref, h_ref,
 ):
@@ -130,17 +138,22 @@
     ones = jnp.ones((rows, depth), jnp.float32)
     zeros = jnp.zeros((rows, depth), jnp.float32)
     for d in range(HALO):
-        for recv, x, there in (
-            (end_ref, HALO - 1 - d, group > 0),
-            (begin_ref, HALO + planes + d, group < groups - 1),
+        for side, recv, x, there in (
+            (1, end_ref, HALO - 1 - d, group > 0),
+            (0, begin_ref, HALO + planes + d, group < groups - 1),
         ):
+            side_r, side_source, own_source = ones, zeros, zeros
+            if d < HALO - 1:
+                far = corner_ref[3 * side + d]
+                side_r, side_source = halo_rows(recv[4 + d], far, core, tile, tiles)
+                own_source = recv[7 + d]
             rr_ref[x, 0:rows] = jnp.where(there, recv[d], 1.0)
-            rr_ref[x, rows:ROWS] = jnp.where(there, recv[4 + d], 1.0) if d < HALO - 1 else ones
-            ss_ref[x, 0:rows] = jnp.where(there, recv[7 + d], 0.0) if d < HALO - 1 else zeros
-            ss_ref[x, rows:ROWS] = jnp.where(there, recv[10 + d], 0.0) if d < HALO - 2 else zeros
+            rr_ref[x, rows:ROWS] = jnp.where(there, side_r, 1.0)
+            ss_ref[x, 0:rows] = jnp.where(there, own_source, 0.0)
+            ss_ref[x, rows:ROWS] = jnp.where(there, side_source, 0.0)
 
     def gather_rows(x, carry):
-        side_r, side_source = halo_rows(near_ref, far_ref, x, core, tile, tiles)
+        side_r, side_source = halo_rows(near_ref[x], far_ref[x], core, tile, tiles)
         rr_ref[HALO + x, 0:rows] = r_ref[x]
         rr_ref[HALO + x, rows:ROWS] = side_r
         ss_ref[HALO + x, 0:rows] = source_ref[x]
@@ -395,19 +408,21 @@
     pairs = [p for i in range(1, tiles - 1, 2) for p in ((i, i + 1), (i + 1, i))]
     far = lax.ppermute(far, TILE_AXES, pairs)
     near = lax.ppermute(near, "core", [(0, 1), (1, 0)])
-    slab = f32(12, rows, depth)
-    begin, end = call(planes_kernel, (slab, slab), [VMEM] * 4, name="planes")(r, source, near, far)
+    slab = f32(10, rows, depth)
+    begin, end = call(planes_kernel, (slab, slab), [VMEM] * 3, name="planes")(r, source, near)
     end = lax.ppermute(end, "group", [(i, i + 1) for i in range(groups - 1)])
     begin = lax.ppermute(begin, "group", [(i + 1, i) for i in range(groups - 1)])
+    corner = call(corners_kernel, f32(6, rows, depth), [VMEM] * 2, name="corners")(begin, end)
+    corner = lax.ppermute(corner, TILE_AXES, pairs)
     wide = f32(planes + 2 * HALO, ROWS, depth)
     scratch = [pltpu.VMEM(wide.shape, jnp.float32)]
     sums, *fields = call(
         functools.partial(fine_kernel, storage),
         (f32(groups * y_size, 1, 128),) + (wide,) * 6,
-        [VMEM] * 6,
+        [VMEM] * 7,
         scratch * 3,
         name="fine",
-    )(r, source, near, far, begin, end)
+    )(r, source, near, far, begin, end, corner)
     sums = spread(sums, ("group", "y"))
     sums = call(merge_kernel, f32(z_size * cores, 1, 128), [VMEM], name="merge")(sums)
     sums = spread(sums, ("z", "core"))

time: 84.4 us -> 81.7 us (0.968)
  waiting for transfers between devices: 10.2 us -> 3.22 us
  starting transfers between devices: 23.3 us -> 28 us
    ppermute x1, waiting for transfers between devices: 8.56 us -> 0.01 us  [on_device(): far = lax.ppermute(far, TILE_AXES, pairs)]
    ppermute x0 -> x1, starting transfers between devices: none -> 4.78 us  [on_device(): corner = lax.ppermute(corner, TILE_AXES, pairs)]
    ppermute x0 -> x1, waiting for transfers between devices: none -> 1.75 us  [on_device(): corner = lax.ppermute(corner, TILE_AXES, pairs)]
  transfers between devices with their start and end apart: 4 -> 5, of which waited for: 3 -> 3; matrix products, arithmetic and copies ran while one was open for 0% -> 0% of each run, Pallas kernels for 0% -> 0%
where the time goes in v4:
time: 81.7 us; the launch traced here: 81.4 us
  blocking collectives  40.1 us (49%)
  starting transfers between devices  28 us (34%)
  Pallas kernels  9.94 us (12%)
  waiting for transfers between devices  3.22 us (4%)
    all_to_all x2, blocking collectives, spread(): return lax.all_to_all(block, axes, 0, 0)  40.1 us
    ppermute x1, starting transfers between devices, on_device(): near = lax.ppermute(near, 'core', [(0, 1), (1, 0)])  16.1 us
    ppermute x1, starting transfers between devices, on_device(): corner = lax.ppermute(corner, TILE_AXES, pairs)  4.78 us
    pallas_call x1, Pallas kernels, on_device(): call(functools.partial(last_kernel, storage * planes * rows * depth, tile...  4.26 us
    pallas_call x1, Pallas kernels, on_device(): call(functools.partial(fine_kernel, storage), (f32(groups * y_size, 1, 12...  4.12 us
    ppermute x1, starting transfers between devices, on_device(): end = lax.ppermute(end, 'group', [(i, i + 1) for i in range(groups - 1)])  3.99 us
    ppermute x1, starting transfers between devices, on_device(): far = lax.ppermute(far, TILE_AXES, pairs)  1.92 us
    ppermute x1, waiting for transfers between devices, on_device(): corner = lax.ppermute(corner, TILE_AXES, pairs)  1.75 us
  transfers between devices with their start and end apart: 5, of which 3 were waited for; matrix products, arithmetic and copies ran while one was open for 0% of the time, Pallas kernels for 0%

profile of v4, /device:TPU:1, one launch (start us, length us, event | category | flops | bytes accessed | tf_op | source)
XLA Modules:
  0.0 81.4 jit_solution(9022722437282979353)
XLA Ops:
  0.0 1.5 %rows.1 = (f32[64,8,256]{2,1,0:T(8,128)S(1)}, f32[64,8,256]{2,1,0:T(8,128)S(1)}, f32[64,8,256]{2,1,0:T(8,128)S(1)}, f32[64,8,256]{2,1,0:T(8,128)S(1)}) custom-call(f32[8]{0:T(128)} %table_hbm.1, s32[64,8,256]{2,1,0:T(8,128)} %facies_hbm.1, f32[64,8,256]{2,1,0:T(8,128)} %source_hbm.1), custom_call_target="tpu_custom_call" | custom-call | tf_op jit(solution)/shard_map/rows/pallas_call | solution.py:396
  1.5 16.1 %collective-permute-start = (f32[64,8,256]{2,1,0:T(8,128)S(1)}, f32[64,8,256]{2,1,0:T(8,128)S(1)}, u32[]{:S(2)}, u32[]{:S(2)}) collective-permute-start(f32[64,8,256]{2,1,0:T(8,128)S(1)} %get-tuple-element.20), channel_id=1, source_target_pairs={{0,1},{1,0},{2,3},{3,2},{4,5},{5,4},{6,7},{7,6},{8,9},{9,8},{10,11... | collective-permute-start | bytes 1572872 | tf_op jit(solution)/shard_map/ppermute | solution.py:410
  17.6 1.9 %collective-permute-start.1 = (f32[64,8,256]{2,1,0:T(8,128)S(1)}, f32[64,8,256]{2,1,0:T(8,128)S(1)}, u32[]{:S(2)}, u32[]{:S(2)}) collective-permute-start(f32[64,8,256]{2,1,0:T(8,128)S(1)} %get-tuple-element.21), channel_id=1, source_target_pairs={{1,2},{2,1},{3,4},{4,3},{5,6},{6,5},{7,8},{8,7},{9,10},{10,9},{11,... | collective-permute-start | bytes 1572872 | tf_op jit(solution)/shard_map/ppermute | solution.py:409
  19.5 0.0 collective-permute-done.near_ref
  19.5 1.3 %collective-permute-start.2 = (f32[10,8,256]{2,1,0:T(8,128)S(1)}, f32[10,8,256]{2,1,0:T(8,128)S(1)}, u32[]{:S(2)}, u32[]{:S(2)}) collective-permute-start(f32[10,8,256]{2,1,0:T(8,128)S(1)} %get-tuple-element.22), channel_id=1, source_target_pairs={{256,0},{512,256},{768,512},{257,1},{513,257},{769,513},{258,2},{5... | collective-permute-start | bytes 245768 | tf_op jit(solution)/shard_map/ppermute | solution.py:414
  20.8 4.0 %collective-permute-start.3 = (f32[10,8,256]{2,1,0:T(8,128)S(1)}, f32[10,8,256]{2,1,0:T(8,128)S(1)}, u32[]{:S(2)}, u32[]{:S(2)}) collective-permute-start(f32[10,8,256]{2,1,0:T(8,128)S(1)} %get-tuple-element.23), channel_id=1, source_target_pairs={{0,256},{256,512},{512,768},{1,257},{257,513},{513,769},{2,258},{2... | collective-permute-start | bytes 245768 | tf_op jit(solution)/shard_map/ppermute | solution.py:413
  24.8 0.7 collective-permute-done.2.begin_ref
  25.6 0.7 collective-permute-done.3.end_ref
  26.3 4.8 %collective-permute-start.4 = (f32[6,8,256]{2,1,0:T(8,128)S(1)}, f32[6,8,256]{2,1,0:T(8,128)S(1)}, u32[]{:S(2)}, u32[]{:S(2)}) collective-permute-start(f32[6,8,256]{2,1,0:T(8,128)S(1)} %corners.1), channel_id=1, source_target_pairs={{1,2},{2,1},{3,4},{4,3},{5,6},{6,5},{7,8},{8,7},{9,10},{10,9},{11,... | collective-permute-start | bytes 147464 | tf_op jit(solution)/shard_map/ppermute | solution.py:416
  31.1 0.0 collective-permute-done.1.far_ref
  31.1 1.7 %collective-permute-done.4.corner_ref = f32[6,8,256]{2,1,0:T(8,128)S(1)} collective-permute-done((f32[6,8,256]{2,1,0:T(8,128)S(1)}, f32[6,8,256]{2,1,0:T(8,128)S(1)}, u32[]{:S(2)}, u32[]{:S(2)}) %collective-permute-start.4) | collective-permute-done | bytes 49184 | tf_op jit(solution)/shard_map/ppermute | solution.py:416
  32.9 4.1 %fine.1 = (f32[32,1,128]{2,1,0:T(1,128)S(1)}, f32[72,16,256]{2,1,0:T(8,128)S(1)}, f32[72,16,256]{2,1,0:T(8,128)S(1)}, f32[72,16,256]{2,1,0:T(8,128)S(1)}, f32[72...) custom-call(f32[64,8,256]{2,1,0:T(8,128)S(1)} %get-tuple-element.18.r_ref, ...), custom_call_target="tpu_custom_call" | custom-call | tf_op jit(solution)/shard_map/fine/pallas_call | solution.py:419
  37.0 12.3 %all_to_all.10.part_ref = f32[32,1,128]{2,1,0:T(1,128)S(1)} all-to-all(f32[32,1,128]{2,1,0:T(1,128)S(1)} %get-tuple-element.24), channel_id=1, replica_groups=mesh['group'=4,'z'=16,'y'=8,'core'=2] {'group','y'}, dimensions={0} | all-to-all | bytes 32768 | tf_op jit(solution)/shard_map/all_to_all | solution.py:385
  49.3 27.8 %all_to_all.11.sums_ref = f32[32,1,128]{2,1,0:T(1,128)S(1)} all-to-all(f32[32,1,128]{2,1,0:T(1,128)S(1)} %merge.1), channel_id=1, replica_groups=mesh['group'=4,'z'=16,'y'=8,'core'=2] {'z','core'}, dimensions={0} | all-to-all | bytes 32768 | tf_op jit(solution)/shard_map/all_to_all | solution.py:385
  77.1 4.3 %last.1 = f32[64,8,256]{2,1,0:T(8,128)} custom-call(f32[32,1,128]{2,1,0:T(1,128)S(1)} %all_to_all.11.sums_ref, f32[72,16,256]{2,1,0:T(8,128)S(1)} %get-tuple-element.25.v_ref, f32[72,16,256]{2,1,0:T(8,128)S(1)} %get-tuple-element.26.tx_ref, f32[72,16,256]{2,1,0:T(8,128)S(1)} %get-tuple-element.27.ty_ref, f32[72,16,256]{2,1,0:T(8,128)S(1)} %get-tuple-element.28.tz_ref, ...), custom_call_target="tpu_custom_call" | custom-call | tf_op jit(solution)/shard_map/last/pallas_call | solution.py:430
  (3 shorter events, 0.1 us)
Async XLA Ops:
  1.5 18.0 %collective-permute-start = (f32[64,8,256]{2,1,0:T(8,128)S(1)}, f32[64,8,256]{2,1,0:T(8,128)S(1)}, u32[]{:S(2)}, u32[]{:S(2)}) collective-permute-start(f32[64,8,256]{2,1,0:T(8,128)S(1)} %get-tuple-element.20), channel_id=1, source_target_pairs={{0,1},{1,0},{2,3},{3,2},{4,5},{5,4},{6,7},{7,6},{8,9},{9,8},{10,11... | collective-permute-start | bytes 1572872 | tf_op jit(solution)/shard_map/ppermute | solution.py:410
  17.6 13.5 %collective-permute-start.1 = (f32[64,8,256]{2,1,0:T(8,128)S(1)}, f32[64,8,256]{2,1,0:T(8,128)S(1)}, u32[]{:S(2)}, u32[]{:S(2)}) collective-permute-start(f32[64,8,256]{2,1,0:T(8,128)S(1)} %get-tuple-element.21), channel_id=1, source_target_pairs={{1,2},{2,1},{3,4},{4,3},{5,6},{6,5},{7,8},{8,7},{9,10},{10,9},{11,... | collective-permute-start | bytes 1572872 | tf_op jit(solution)/shard_map/ppermute | solution.py:409
  19.5 6.0 %collective-permute-start.2 = (f32[10,8,256]{2,1,0:T(8,128)S(1)}, f32[10,8,256]{2,1,0:T(8,128)S(1)}, u32[]{:S(2)}, u32[]{:S(2)}) collective-permute-start(f32[10,8,256]{2,1,0:T(8,128)S(1)} %get-tuple-element.22), channel_id=1, source_target_pairs={{256,0},{512,256},{768,512},{257,1},{513,257},{769,513},{258,2},{5... | collective-permute-start | bytes 245768 | tf_op jit(solution)/shard_map/ppermute | solution.py:414
  20.8 5.5 %collective-permute-start.3 = (f32[10,8,256]{2,1,0:T(8,128)S(1)}, f32[10,8,256]{2,1,0:T(8,128)S(1)}, u32[]{:S(2)}, u32[]{:S(2)}) collective-permute-start(f32[10,8,256]{2,1,0:T(8,128)S(1)} %get-tuple-element.23), channel_id=1, source_target_pairs={{0,256},{256,512},{512,768},{1,257},{257,513},{513,769},{2,258},{2... | collective-permute-start | bytes 245768 | tf_op jit(solution)/shard_map/ppermute | solution.py:413
  26.3 6.5 %collective-permute-start.4 = (f32[6,8,256]{2,1,0:T(8,128)S(1)}, f32[6,8,256]{2,1,0:T(8,128)S(1)}, u32[]{:S(2)}, u32[]{:S(2)}) collective-permute-start(f32[6,8,256]{2,1,0:T(8,128)S(1)} %corners.1), channel_id=1, source_target_pairs={{1,2},{2,1},{3,4},{4,3},{5,6},{6,5},{7,8},{8,7},{9,10},{10,9},{11,... | collective-permute-start | bytes 147464 | tf_op jit(solution)/shard_map/ppermute | solution.py:416

commit v5 on v4

--- a/solution.py
+++ b/solution.py
@@ -23,7 +23,7 @@
     return lax.axis_index("group"), tile, core, y
 
 
-def call(kernel, out_shape, in_specs, scratch=(), name=None, cost=None):
+def call(kernel, out_shape, in_specs, scratch=(), name=None, aliases=None):
     outs = jax.tree.map(lambda _: VMEM, out_shape)
     return pl.pallas_call(
         kernel,
@@ -32,7 +32,7 @@
         out_specs=outs,
         scratch_shapes=list(scratch),
         name=name,
-        cost_estimate=cost,
+        input_output_aliases=aliases or {},
         compiler_params=pltpu.CompilerParams(vmem_limit_bytes=24 * 1024 * 1024),
     )
 
@@ -124,100 +124,149 @@
             out_ref[3 * side + d] = jnp.where(first, begin, end)
 
 
-def fine_kernel(
+class Walls:
+    def __init__(self, planes, rows, depth):
+        self.group, self.tile, self.core, self.y = position()
+        self.groups = lax.axis_size("group")
+        self.tiles = lax.axis_size("z") * lax.axis_size("y") * lax.axis_size("core")
+        self.planes, self.rows, self.depth = planes, rows, depth
+        self.row = lax.broadcasted_iota(jnp.int32, (ROWS, depth), 0)
+        column = lax.broadcasted_iota(jnp.int32, (ROWS, depth), 1)
+        top = (self.row == ROWS - 1) & (self.tile == 0)
+        self.in_y = top | ((self.row == rows - 1) & (self.tile == self.tiles - 1))
+        self.in_z = column == depth - 1
+
+    def faces(self, storage, x, before, tx, rr_ref, ss_ref, refs):
+        ty_ref, tz_ref, w_ref, ws_ref = refs
+        r = rr_ref[x]
+        ty = jnp.where(self.in_y, 0.0, 2.0 / (r + pltpu.roll(r, ROWS - 1, 0)))
+        tz = jnp.where(self.in_z, 0.0, 2.0 / (r + pltpu.roll(r, self.depth - 1, 1)))
+        diagonal = storage + tx + before + ty + pltpu.roll(ty, 1, 0) + tz + pltpu.roll(tz, 1, 1)
+        w = RELAX / diagonal
+        ty_ref[x] = ty
+        tz_ref[x] = tz
+        w_ref[x] = w
+        ws_ref[x] = w * ss_ref[x]
+
+
+def middle_kernel(
     storage,
-    r_ref, source_ref, near_ref, far_ref, begin_ref, end_ref, corner_ref,
-    sums_ref, v_ref, tx_ref, ty_ref, tz_ref, w_ref, ws_ref,
-    rr_ref, ss_ref, h_ref,
+    r_ref, source_ref, near_ref, far_ref,
+    part_ref, v_ref, tx_ref, ty_ref, tz_ref, w_ref, ws_ref, rr_ref, ss_ref,
 ):
-    group, tile, core, y_pos = position()
-    groups = lax.axis_size("group")
-    tiles = lax.axis_size("z") * lax.axis_size("y") * lax.axis_size("core")
     planes, rows, depth = r_ref.shape
-    wide = planes + 2 * HALO
+    walls = Walls(planes, rows, depth)
+    first, last = HALO, HALO + planes - 1
+
+    def gather_rows(x, carry):
+        side_r, side_source = halo_rows(near_ref[x], far_ref[x], walls.core, walls.tile, walls.tiles)
+        rr_ref[HALO + x, 0:rows] = r_ref[x]
+        rr_ref[HALO + x, rows:ROWS] = side_r
+        ss_ref[HALO + x, 0:rows] = source_ref[x]
+        ss_ref[HALO + x, rows:ROWS] = side_source
+        return carry
+
+    lax.fori_loop(0, planes, gather_rows, 0, unroll=16)
+    refs = ty_ref, tz_ref, w_ref, ws_ref
+
+    def faces(x, before):
+        tx = 2.0 / (rr_ref[x] + rr_ref[x + 1])
+        tx_ref[x] = tx
+        walls.faces(storage, x, before, tx, rr_ref, ss_ref, refs)
+        return tx
+
+    start = 2.0 / (rr_ref[first] + rr_ref[first + 1])
+    tx_ref[first] = start
+    lax.fori_loop(first + 1, last, faces, start, unroll=16)
+
+    def second(x, carry):
+        total, y_flux, link_y, before = carry
+        ty = ty_ref[x]
+        v, ahead = relax(
+            ws_ref[x], ws_ref[x + 1], before, tx_ref[x], ty, tz_ref[x], w_ref[x], ws_ref[x], depth
+        )
+        v_ref[x] = v
+        total = total + ss_ref[x, 0:rows] - storage * v[0:rows]
+        y_flux = y_flux + ty * (v - pltpu.roll(v, ROWS - 1, 0))
+        return total, y_flux, link_y + ty[0:rows], ahead
+
+    zeros = jnp.zeros((rows, depth), jnp.float32)
+    carry = zeros, jnp.zeros((ROWS, depth), jnp.float32), zeros, start_flow(tx_ref, ws_ref, first + 1)
+    total, y_flux, link_y, _ = lax.fori_loop(first + 2, last - 1, second, carry, unroll=15)
+    part_ref[0:rows] = total
+    part_ref[rows : rows + ROWS] = y_flux
+    part_ref[rows + ROWS :] = link_y
+
+
+def start_flow(tx_ref, h_ref, x):
+    return tx_ref[x] * h_ref[x]
+
+
+def edges_kernel(
+    storage,
+    begin_ref, end_ref, corner_ref,
+    part_ref, v_in, tx_in, ty_in, tz_in, w_in, ws_in, rr_in, ss_in,
+    sums_ref, v_ref, tx_ref, ty_ref, tz_ref, w_ref, ws_ref, rr_ref, ss_ref,
+):
+    wide, _, depth = v_ref.shape
+    planes, rows = wide - 2 * HALO, begin_ref.shape[1]
+    walls = Walls(planes, rows, depth)
+    first, last = HALO, HALO + planes - 1
+    group, row = walls.group, walls.row
     ones = jnp.ones((rows, depth), jnp.float32)
     zeros = jnp.zeros((rows, depth), jnp.float32)
     for d in range(HALO):
         for side, recv, x, there in (
-            (1, end_ref, HALO - 1 - d, group > 0),
-            (0, begin_ref, HALO + planes + d, group < groups - 1),
+            (1, end_ref, first - 1 - d, group > 0),
+            (0, begin_ref, last + 1 + d, group < walls.groups - 1),
         ):
             side_r, side_source, own_source = ones, zeros, zeros
             if d < HALO - 1:
                 far = corner_ref[3 * side + d]
-                side_r, side_source = halo_rows(recv[4 + d], far, core, tile, tiles)
+                side_r, side_source = halo_rows(recv[4 + d], far, walls.core, walls.tile, walls.tiles)
                 own_source = recv[7 + d]
             rr_ref[x, 0:rows] = jnp.where(there, recv[d], 1.0)
             rr_ref[x, rows:ROWS] = jnp.where(there, side_r, 1.0)
             ss_ref[x, 0:rows] = jnp.where(there, own_source, 0.0)
             ss_ref[x, rows:ROWS] = jnp.where(there, side_source, 0.0)
 
-    def gather_rows(x, carry):
-        side_r, side_source = halo_rows(near_ref[x], far_ref[x], core, tile, tiles)
-        rr_ref[HALO + x, 0:rows] = r_ref[x]
-        rr_ref[HALO + x, rows:ROWS] = side_r
-        ss_ref[HALO + x, 0:rows] = source_ref[x]
-        ss_ref[HALO + x, rows:ROWS] = side_source
-        return carry
-
-    lax.fori_loop(0, planes, gather_rows, 0, unroll=16)
-
-    row = lax.broadcasted_iota(jnp.int32, (ROWS, depth), 0)
-    column = lax.broadcasted_iota(jnp.int32, (ROWS, depth), 1)
-    y_wall = ((row == ROWS - 1) & (tile == 0)) | ((row == rows - 1) & (tile == tiles - 1))
-    z_wall = column == depth - 1
-
-    def faces(x, before):
-        r = rr_ref[x]
-        x_wall = ((x == HALO - 1) & (group == 0)) | ((x == HALO + planes - 1) & (group == groups - 1))
-        tx = jnp.where(x_wall, 0.0, 2.0 / (r + rr_ref[x + 1]))
-        ty = jnp.where(y_wall, 0.0, 2.0 / (r + pltpu.roll(r, ROWS - 1, 0)))
-        tz = jnp.where(z_wall, 0.0, 2.0 / (r + pltpu.roll(r, depth - 1, 1)))
-        diagonal = storage + tx + before + ty + pltpu.roll(ty, 1, 0) + tz + pltpu.roll(tz, 1, 1)
-        w = RELAX / diagonal
-        ws = w * ss_ref[x]
-        tx_ref[x] = tx
-        ty_ref[x] = ty
-        tz_ref[x] = tz
-        w_ref[x] = w
-        ws_ref[x] = ws
-        h_ref[x] = ws
-        return tx
-
-    start = 2.0 / (rr_ref[0] + rr_ref[1])
-    lax.fori_loop(1, wide - 1, faces, start, unroll=16)
-
-    def second(x, carry):
-        total, y_flux, before = carry
-        h = h_ref[x]
-        tx = tx_ref[x]
-        v, ahead = relax(h, h_ref[x + 1], before, tx, ty_ref[x], tz_ref[x], w_ref[x], ws_ref[x], depth)
-        v_ref[x] = v
-        inside = (x >= HALO) & (x < HALO + planes)
-        total = total + jnp.where(inside, ss_ref[x, 0:rows] - storage * v[0:rows], 0.0)
-        flux = ty_ref[x] * (v - pltpu.roll(v, ROWS - 1, 0))
-        y_flux = y_flux + jnp.where(inside, flux, 0.0)
-        return total, y_flux, ahead
-
-    wide_zeros = jnp.zeros((ROWS, depth), jnp.float32)
-    first_flow = tx_ref[1] * h_ref[1]
-    total, y_flux, _ = lax.fori_loop(
-        2, wide - 2, second, (zeros, wide_zeros, first_flow), unroll=16
-    )
-    left, right = HALO - 1, HALO + planes - 1
-    out_left = tx_ref[left, 0:rows] * (v_ref[left + 1, 0:rows] - v_ref[left, 0:rows])
-    out_right = tx_ref[right, 0:rows] * (v_ref[right, 0:rows] - v_ref[right + 1, 0:rows])
+    refs = ty_ref, tz_ref, w_ref, ws_ref
+    for begin, end in ((1, first), (last, wide - 2)):
+        before = tx_ref[last - 1] if begin == last else 2.0 / (rr_ref[0] + rr_ref[1])
+        for x in range(begin, end + 1):
+            tx = 2.0 / (rr_ref[x] + rr_ref[x + 1])
+            if x == first - 1:
+                tx = jnp.where(group == 0, 0.0, tx)
+            if x == last:
+                tx = jnp.where(group == walls.groups - 1, 0.0, tx)
+            tx_ref[x] = tx
+            walls.faces(storage, x, before, tx, rr_ref, ss_ref, refs)
+            before = tx
+
+    total = part_ref[0:rows]
+    y_flux = part_ref[rows : rows + ROWS]
+    link_y = part_ref[rows + ROWS :]
+    for begin, end in ((2, first + 1), (last - 1, wide - 3)):
+        before = start_flow(tx_ref, ws_ref, begin - 1)
+        for x in range(begin, end + 1):
+            ty = ty_ref[x]
+            v, before = relax(
+                ws_ref[x], ws_ref[x + 1], before, tx_ref[x], ty, tz_ref[x], w_ref[x], ws_ref[x], depth
+            )
+            v_ref[x] = v
+            if first <= x <= last:
+                total = total + ss_ref[x, 0:rows] - storage * v[0:rows]
+                y_flux = y_flux + ty * (v - pltpu.roll(v, ROWS - 1, 0))
+                link_y = link_y + ty[0:rows]
+
+    out_left = tx_ref[first - 1, 0:rows] * (v_ref[first, 0:rows] - v_ref[first - 1, 0:rows])
+    out_right = tx_ref[last, 0:rows] * (v_ref[last, 0:rows] - v_ref[last + 1, 0:rows])
     side = jnp.where(row == ROWS - 1, y_flux, jnp.where(row == rows - 1, -y_flux, 0.0))
     rhs = total - out_left - out_right + side[0:rows] + side[rows:ROWS]
     rhs = jnp.sum(rhs, keepdims=True)
-    link_x = jnp.sum(tx_ref[right, 0:rows], keepdims=True)
-
-    def y_links(x, acc):
-        return acc + ty_ref[HALO + x, 0:rows]
-
-    link_y = lax.fori_loop(0, planes, y_links, zeros, unroll=8)
+    link_x = jnp.sum(tx_ref[last, 0:rows], keepdims=True)
     link_y = jnp.sum(jnp.where(row[0:rows] == rows - 1, link_y, 0.0), keepdims=True)
-    lane = lax.broadcasted_iota(jnp.int32, (1, 128), 1) - (32 * group + 4 * y_pos)
+    lane = lax.broadcasted_iota(jnp.int32, (1, 128), 1) - (32 * group + 4 * walls.y)
     packed = jnp.where(lane == 0, rhs, 0.0) + jnp.where(lane == 1, link_x, 0.0)
     packed = packed + jnp.where(lane == 2, link_y, 0.0)
     for peer in range(sums_ref.shape[0]):
@@ -416,13 +465,20 @@
     corner = lax.ppermute(corner, TILE_AXES, pairs)
     wide = f32(planes + 2 * HALO, ROWS, depth)
     scratch = [pltpu.VMEM(wide.shape, jnp.float32)]
+    part, *fields = call(
+        functools.partial(middle_kernel, storage),
+        (f32(2 * rows + ROWS, depth),) + (wide,) * 8,
+        [VMEM] * 4,
+        name="middle",
+    )(r, source, near, far)
     sums, *fields = call(
-        functools.partial(fine_kernel, storage),
-        (f32(groups * y_size, 1, 128),) + (wide,) * 6,
-        [VMEM] * 7,
-        scratch * 3,
-        name="fine",
-    )(r, source, near, far, begin, end, corner)
+        functools.partial(edges_kernel, storage),
+        (f32(groups * y_size, 1, 128),) + (wide,) * 8,
+        [VMEM] * 12,
+        name="edges",
+        aliases={4 + i: 1 + i for i in range(8)},
+    )(begin, end, corner, part, *fields)
+    fields = fields[:6]
     sums = spread(sums, ("group", "y"))
     sums = call(merge_kernel, f32(z_size * cores, 1, 128), [VMEM], name="merge")(sums)
     sums = spread(sums, ("z", "core"))

time: 81.7 us -> 78.6 us (0.962)
  blocking collectives: 40.1 us -> 38.1 us
  waiting for transfers between devices: 3.22 us -> 1.47 us
    all_to_all x2, blocking collectives: 40.1 us -> 38.1 us  [spread(): return lax.all_to_all(block, axes, 0, 0)]
    ppermute x1, waiting for transfers between devices: 1.75 us -> 0.01 us  [on_device(): corner = lax.ppermute(corner, TILE_AXES, pairs)]
    pallas_call x1 -> x2, Pallas kernels: 4.12 us -> 4.71 us  [the longest x1 4.27 us: on_device(): call(functools.partial(middle_kernel, storage), (f32(2 * rows + ROWS, dep...]
  transfers between devices with their start and end apart: 5 -> 5, of which waited for: 3 -> 2; matrix products, arithmetic and copies ran while one was open for 0% -> 0% of each run, Pallas kernels for 0% -> 5%
where the time goes in v5:
time: 78.6 us; the launch traced here: 78.3 us
  blocking collectives  38.1 us (48%)
  starting transfers between devices  28 us (36%)
  Pallas kernels  10.5 us (13%)
  waiting for transfers between devices  1.47 us (2%)
    all_to_all x2, blocking collectives, spread(): return lax.all_to_all(block, axes, 0, 0)  38.1 us
    ppermute x1, starting transfers between devices, on_device(): near = lax.ppermute(near, 'core', [(0, 1), (1, 0)])  16.1 us
    ppermute x1, starting transfers between devices, on_device(): corner = lax.ppermute(corner, TILE_AXES, pairs)  4.78 us
    pallas_call x1, Pallas kernels, on_device(): call(functools.partial(middle_kernel, storage), (f32(2 * rows + ROWS, dep...  4.27 us
    pallas_call x1, Pallas kernels, on_device(): call(functools.partial(last_kernel, storage * planes * rows * depth, tile...  4.26 us
    ppermute x1, starting transfers between devices, on_device(): end = lax.ppermute(end, 'group', [(i, i + 1) for i in range(groups - 1)])  3.99 us
    ppermute x1, starting transfers between devices, on_device(): far = lax.ppermute(far, TILE_AXES, pairs)  1.92 us
  transfers between devices with their start and end apart: 5, of which 2 were waited for; matrix products, arithmetic and copies ran while one was open for 0% of the time, Pallas kernels for 5%

profile of v5, /device:TPU:1, one launch (start us, length us, event | category | flops | bytes accessed | tf_op | source)
XLA Modules:
  0.0 78.3 jit_solution(10475176563046889663)
XLA Ops:
  0.0 1.5 %rows.1 = (f32[64,8,256]{2,1,0:T(8,128)S(1)}, f32[64,8,256]{2,1,0:T(8,128)S(1)}, f32[64,8,256]{2,1,0:T(8,128)S(1)}, f32[64,8,256]{2,1,0:T(8,128)S(1)}) custom-call(f32[8]{0:T(128)} %table_hbm.1, s32[64,8,256]{2,1,0:T(8,128)} %facies_hbm.1, f32[64,8,256]{2,1,0:T(8,128)} %source_hbm.1), custom_call_target="tpu_custom_call" | custom-call | tf_op jit(solution)/shard_map/rows/pallas_call | solution.py:445
  1.5 16.1 %collective-permute-start = (f32[64,8,256]{2,1,0:T(8,128)S(1)}, f32[64,8,256]{2,1,0:T(8,128)S(1)}, u32[]{:S(2)}, u32[]{:S(2)}) collective-permute-start(f32[64,8,256]{2,1,0:T(8,128)S(1)} %get-tuple-element.29), channel_id=1, source_target_pairs={{0,1},{1,0},{2,3},{3,2},{4,5},{5,4},{6,7},{7,6},{8,9},{9,8},{10,11... | collective-permute-start | bytes 1572872 | tf_op jit(solution)/shard_map/ppermute | solution.py:459
  17.6 1.9 %collective-permute-start.4 = (f32[64,8,256]{2,1,0:T(8,128)S(1)}, f32[64,8,256]{2,1,0:T(8,128)S(1)}, u32[]{:S(2)}, u32[]{:S(2)}) collective-permute-start(f32[64,8,256]{2,1,0:T(8,128)S(1)} %get-tuple-element.32), channel_id=1, source_target_pairs={{1,2},{2,1},{3,4},{4,3},{5,6},{6,5},{7,8},{8,7},{9,10},{10,9},{11,... | collective-permute-start | bytes 1572872 | tf_op jit(solution)/shard_map/ppermute | solution.py:458
  19.5 0.0 collective-permute-done.near_ref
  19.5 1.3 %collective-permute-start.1 = (f32[10,8,256]{2,1,0:T(8,128)S(1)}, f32[10,8,256]{2,1,0:T(8,128)S(1)}, u32[]{:S(2)}, u32[]{:S(2)}) collective-permute-start(f32[10,8,256]{2,1,0:T(8,128)S(1)} %get-tuple-element.30), channel_id=1, source_target_pairs={{256,0},{512,256},{768,512},{257,1},{513,257},{769,513},{258,2},{5... | collective-permute-start | bytes 245768 | tf_op jit(solution)/shard_map/ppermute | solution.py:463
  20.8 4.0 %collective-permute-start.2 = (f32[10,8,256]{2,1,0:T(8,128)S(1)}, f32[10,8,256]{2,1,0:T(8,128)S(1)}, u32[]{:S(2)}, u32[]{:S(2)}) collective-permute-start(f32[10,8,256]{2,1,0:T(8,128)S(1)} %get-tuple-element.31), channel_id=1, source_target_pairs={{0,256},{256,512},{512,768},{1,257},{257,513},{513,769},{2,258},{2... | collective-permute-start | bytes 245768 | tf_op jit(solution)/shard_map/ppermute | solution.py:462
  24.8 0.7 collective-permute-done.1.begin_ref
  25.6 0.7 collective-permute-done.2.end_ref
  26.3 4.8 %collective-permute-start.3 = (f32[6,8,256]{2,1,0:T(8,128)S(1)}, f32[6,8,256]{2,1,0:T(8,128)S(1)}, u32[]{:S(2)}, u32[]{:S(2)}) collective-permute-start(f32[6,8,256]{2,1,0:T(8,128)S(1)} %corners.1), channel_id=1, source_target_pairs={{1,2},{2,1},{3,4},{4,3},{5,6},{6,5},{7,8},{8,7},{9,10},{10,9},{11,... | collective-permute-start | bytes 147464 | tf_op jit(solution)/shard_map/ppermute | solution.py:465
  31.1 0.0 collective-permute-done.4.far_ref
  31.1 4.3 %middle.1 = (f32[32,256]{1,0:T(8,128)S(1)}, f32[72,16,256]{2,1,0:T(8,128)S(1)}, f32[72,16,256]{2,1,0:T(8,128)S(1)}, f32[72,16,256]{2,1,0:T(8,128)S(1)}, f32[72,1...) custom-call(f32[64,8,256]{2,1,0:T(8,128)S(1)} %get-tuple-element.27., ...), custom_call_target="tpu_custom_call" | custom-call | tf_op jit(solution)/shard_map/middle/pallas_call | solution.py:468
  35.4 0.0 collective-permute-done.3.corner_ref
  35.4 0.4 edges.1
  35.8 12.3 %all_to_all.10.part_ref = f32[32,1,128]{2,1,0:T(1,128)S(1)} all-to-all(f32[32,1,128]{2,1,0:T(1,128)S(1)} %get-tuple-element.42), channel_id=1, replica_groups=mesh['group'=4,'z'=16,'y'=8,'core'=2] {'group','y'}, dimensions={0} | all-to-all | bytes 32768 | tf_op jit(solution)/shard_map/all_to_all | solution.py:434
  48.2 25.8 %all_to_all.11.sums_ref = f32[32,1,128]{2,1,0:T(1,128)S(1)} all-to-all(f32[32,1,128]{2,1,0:T(1,128)S(1)} %merge.1), channel_id=1, replica_groups=mesh['group'=4,'z'=16,'y'=8,'core'=2] {'z','core'}, dimensions={0} | all-to-all | bytes 32768 | tf_op jit(solution)/shard_map/all_to_all | solution.py:434
  74.0 4.3 %last.1 = f32[64,8,256]{2,1,0:T(8,128)} custom-call(f32[32,1,128]{2,1,0:T(1,128)S(1)} %all_to_all.11.sums_ref, f32[72,16,256]{2,1,0:T(8,128)S(1)} %get-tuple-element.43.v_ref, f32[72,16,256]{2,1,0:T(8,128)S(1)} %get-tuple-element.44.tx_ref, f32[72,16,256]{2,1,0:T(8,128)S(1)} %get-tuple-element.45.ty_ref, f32[72,16,256]{2,1,0:T(8,128)S(1)} %get-tuple-element.46.tz_ref, ...), custom_call_target="tpu_custom_call" | custom-call | tf_op jit(solution)/shard_map/last/pallas_call | solution.py:486
  (3 shorter events, 0.1 us)
Async XLA Ops:
  1.5 18.0 %collective-permute-start = (f32[64,8,256]{2,1,0:T(8,128)S(1)}, f32[64,8,256]{2,1,0:T(8,128)S(1)}, u32[]{:S(2)}, u32[]{:S(2)}) collective-permute-start(f32[64,8,256]{2,1,0:T(8,128)S(1)} %get-tuple-element.29), channel_id=1, source_target_pairs={{0,1},{1,0},{2,3},{3,2},{4,5},{5,4},{6,7},{7,6},{8,9},{9,8},{10,11... | collective-permute-start | bytes 1572872 | tf_op jit(solution)/shard_map/ppermute | solution.py:459
  17.6 13.5 %collective-permute-start.4 = (f32[64,8,256]{2,1,0:T(8,128)S(1)}, f32[64,8,256]{2,1,0:T(8,128)S(1)}, u32[]{:S(2)}, u32[]{:S(2)}) collective-permute-start(f32[64,8,256]{2,1,0:T(8,128)S(1)} %get-tuple-element.32), channel_id=1, source_target_pairs={{1,2},{2,1},{3,4},{4,3},{5,6},{6,5},{7,8},{8,7},{9,10},{10,9},{11,... | collective-permute-start | bytes 1572872 | tf_op jit(solution)/shard_map/ppermute | solution.py:458
  19.5 6.0 %collective-permute-start.1 = (f32[10,8,256]{2,1,0:T(8,128)S(1)}, f32[10,8,256]{2,1,0:T(8,128)S(1)}, u32[]{:S(2)}, u32[]{:S(2)}) collective-permute-start(f32[10,8,256]{2,1,0:T(8,128)S(1)} %get-tuple-element.30), channel_id=1, source_target_pairs={{256,0},{512,256},{768,512},{257,1},{513,257},{769,513},{258,2},{5... | collective-permute-start | bytes 245768 | tf_op jit(solution)/shard_map/ppermute | solution.py:463
  20.8 5.5 %collective-permute-start.2 = (f32[10,8,256]{2,1,0:T(8,128)S(1)}, f32[10,8,256]{2,1,0:T(8,128)S(1)}, u32[]{:S(2)}, u32[]{:S(2)}) collective-permute-start(f32[10,8,256]{2,1,0:T(8,128)S(1)} %get-tuple-element.31), channel_id=1, source_target_pairs={{0,256},{256,512},{512,768},{1,257},{257,513},{513,769},{2,258},{2... | collective-permute-start | bytes 245768 | tf_op jit(solution)/shard_map/ppermute | solution.py:462
  26.3 9.1 %collective-permute-start.3 = (f32[6,8,256]{2,1,0:T(8,128)S(1)}, f32[6,8,256]{2,1,0:T(8,128)S(1)}, u32[]{:S(2)}, u32[]{:S(2)}) collective-permute-start(f32[6,8,256]{2,1,0:T(8,128)S(1)} %corners.1), channel_id=1, source_target_pairs={{1,2},{2,1},{3,4},{4,3},{5,6},{6,5},{7,8},{8,7},{9,10},{10,9},{11,... | collective-permute-start | bytes 147464 | tf_op jit(solution)/shard_map/ppermute | solution.py:465

commit v6 on v5

--- a/solution.py
+++ b/solution.py
@@ -23,8 +23,8 @@
     return lax.axis_index("group"), tile, core, y
 
 
-def call(kernel, out_shape, in_specs, scratch=(), name=None, aliases=None):
-    outs = jax.tree.map(lambda _: VMEM, out_shape)
+def call(kernel, out_shape, in_specs, scratch=(), name=None, aliases=None, out_spec=VMEM):
+    outs = jax.tree.map(lambda _: out_spec, out_shape)
     return pl.pallas_call(
         kernel,
         out_shape=out_shape,
@@ -136,17 +136,28 @@
         self.in_y = top | ((self.row == rows - 1) & (self.tile == self.tiles - 1))
         self.in_z = column == depth - 1
 
-    def faces(self, storage, x, before, tx, rr_ref, ss_ref, refs):
-        ty_ref, tz_ref, w_ref, ws_ref = refs
+    def faces(self, storage, x, before, rr_ref, ss_ref, refs, x_wall=None):
+        tx_ref, ty_ref, tz_ref, w_ref, ws_ref = refs
         r = rr_ref[x]
-        ty = jnp.where(self.in_y, 0.0, 2.0 / (r + pltpu.roll(r, ROWS - 1, 0)))
-        tz = jnp.where(self.in_z, 0.0, 2.0 / (r + pltpu.roll(r, self.depth - 1, 1)))
+        over_x = r + rr_ref[x + 1]
+        over_y = r + pltpu.roll(r, ROWS - 1, 0)
+        over_z = r + pltpu.roll(r, self.depth - 1, 1)
+        over_xy = over_x * over_y
+        share = 2.0 / (over_xy * over_z)
+        rest = share * over_z
+        tx = rest * over_y
+        if x_wall is not None:
+            tx = jnp.where(x_wall, 0.0, tx)
+        ty = jnp.where(self.in_y, 0.0, rest * over_x)
+        tz = jnp.where(self.in_z, 0.0, share * over_xy)
         diagonal = storage + tx + before + ty + pltpu.roll(ty, 1, 0) + tz + pltpu.roll(tz, 1, 1)
         w = RELAX / diagonal
+        tx_ref[x] = tx
         ty_ref[x] = ty
         tz_ref[x] = tz
         w_ref[x] = w
         ws_ref[x] = w * ss_ref[x]
+        return tx
 
 
 def middle_kernel(
@@ -167,17 +178,14 @@
         return carry
 
     lax.fori_loop(0, planes, gather_rows, 0, unroll=16)
-    refs = ty_ref, tz_ref, w_ref, ws_ref
+    refs = tx_ref, ty_ref, tz_ref, w_ref, ws_ref
 
     def faces(x, before):
-        tx = 2.0 / (rr_ref[x] + rr_ref[x + 1])
-        tx_ref[x] = tx
-        walls.faces(storage, x, before, tx, rr_ref, ss_ref, refs)
-        return tx
+        return walls.faces(storage, x, before, rr_ref, ss_ref, refs)
 
     start = 2.0 / (rr_ref[first] + rr_ref[first + 1])
     tx_ref[first] = start
-    lax.fori_loop(first + 1, last, faces, start, unroll=16)
+    lax.fori_loop(first + 1, last, faces, start, unroll=31)
 
     def second(x, carry):
         total, y_flux, link_y, before = carry
@@ -230,18 +238,12 @@
             ss_ref[x, 0:rows] = jnp.where(there, own_source, 0.0)
             ss_ref[x, rows:ROWS] = jnp.where(there, side_source, 0.0)
 
-    refs = ty_ref, tz_ref, w_ref, ws_ref
+    refs = tx_ref, ty_ref, tz_ref, w_ref, ws_ref
     for begin, end in ((1, first), (last, wide - 2)):
         before = tx_ref[last - 1] if begin == last else 2.0 / (rr_ref[0] + rr_ref[1])
         for x in range(begin, end + 1):
-            tx = 2.0 / (rr_ref[x] + rr_ref[x + 1])
-            if x == first - 1:
-                tx = jnp.where(group == 0, 0.0, tx)
-            if x == last:
-                tx = jnp.where(group == walls.groups - 1, 0.0, tx)
-            tx_ref[x] = tx
-            walls.faces(storage, x, before, tx, rr_ref, ss_ref, refs)
-            before = tx
+            wall = {first - 1: group == 0, last: group == walls.groups - 1}.get(x)
+            before = walls.faces(storage, x, before, rr_ref, ss_ref, refs, wall)
 
     total = part_ref[0:rows]
     y_flux = part_ref[rows : rows + ROWS]
@@ -365,10 +367,10 @@
 
 
 def last_kernel(
-    store_brick, levels,
+    store_brick, levels, chunks,
     sums_ref, v_ref, tx_ref, ty_ref, tz_ref, w_ref, ws_ref,
     out_ref,
-    lines_ref, h_ref, g_ref,
+    lines_ref, g_ref, done_ref, sems,
 ):
     group, tile, core, _ = position()
     planes, rows, depth = out_ref.shape
@@ -393,25 +395,25 @@
         return jnp.where(row < rows, own, jnp.where(row < rows + HALO, up, down))
 
     shifts = [shift_of(offset) for offset in (-1, 0, 1)]
-    for x in (2, 3):
-        h_ref[x] = v_ref[x] + shifts[0]
-        h_ref[HALO + planes + x - 2] = v_ref[HALO + planes + x - 2] + shifts[2]
-    middle = shifts[1]
-
-    def lift(x, carry):
-        h_ref[x] = v_ref[x] + middle
-        return carry
-
-    lax.fori_loop(HALO, HALO + planes, lift, 0, unroll=4)
-
-    def third(x, before):
-        v, ahead = relax(
-            h_ref[x], h_ref[x + 1], before, tx_ref[x], ty_ref[x], tz_ref[x], w_ref[x], ws_ref[x], depth
-        )
+    first, end = HALO, HALO + planes
+
+    def third(x, h, h_next, before):
+        v, ahead = relax(h, h_next, before, tx_ref[x], ty_ref[x], tz_ref[x], w_ref[x], ws_ref[x], depth)
         g_ref[x] = v
         return ahead
 
-    lax.fori_loop(HALO - 1, HALO + planes + 1, third, tx_ref[HALO - 2] * h_ref[HALO - 2], unroll=16)
+    def third_inside(x, carry):
+        h, before = carry
+        h_next = v_ref[x + 1] + shifts[1]
+        return h_next, third(x, h, h_next, before)
+
+    h = v_ref[first - 1] + shifts[0]
+    h_next = v_ref[first] + shifts[1]
+    before = third(first - 1, h, h_next, tx_ref[first - 2] * (v_ref[first - 2] + shifts[0]))
+    h, before = lax.fori_loop(first, end - 1, third_inside, (h_next, before), unroll=31)
+    h_next = v_ref[end] + shifts[2]
+    before = third(end - 1, h, h_next, before)
+    third(end, h_next, v_ref[end + 1] + shifts[2], before)
 
     def fourth(x, before):
         h = g_ref[x]
@@ -423,11 +425,20 @@
         flow = before + tx * g_ref[x + 1, 0:rows]
         flow = flow + (ty * pltpu.roll(h, ROWS - 1, 0) + pltpu.roll(ty * h, 1, 0))[0:rows]
         flow = flow + tz * pltpu.roll(h_own, depth - 1, 1) + pltpu.roll(tz * h_own, 1, 1)
-        out_ref[x - HALO] = (1.0 - RELAX) * h_own + ws_ref[x, 0:rows] + w_ref[x, 0:rows] * flow
+        done_ref[x - HALO] = (1.0 - RELAX) * h_own + ws_ref[x, 0:rows] + w_ref[x, 0:rows] * flow
         return ahead
 
-    first = tx_ref[HALO - 1, 0:rows] * g_ref[HALO - 1, 0:rows]
-    lax.fori_loop(HALO, HALO + planes, fourth, first, unroll=16)
+    before = tx_ref[first - 1, 0:rows] * g_ref[first - 1, 0:rows]
+    step = planes // chunks
+    copies = []
+    for chunk in range(chunks):
+        begin = first + chunk * step
+        before = lax.fori_loop(begin, begin + step, fourth, before, unroll=16)
+        part = pl.ds(chunk * step, step)
+        copies.append(pltpu.make_async_copy(done_ref.at[part], out_ref.at[part], sems.at[chunk]))
+        copies[-1].start()
+    for copy in copies:
+        copy.wait()
 
 
 def spread(block, axes):
@@ -464,7 +475,6 @@
     corner = call(corners_kernel, f32(6, rows, depth), [VMEM] * 2, name="corners")(begin, end)
     corner = lax.ppermute(corner, TILE_AXES, pairs)
     wide = f32(planes + 2 * HALO, ROWS, depth)
-    scratch = [pltpu.VMEM(wide.shape, jnp.float32)]
     part, *fields = call(
         functools.partial(middle_kernel, storage),
         (f32(2 * rows + ROWS, depth),) + (wide,) * 8,
@@ -483,12 +493,19 @@
     sums = call(merge_kernel, f32(z_size * cores, 1, 128), [VMEM], name="merge")(sums)
     sums = spread(sums, ("z", "core"))
     length = z_size * y_size
+    chunks = 4
     return call(
-        functools.partial(last_kernel, storage * planes * rows * depth, tiles.bit_length() - 1),
+        functools.partial(last_kernel, storage * planes * rows * depth, tiles.bit_length() - 1, chunks),
         brick,
         [VMEM] * 7,
-        [pltpu.VMEM((2, length + 16, 128), jnp.float32)] + scratch * 2,
+        [
+            pltpu.VMEM((2, length + 16, 128), jnp.float32),
+            pltpu.VMEM(wide.shape, jnp.float32),
+            pltpu.VMEM(brick.shape, jnp.float32),
+            pltpu.SemaphoreType.DMA((chunks,)),
+        ],
         name="last",
+        out_spec=HBM,
     )(sums, *fields)
 
 

time: 78.6 us -> 77.5 us (0.986)
  Pallas kernels: 10.5 us -> 9.44 us
where the time goes in v6:
time: 77.5 us; the launch traced here: 77.2 us
  blocking collectives  38.1 us (49%)
  starting transfers between devices  28 us (36%)
  Pallas kernels  9.44 us (12%)
  waiting for transfers between devices  1.47 us (2%)
    all_to_all x2, blocking collectives, spread(): return lax.all_to_all(block, axes, 0, 0)  38.1 us
    ppermute x1, starting transfers between devices, on_device(): near = lax.ppermute(near, 'core', [(0, 1), (1, 0)])  16.1 us
    ppermute x1, starting transfers between devices, on_device(): corner = lax.ppermute(corner, TILE_AXES, pairs)  4.78 us
    ppermute x1, starting transfers between devices, on_device(): end = lax.ppermute(end, 'group', [(i, i + 1) for i in range(groups - 1)])  3.99 us
    pallas_call x1, Pallas kernels, on_device(): call(functools.partial(last_kernel, storage * planes * rows * depth, tile...  3.75 us
    pallas_call x1, Pallas kernels, on_device(): call(functools.partial(middle_kernel, storage), (f32(2 * rows + ROWS, dep...  3.67 us
    ppermute x1, starting transfers between devices, on_device(): far = lax.ppermute(far, TILE_AXES, pairs)  1.92 us
  transfers between devices with their start and end apart: 5, of which 2 were waited for; matrix products, arithmetic and copies ran while one was open for 0% of the time, Pallas kernels for 5%

profile of v6, /device:TPU:1, one launch (start us, length us, event | category | flops | bytes accessed | tf_op | source)
XLA Modules:
  0.0 77.2 jit_solution(3882178767716847231)
XLA Ops:
  0.0 1.5 %rows.1 = (f32[64,8,256]{2,1,0:T(8,128)S(1)}, f32[64,8,256]{2,1,0:T(8,128)S(1)}, f32[64,8,256]{2,1,0:T(8,128)S(1)}, f32[64,8,256]{2,1,0:T(8,128)S(1)}) custom-call(f32[8]{0:T(128)} %table_hbm.1, s32[64,8,256]{2,1,0:T(8,128)} %facies_hbm.1, f32[64,8,256]{2,1,0:T(8,128)} %source_hbm.1), custom_call_target="tpu_custom_call" | custom-call | tf_op jit(solution)/shard_map/rows/pallas_call | solution.py:456
  1.5 16.1 %collective-permute-start = (f32[64,8,256]{2,1,0:T(8,128)S(1)}, f32[64,8,256]{2,1,0:T(8,128)S(1)}, u32[]{:S(2)}, u32[]{:S(2)}) collective-permute-start(f32[64,8,256]{2,1,0:T(8,128)S(1)} %get-tuple-element.29), channel_id=1, source_target_pairs={{0,1},{1,0},{2,3},{3,2},{4,5},{5,4},{6,7},{7,6},{8,9},{9,8},{10,11... | collective-permute-start | bytes 1572872 | tf_op jit(solution)/shard_map/ppermute | solution.py:470
  17.6 1.9 %collective-permute-start.4 = (f32[64,8,256]{2,1,0:T(8,128)S(1)}, f32[64,8,256]{2,1,0:T(8,128)S(1)}, u32[]{:S(2)}, u32[]{:S(2)}) collective-permute-start(f32[64,8,256]{2,1,0:T(8,128)S(1)} %get-tuple-element.32), channel_id=1, source_target_pairs={{1,2},{2,1},{3,4},{4,3},{5,6},{6,5},{7,8},{8,7},{9,10},{10,9},{11,... | collective-permute-start | bytes 1572872 | tf_op jit(solution)/shard_map/ppermute | solution.py:469
  19.5 0.0 collective-permute-done.near_ref
  19.5 1.3 %collective-permute-start.1 = (f32[10,8,256]{2,1,0:T(8,128)S(1)}, f32[10,8,256]{2,1,0:T(8,128)S(1)}, u32[]{:S(2)}, u32[]{:S(2)}) collective-permute-start(f32[10,8,256]{2,1,0:T(8,128)S(1)} %get-tuple-element.30), channel_id=1, source_target_pairs={{256,0},{512,256},{768,512},{257,1},{513,257},{769,513},{258,2},{5... | collective-permute-start | bytes 245768 | tf_op jit(solution)/shard_map/ppermute | solution.py:474
  20.8 4.0 %collective-permute-start.2 = (f32[10,8,256]{2,1,0:T(8,128)S(1)}, f32[10,8,256]{2,1,0:T(8,128)S(1)}, u32[]{:S(2)}, u32[]{:S(2)}) collective-permute-start(f32[10,8,256]{2,1,0:T(8,128)S(1)} %get-tuple-element.31), channel_id=1, source_target_pairs={{0,256},{256,512},{512,768},{1,257},{257,513},{513,769},{2,258},{2... | collective-permute-start | bytes 245768 | tf_op jit(solution)/shard_map/ppermute | solution.py:473
  24.8 0.7 collective-permute-done.1.begin_ref
  25.6 0.7 collective-permute-done.2.end_ref
  26.3 4.8 %collective-permute-start.3 = (f32[6,8,256]{2,1,0:T(8,128)S(1)}, f32[6,8,256]{2,1,0:T(8,128)S(1)}, u32[]{:S(2)}, u32[]{:S(2)}) collective-permute-start(f32[6,8,256]{2,1,0:T(8,128)S(1)} %corners.1), channel_id=1, source_target_pairs={{1,2},{2,1},{3,4},{4,3},{5,6},{6,5},{7,8},{8,7},{9,10},{10,9},{11,... | collective-permute-start | bytes 147464 | tf_op jit(solution)/shard_map/ppermute | solution.py:476
  31.1 0.0 collective-permute-done.4.far_ref
  31.1 3.7 %middle.1 = (f32[32,256]{1,0:T(8,128)S(1)}, f32[72,16,256]{2,1,0:T(8,128)S(1)}, f32[72,16,256]{2,1,0:T(8,128)S(1)}, f32[72,16,256]{2,1,0:T(8,128)S(1)}, f32[72,1...) custom-call(f32[64,8,256]{2,1,0:T(8,128)S(1)} %get-tuple-element.27., ...), custom_call_target="tpu_custom_call" | custom-call | tf_op jit(solution)/shard_map/middle/pallas_call | solution.py:478
  34.8 0.0 collective-permute-done.3.corner_ref
  34.8 0.5 edges.1
  35.3 12.3 %all_to_all.10.part_ref = f32[32,1,128]{2,1,0:T(1,128)S(1)} all-to-all(f32[32,1,128]{2,1,0:T(1,128)S(1)} %get-tuple-element.42), channel_id=1, replica_groups=mesh['group'=4,'z'=16,'y'=8,'core'=2] {'group','y'}, dimensions={0} | all-to-all | bytes 32768 | tf_op jit(solution)/shard_map/all_to_all | solution.py:445
  47.6 25.9 %all_to_all.11.sums_ref = f32[32,1,128]{2,1,0:T(1,128)S(1)} all-to-all(f32[32,1,128]{2,1,0:T(1,128)S(1)} %merge.1), channel_id=1, replica_groups=mesh['group'=4,'z'=16,'y'=8,'core'=2] {'z','core'}, dimensions={0} | all-to-all | bytes 32768 | tf_op jit(solution)/shard_map/all_to_all | solution.py:445
  73.4 3.8 %last.1 = f32[64,8,256]{2,1,0:T(8,128)} custom-call(f32[32,1,128]{2,1,0:T(1,128)S(1)} %all_to_all.11.sums_ref, f32[72,16,256]{2,1,0:T(8,128)S(1)} %get-tuple-element.43.v_ref, f32[72,16,256]{2,1,0:T(8,128)S(1)} %get-tuple-element.44.tx_ref, f32[72,16,256]{2,1,0:T(8,128)S(1)} %get-tuple-element.45.ty_ref, f32[72,16,256]{2,1,0:T(8,128)S(1)} %get-tuple-element.46.tz_ref, ...), custom_call_target="tpu_custom_call" | custom-call | tf_op jit(solution)/shard_map/last/pallas_call | solution.py:497
  (3 shorter events, 0.1 us)
Async XLA Ops:
  1.5 18.0 %collective-permute-start = (f32[64,8,256]{2,1,0:T(8,128)S(1)}, f32[64,8,256]{2,1,0:T(8,128)S(1)}, u32[]{:S(2)}, u32[]{:S(2)}) collective-permute-start(f32[64,8,256]{2,1,0:T(8,128)S(1)} %get-tuple-element.29), channel_id=1, source_target_pairs={{0,1},{1,0},{2,3},{3,2},{4,5},{5,4},{6,7},{7,6},{8,9},{9,8},{10,11... | collective-permute-start | bytes 1572872 | tf_op jit(solution)/shard_map/ppermute | solution.py:470
  17.6 13.5 %collective-permute-start.4 = (f32[64,8,256]{2,1,0:T(8,128)S(1)}, f32[64,8,256]{2,1,0:T(8,128)S(1)}, u32[]{:S(2)}, u32[]{:S(2)}) collective-permute-start(f32[64,8,256]{2,1,0:T(8,128)S(1)} %get-tuple-element.32), channel_id=1, source_target_pairs={{1,2},{2,1},{3,4},{4,3},{5,6},{6,5},{7,8},{8,7},{9,10},{10,9},{11,... | collective-permute-start | bytes 1572872 | tf_op jit(solution)/shard_map/ppermute | solution.py:469
  19.5 6.0 %collective-permute-start.1 = (f32[10,8,256]{2,1,0:T(8,128)S(1)}, f32[10,8,256]{2,1,0:T(8,128)S(1)}, u32[]{:S(2)}, u32[]{:S(2)}) collective-permute-start(f32[10,8,256]{2,1,0:T(8,128)S(1)} %get-tuple-element.30), channel_id=1, source_target_pairs={{256,0},{512,256},{768,512},{257,1},{513,257},{769,513},{258,2},{5... | collective-permute-start | bytes 245768 | tf_op jit(solution)/shard_map/ppermute | solution.py:474
  20.8 5.5 %collective-permute-start.2 = (f32[10,8,256]{2,1,0:T(8,128)S(1)}, f32[10,8,256]{2,1,0:T(8,128)S(1)}, u32[]{:S(2)}, u32[]{:S(2)}) collective-permute-start(f32[10,8,256]{2,1,0:T(8,128)S(1)} %get-tuple-element.31), channel_id=1, source_target_pairs={{0,256},{256,512},{512,768},{1,257},{257,513},{513,769},{2,258},{2... | collective-permute-start | bytes 245768 | tf_op jit(solution)/shard_map/ppermute | solution.py:473
  26.3 8.5 %collective-permute-start.3 = (f32[6,8,256]{2,1,0:T(8,128)S(1)}, f32[6,8,256]{2,1,0:T(8,128)S(1)}, u32[]{:S(2)}, u32[]{:S(2)}) collective-permute-start(f32[6,8,256]{2,1,0:T(8,128)S(1)} %corners.1), channel_id=1, source_target_pairs={{1,2},{2,1},{3,4},{4,3},{5,6},{6,5},{7,8},{8,7},{9,10},{10,9},{11,... | collective-permute-start | bytes 147464 | tf_op jit(solution)/shard_map/ppermute | solution.py:476

commit v7 on v6

--- a/solution.py
+++ b/solution.py
@@ -92,6 +92,8 @@
             return carry
 
         lax.fori_loop(chunk * step, (chunk + 1) * step, body, 0, unroll=8)
+    for x in range(planes, far_ref.shape[0]):
+        far_ref[x] = jnp.zeros((rows, depth), jnp.float32)
 
 
 def halo_rows(near, far, core, tile, tiles):
@@ -106,22 +108,24 @@
     return jnp.where(absent, 1.0, r), jnp.where(absent, 0.0, source)
 
 
-def planes_kernel(r_ref, source_ref, near_ref, begin_ref, end_ref):
+def planes_kernel(r_ref, source_ref, begin_ref, end_ref):
     planes = r_ref.shape[0]
     for d in range(HALO):
         for out, x in ((begin_ref, d), (end_ref, planes - 1 - d)):
             out[d] = r_ref[x]
             if d < HALO - 1:
-                out[4 + d] = near_ref[x]
-                out[7 + d] = source_ref[x]
-
-
-def corners_kernel(begin_ref, end_ref, out_ref):
+                out[4 + d] = source_ref[x]
+
+
+def corners_kernel(begin_ref, end_ref, near_in, near_ref, corner_ref):
     first = position()[2] == 0
+    count = HALO - 1
+    own = near_ref.shape[0] - 2 * count
     for side, recv in enumerate((begin_ref, end_ref)):
-        for d in range(HALO - 1):
-            begin, end = row_tiles(recv[d], recv[7 + d])
-            out_ref[3 * side + d] = jnp.where(first, begin, end)
+        for d in range(count):
+            begin, end = row_tiles(recv[d], recv[4 + d])
+            near_ref[own + count * side + d] = jnp.where(first, end, begin)
+            corner_ref[count * side + d] = jnp.where(first, begin, end)
 
 
 class Walls:
@@ -212,7 +216,7 @@
 
 def edges_kernel(
     storage,
-    begin_ref, end_ref, corner_ref,
+    begin_ref, end_ref, near_ref, corner_ref,
     part_ref, v_in, tx_in, ty_in, tz_in, w_in, ws_in, rr_in, ss_in,
     sums_ref, v_ref, tx_ref, ty_ref, tz_ref, w_ref, ws_ref, rr_ref, ss_ref,
 ):
@@ -230,9 +234,10 @@
         ):
             side_r, side_source, own_source = ones, zeros, zeros
             if d < HALO - 1:
-                far = corner_ref[3 * side + d]
-                side_r, side_source = halo_rows(recv[4 + d], far, walls.core, walls.tile, walls.tiles)
-                own_source = recv[7 + d]
+                at = (HALO - 1) * side + d
+                near, far = near_ref[planes + at], corner_ref[at]
+                side_r, side_source = halo_rows(near, far, walls.core, walls.tile, walls.tiles)
+                own_source = recv[4 + d]
             rr_ref[x, 0:rows] = jnp.where(there, recv[d], 1.0)
             rr_ref[x, rows:ROWS] = jnp.where(there, side_r, 1.0)
             ss_ref[x, 0:rows] = jnp.where(there, own_source, 0.0)
@@ -455,7 +460,7 @@
     chunks = 4
     r, source, near, far = call(
         functools.partial(rows_kernel, chunks),
-        (brick,) * 4,
+        (brick, brick, f32(planes + 2 * (HALO - 1), rows, depth), f32(planes + 4 * HALO, rows, depth)),
         [HBM] * 3,
         [
             pltpu.SMEM(perm_table.shape, jnp.float32),
@@ -467,12 +472,18 @@
     )(*(pltpu.with_memory_space_constraint(a, pltpu.HBM) for a in (perm_table, facies, source)))
     pairs = [p for i in range(1, tiles - 1, 2) for p in ((i, i + 1), (i + 1, i))]
     far = lax.ppermute(far, TILE_AXES, pairs)
-    near = lax.ppermute(near, "core", [(0, 1), (1, 0)])
-    slab = f32(10, rows, depth)
-    begin, end = call(planes_kernel, (slab, slab), [VMEM] * 3, name="planes")(r, source, near)
+    slab = f32(7, rows, depth)
+    begin, end = call(planes_kernel, (slab, slab), [VMEM] * 2, name="planes")(r, source)
     end = lax.ppermute(end, "group", [(i, i + 1) for i in range(groups - 1)])
     begin = lax.ppermute(begin, "group", [(i + 1, i) for i in range(groups - 1)])
-    corner = call(corners_kernel, f32(6, rows, depth), [VMEM] * 2, name="corners")(begin, end)
+    near, corner = call(
+        corners_kernel,
+        (f32(*near.shape), f32(2 * (HALO - 1), rows, depth)),
+        [VMEM] * 3,
+        name="corners",
+        aliases={2: 0},
+    )(begin, end, near)
+    near = lax.ppermute(near, "core", [(0, 1), (1, 0)])
     corner = lax.ppermute(corner, TILE_AXES, pairs)
     wide = f32(planes + 2 * HALO, ROWS, depth)
     part, *fields = call(
@@ -484,10 +495,10 @@
     sums, *fields = call(
         functools.partial(edges_kernel, storage),
         (f32(groups * y_size, 1, 128),) + (wide,) * 8,
-        [VMEM] * 12,
+        [VMEM] * 13,
         name="edges",
-        aliases={4 + i: 1 + i for i in range(8)},
-    )(begin, end, corner, part, *fields)
+        aliases={5 + i: 1 + i for i in range(8)},
+    )(begin, end, near, corner, part, *fields)
     fields = fields[:6]
     sums = spread(sums, ("group", "y"))
     sums = call(merge_kernel, f32(z_size * cores, 1, 128), [VMEM], name="merge")(sums)

time: 77.5 us -> 77.3 us (level)
  blocking collectives: 38.1 us -> 41.1 us
  starting transfers between devices: 28 us -> 25.1 us
    all_to_all x2, blocking collectives: 38.1 us -> 41.1 us  [spread(): return lax.all_to_all(block, axes, 0, 0)]
    ppermute x1, starting transfers between devices: 4.78 us -> 1.92 us  [on_device(): corner = lax.ppermute(corner, TILE_AXES, pairs)]
    ppermute x1, starting transfers between devices: 16.1 us -> 13.3 us  [on_device(): near = lax.ppermute(near, 'core', [(0, 1), (1, 0)])]
    ppermute x1, starting transfers between devices: 1.92 us -> 4.59 us  [on_device(): far = lax.ppermute(far, TILE_AXES, pairs)]
  transfers between devices with their start and end apart: 5 -> 5, of which waited for: 2 -> 1; matrix products, arithmetic and copies ran while one was open for 0% -> 0% of each run, Pallas kernels for 5% -> 5%
where the time goes in v7:
time: 77.3 us; the launch traced here: 77 us
  blocking collectives  41.1 us (53%)
  starting transfers between devices  25.1 us (32%)
  Pallas kernels  9.46 us (12%)
  waiting for transfers between devices  1.23 us (2%)
    all_to_all x2, blocking collectives, spread(): return lax.all_to_all(block, axes, 0, 0)  41.1 us
    ppermute x1, starting transfers between devices, on_device(): near = lax.ppermute(near, 'core', [(0, 1), (1, 0)])  13.3 us
    ppermute x1, starting transfers between devices, on_device(): far = lax.ppermute(far, TILE_AXES, pairs)  4.59 us
    ppermute x1, starting transfers between devices, on_device(): end = lax.ppermute(end, 'group', [(i, i + 1) for i in range(groups - 1)])  3.99 us
    pallas_call x1, Pallas kernels, on_device(): call(functools.partial(last_kernel, storage * planes * rows * depth, tile...  3.75 us
    pallas_call x1, Pallas kernels, on_device(): call(functools.partial(middle_kernel, storage), (f32(2 * rows + ROWS, dep...  3.67 us
    ppermute x1, starting transfers between devices, on_device(): corner = lax.ppermute(corner, TILE_AXES, pairs)  1.92 us
  transfers between devices with their start and end apart: 5, of which 1 were waited for; matrix products, arithmetic and copies ran while one was open for 0% of the time, Pallas kernels for 5%

profile of v7, /device:TPU:1, one launch (start us, length us, event | category | flops | bytes accessed | tf_op | source)
XLA Modules:
  0.0 77.0 jit_solution(17134964566485094090)
XLA Ops:
  0.0 1.5 %rows.1 = (f32[64,8,256]{2,1,0:T(8,128)S(1)}, f32[64,8,256]{2,1,0:T(8,128)S(1)}, f32[70,8,256]{2,1,0:T(8,128)S(1)}, f32[80,8,256]{2,1,0:T(8,128)S(1)}) custom-call(f32[8]{0:T(128)} %table_hbm.1, s32[64,8,256]{2,1,0:T(8,128)} %facies_hbm.1, f32[64,8,256]{2,1,0:T(8,128)} %source_hbm.1), custom_call_target="tpu_custom_call" | custom-call | tf_op jit(solution)/shard_map/rows/pallas_call | solution.py:461
  1.5 4.6 %collective-permute-start.4 = (f32[80,8,256]{2,1,0:T(8,128)S(1)}, f32[80,8,256]{2,1,0:T(8,128)S(1)}, u32[]{:S(2)}, u32[]{:S(2)}) collective-permute-start(f32[80,8,256]{2,1,0:T(8,128)S(1)} %get-tuple-element.36), channel_id=1, source_target_pairs={{1,2},{2,1},{3,4},{4,3},{5,6},{6,5},{7,8},{8,7},{9,10},{10,9},{11,... | collective-permute-start | bytes 1966088 | tf_op jit(solution)/shard_map/ppermute | solution.py:474
  6.1 1.3 %collective-permute-start = (f32[7,8,256]{2,1,0:T(8,128)S(1)}, f32[7,8,256]{2,1,0:T(8,128)S(1)}, u32[]{:S(2)}, u32[]{:S(2)}) collective-permute-start(f32[7,8,256]{2,1,0:T(8,128)S(1)} %get-tuple-element.31), channel_id=1, source_target_pairs={{256,0},{512,256},{768,512},{257,1},{513,257},{769,513},{258,2},{5... | collective-permute-start | bytes 172040 | tf_op jit(solution)/shard_map/ppermute | solution.py:478
  7.4 4.0 %collective-permute-start.1 = (f32[7,8,256]{2,1,0:T(8,128)S(1)}, f32[7,8,256]{2,1,0:T(8,128)S(1)}, u32[]{:S(2)}, u32[]{:S(2)}) collective-permute-start(f32[7,8,256]{2,1,0:T(8,128)S(1)} %get-tuple-element.32), channel_id=1, source_target_pairs={{0,256},{256,512},{512,768},{1,257},{257,513},{513,769},{2,258},{2... | collective-permute-start | bytes 172040 | tf_op jit(solution)/shard_map/ppermute | solution.py:477
  11.4 0.0 collective-permute-done.begin_ref
  11.4 1.2 %collective-permute-done.1.end_ref = f32[7,8,256]{2,1,0:T(8,128)S(1)} collective-permute-done((f32[7,8,256]{2,1,0:T(8,128)S(1)}, f32[7,8,256]{2,1,0:T(8,128)S(1)}, u32[]{:S(2)}, u32[]{:S(2)}) %collective-permute-start.1) | collective-permute-done | bytes 57376 | tf_op jit(solution)/shard_map/ppermute | solution.py:477
  12.7 13.3 %collective-permute-start.2 = (f32[70,8,256]{2,1,0:T(8,128)S(1)}, f32[70,8,256]{2,1,0:T(8,128)S(1)}, u32[]{:S(2)}, u32[]{:S(2)}) collective-permute-start(f32[70,8,256]{2,1,0:T(8,128)S(1)} %get-tuple-element.34), channel_id=1, source_target_pairs={{0,1},{1,0},{2,3},{3,2},{4,5},{5,4},{6,7},{7,6},{8,9},{9,8},{10,11... | collective-permute-start | bytes 1720328 | tf_op jit(solution)/shard_map/ppermute | solution.py:486
  26.0 1.9 %collective-permute-start.3 = (f32[6,8,256]{2,1,0:T(8,128)S(1)}, f32[6,8,256]{2,1,0:T(8,128)S(1)}, u32[]{:S(2)}, u32[]{:S(2)}) collective-permute-start(f32[6,8,256]{2,1,0:T(8,128)S(1)} %get-tuple-element.35), channel_id=1, source_target_pairs={{1,2},{2,1},{3,4},{4,3},{5,6},{6,5},{7,8},{8,7},{9,10},{10,9},{11,... | collective-permute-start | bytes 147464 | tf_op jit(solution)/shard_map/ppermute | solution.py:487
  27.9 0.0 collective-permute-done.2.near_ref
  27.9 0.0 collective-permute-done.4.far_ref
  27.9 3.7 %middle.1 = (f32[32,256]{1,0:T(8,128)S(1)}, f32[72,16,256]{2,1,0:T(8,128)S(1)}, f32[72,16,256]{2,1,0:T(8,128)S(1)}, f32[72,16,256]{2,1,0:T(8,128)S(1)}, f32[72,1...) custom-call(f32[64,8,256]{2,1,0:T(8,128)S(1)} %get-tuple-element.29., ...), custom_call_target="tpu_custom_call" | custom-call | tf_op jit(solution)/shard_map/middle/pallas_call | solution.py:489
  31.6 0.0 collective-permute-done.3.corner_ref
  31.6 0.5 edges.1
  32.1 12.2 %all_to_all.10.part_ref = f32[32,1,128]{2,1,0:T(1,128)S(1)} all-to-all(f32[32,1,128]{2,1,0:T(1,128)S(1)} %get-tuple-element.46), channel_id=1, replica_groups=mesh['group'=4,'z'=16,'y'=8,'core'=2] {'group','y'}, dimensions={0} | all-to-all | bytes 32768 | tf_op jit(solution)/shard_map/all_to_all | solution.py:450
  44.4 28.8 %all_to_all.11.sums_ref = f32[32,1,128]{2,1,0:T(1,128)S(1)} all-to-all(f32[32,1,128]{2,1,0:T(1,128)S(1)} %merge.1), channel_id=1, replica_groups=mesh['group'=4,'z'=16,'y'=8,'core'=2] {'z','core'}, dimensions={0} | all-to-all | bytes 32768 | tf_op jit(solution)/shard_map/all_to_all | solution.py:450
  73.2 3.8 %last.1 = f32[64,8,256]{2,1,0:T(8,128)} custom-call(f32[32,1,128]{2,1,0:T(1,128)S(1)} %all_to_all.11.sums_ref, f32[72,16,256]{2,1,0:T(8,128)S(1)} %get-tuple-element.47.v_ref, f32[72,16,256]{2,1,0:T(8,128)S(1)} %get-tuple-element.48.tx_ref, f32[72,16,256]{2,1,0:T(8,128)S(1)} %get-tuple-element.49.ty_ref, f32[72,16,256]{2,1,0:T(8,128)S(1)} %get-tuple-element.50.tz_ref, ...), custom_call_target="tpu_custom_call" | custom-call | tf_op jit(solution)/shard_map/last/pallas_call | solution.py:508
  (3 shorter events, 0.1 us)
Async XLA Ops:
  1.5 26.4 %collective-permute-start.4 = (f32[80,8,256]{2,1,0:T(8,128)S(1)}, f32[80,8,256]{2,1,0:T(8,128)S(1)}, u32[]{:S(2)}, u32[]{:S(2)}) collective-permute-start(f32[80,8,256]{2,1,0:T(8,128)S(1)} %get-tuple-element.36), channel_id=1, source_target_pairs={{1,2},{2,1},{3,4},{4,3},{5,6},{6,5},{7,8},{8,7},{9,10},{10,9},{11,... | collective-permute-start | bytes 1966088 | tf_op jit(solution)/shard_map/ppermute | solution.py:474
  6.1 5.3 %collective-permute-start = (f32[7,8,256]{2,1,0:T(8,128)S(1)}, f32[7,8,256]{2,1,0:T(8,128)S(1)}, u32[]{:S(2)}, u32[]{:S(2)}) collective-permute-start(f32[7,8,256]{2,1,0:T(8,128)S(1)} %get-tuple-element.31), channel_id=1, source_target_pairs={{256,0},{512,256},{768,512},{257,1},{513,257},{769,513},{258,2},{5... | collective-permute-start | bytes 172040 | tf_op jit(solution)/shard_map/ppermute | solution.py:478
  7.4 5.2 %collective-permute-start.1 = (f32[7,8,256]{2,1,0:T(8,128)S(1)}, f32[7,8,256]{2,1,0:T(8,128)S(1)}, u32[]{:S(2)}, u32[]{:S(2)}) collective-permute-start(f32[7,8,256]{2,1,0:T(8,128)S(1)} %get-tuple-element.32), channel_id=1, source_target_pairs={{0,256},{256,512},{512,768},{1,257},{257,513},{513,769},{2,258},{2... | collective-permute-start | bytes 172040 | tf_op jit(solution)/shard_map/ppermute | solution.py:477
  12.7 15.2 %collective-permute-start.2 = (f32[70,8,256]{2,1,0:T(8,128)S(1)}, f32[70,8,256]{2,1,0:T(8,128)S(1)}, u32[]{:S(2)}, u32[]{:S(2)}) collective-permute-start(f32[70,8,256]{2,1,0:T(8,128)S(1)} %get-tuple-element.34), channel_id=1, source_target_pairs={{0,1},{1,0},{2,3},{3,2},{4,5},{5,4},{6,7},{7,6},{8,9},{9,8},{10,11... | collective-permute-start | bytes 1720328 | tf_op jit(solution)/shard_map/ppermute | solution.py:486
  26.0 5.6 %collective-permute-start.3 = (f32[6,8,256]{2,1,0:T(8,128)S(1)}, f32[6,8,256]{2,1,0:T(8,128)S(1)}, u32[]{:S(2)}, u32[]{:S(2)}) collective-permute-start(f32[6,8,256]{2,1,0:T(8,128)S(1)} %get-tuple-element.35), channel_id=1, source_target_pairs={{1,2},{2,1},{3,4},{4,3},{5,6},{6,5},{7,8},{8,7},{9,10},{10,9},{11,... | collective-permute-start | bytes 147464 | tf_op jit(solution)/shard_map/ppermute | solution.py:487

commit v8 on v7

--- a/solution.py
+++ b/solution.py
@@ -108,22 +108,40 @@
     return jnp.where(absent, 1.0, r), jnp.where(absent, 0.0, source)
 
 
-def planes_kernel(r_ref, source_ref, begin_ref, end_ref):
+def even_group():
+    return lax.rem(position()[0], 2) == 0
+
+
+def planes_kernel(r_ref, source_ref, one_ref, two_ref):
     planes = r_ref.shape[0]
+    even = even_group()
+
+    def put(at, field_ref, d):
+        begin, end = field_ref[d], field_ref[planes - 1 - d]
+        one_ref[at] = jnp.where(even, end, begin)
+        two_ref[at] = jnp.where(even, begin, end)
+
     for d in range(HALO):
-        for out, x in ((begin_ref, d), (end_ref, planes - 1 - d)):
-            out[d] = r_ref[x]
-            if d < HALO - 1:
-                out[4 + d] = source_ref[x]
-
-
-def corners_kernel(begin_ref, end_ref, near_in, near_ref, corner_ref):
+        put(d, r_ref, d)
+        if d < HALO - 1:
+            put(4 + d, source_ref, d)
+
+
+def came(one_ref, two_ref):
+    even = even_group()
+    return (
+        lambda at: jnp.where(even, one_ref[at], two_ref[at]),
+        lambda at: jnp.where(even, two_ref[at], one_ref[at]),
+    )
+
+
+def corners_kernel(one_ref, two_ref, near_in, near_ref, corner_ref):
     first = position()[2] == 0
     count = HALO - 1
     own = near_ref.shape[0] - 2 * count
-    for side, recv in enumerate((begin_ref, end_ref)):
+    for side, recv in enumerate(came(one_ref, two_ref)):
         for d in range(count):
-            begin, end = row_tiles(recv[d], recv[4 + d])
+            begin, end = row_tiles(recv(d), recv(4 + d))
             near_ref[own + count * side + d] = jnp.where(first, end, begin)
             corner_ref[count * side + d] = jnp.where(first, begin, end)
 
@@ -216,29 +234,30 @@
 
 def edges_kernel(
     storage,
-    begin_ref, end_ref, near_ref, corner_ref,
+    one_ref, two_ref, near_ref, corner_ref,
     part_ref, v_in, tx_in, ty_in, tz_in, w_in, ws_in, rr_in, ss_in,
     sums_ref, v_ref, tx_ref, ty_ref, tz_ref, w_ref, ws_ref, rr_ref, ss_ref,
 ):
     wide, _, depth = v_ref.shape
-    planes, rows = wide - 2 * HALO, begin_ref.shape[1]
+    planes, rows = wide - 2 * HALO, one_ref.shape[1]
     walls = Walls(planes, rows, depth)
     first, last = HALO, HALO + planes - 1
     group, row = walls.group, walls.row
     ones = jnp.ones((rows, depth), jnp.float32)
     zeros = jnp.zeros((rows, depth), jnp.float32)
+    following, preceding = came(one_ref, two_ref)
     for d in range(HALO):
         for side, recv, x, there in (
-            (1, end_ref, first - 1 - d, group > 0),
-            (0, begin_ref, last + 1 + d, group < walls.groups - 1),
+            (1, preceding, first - 1 - d, group > 0),
+            (0, following, last + 1 + d, group < walls.groups - 1),
         ):
             side_r, side_source, own_source = ones, zeros, zeros
             if d < HALO - 1:
                 at = (HALO - 1) * side + d
                 near, far = near_ref[planes + at], corner_ref[at]
                 side_r, side_source = halo_rows(near, far, walls.core, walls.tile, walls.tiles)
-                own_source = recv[4 + d]
-            rr_ref[x, 0:rows] = jnp.where(there, recv[d], 1.0)
+                own_source = recv(4 + d)
+            rr_ref[x, 0:rows] = jnp.where(there, recv(d), 1.0)
             rr_ref[x, rows:ROWS] = jnp.where(there, side_r, 1.0)
             ss_ref[x, 0:rows] = jnp.where(there, own_source, 0.0)
             ss_ref[x, rows:ROWS] = jnp.where(there, side_source, 0.0)
@@ -473,16 +492,18 @@
     pairs = [p for i in range(1, tiles - 1, 2) for p in ((i, i + 1), (i + 1, i))]
     far = lax.ppermute(far, TILE_AXES, pairs)
     slab = f32(7, rows, depth)
-    begin, end = call(planes_kernel, (slab, slab), [VMEM] * 2, name="planes")(r, source)
-    end = lax.ppermute(end, "group", [(i, i + 1) for i in range(groups - 1)])
-    begin = lax.ppermute(begin, "group", [(i + 1, i) for i in range(groups - 1)])
+    one, two = call(planes_kernel, (slab, slab), [VMEM] * 2, name="planes")(r, source)
+    one, two = (
+        lax.ppermute(a, "group", [p for i in range(b, groups - 1, 2) for p in ((i, i + 1), (i + 1, i))])
+        for a, b in ((one, 0), (two, 1))
+    )
     near, corner = call(
         corners_kernel,
         (f32(*near.shape), f32(2 * (HALO - 1), rows, depth)),
         [VMEM] * 3,
         name="corners",
         aliases={2: 0},
-    )(begin, end, near)
+    )(one, two, near)
     near = lax.ppermute(near, "core", [(0, 1), (1, 0)])
     corner = lax.ppermute(corner, TILE_AXES, pairs)
     wide = f32(planes + 2 * HALO, ROWS, depth)
@@ -498,7 +519,7 @@
         [VMEM] * 13,
         name="edges",
         aliases={5 + i: 1 + i for i in range(8)},
-    )(begin, end, near, corner, part, *fields)
+    )(one, two, near, corner, part, *fields)
     fields = fields[:6]
     sums = spread(sums, ("group", "y"))
     sums = call(merge_kernel, f32(z_size * cores, 1, 128), [VMEM], name="merge")(sums)

time: 77.3 us -> 77.9 us (level)
  blocking collectives: 41.1 us -> 43.2 us
  starting transfers between devices: 25.1 us -> 23.6 us
    all_to_all x2, blocking collectives: 41.1 us -> 43.2 us  [spread(): return lax.all_to_all(block, axes, 0, 0)]
    ppermute x2, starting transfers between devices: 5.28 us -> 3.78 us  [on_device(): lax.ppermute(a, 'group', [p for i in range(b, groups - 1, 2) for p in ((i...]
where the time goes in v8:
time: 77.9 us; the launch traced here: 77.6 us
  blocking collectives  43.2 us (55%)
  starting transfers between devices  23.6 us (30%)
  Pallas kernels  9.48 us (12%)
  waiting for transfers between devices  1.13 us (1%)
    all_to_all x2, blocking collectives, spread(): return lax.all_to_all(block, axes, 0, 0)  43.2 us
    ppermute x1, starting transfers between devices, on_device(): near = lax.ppermute(near, 'core', [(0, 1), (1, 0)])  13.3 us
    ppermute x1, starting transfers between devices, on_device(): far = lax.ppermute(far, TILE_AXES, pairs)  4.59 us
    ppermute x2, starting transfers between devices, on_device(): lax.ppermute(a, 'group', [p for i in range(b, groups - 1, 2) for p in ((i...  3.78 us
    pallas_call x1, Pallas kernels, on_device(): call(functools.partial(last_kernel, storage * planes * rows * depth, tile...  3.75 us
    pallas_call x1, Pallas kernels, on_device(): call(functools.partial(middle_kernel, storage), (f32(2 * rows + ROWS, dep...  3.67 us
    ppermute x1, starting transfers between devices, on_device(): corner = lax.ppermute(corner, TILE_AXES, pairs)  1.92 us
  transfers between devices with their start and end apart: 5, of which 1 were waited for; matrix products, arithmetic and copies ran while one was open for 0% of the time, Pallas kernels for 5%

profile of v8, /device:TPU:1, one launch (start us, length us, event | category | flops | bytes accessed | tf_op | source)
XLA Modules:
  0.0 77.6 jit_solution(13444959602764395749)
XLA Ops:
  0.0 1.5 %rows.1 = (f32[64,8,256]{2,1,0:T(8,128)S(1)}, f32[64,8,256]{2,1,0:T(8,128)S(1)}, f32[70,8,256]{2,1,0:T(8,128)S(1)}, f32[80,8,256]{2,1,0:T(8,128)S(1)}) custom-call(f32[8]{0:T(128)} %table_hbm.1, s32[64,8,256]{2,1,0:T(8,128)} %facies_hbm.1, f32[64,8,256]{2,1,0:T(8,128)} %source_hbm.1), custom_call_target="tpu_custom_call" | custom-call | tf_op jit(solution)/shard_map/rows/pallas_call | solution.py:480
  1.5 4.6 %collective-permute-start.4 = (f32[80,8,256]{2,1,0:T(8,128)S(1)}, f32[80,8,256]{2,1,0:T(8,128)S(1)}, u32[]{:S(2)}, u32[]{:S(2)}) collective-permute-start(f32[80,8,256]{2,1,0:T(8,128)S(1)} %get-tuple-element.36), channel_id=1, source_target_pairs={{1,2},{2,1},{3,4},{4,3},{5,6},{6,5},{7,8},{8,7},{9,10},{10,9},{11,... | collective-permute-start | bytes 1966088 | tf_op jit(solution)/shard_map/ppermute | solution.py:493
  6.1 3.1 %collective-permute-start = (f32[7,8,256]{2,1,0:T(8,128)S(1)}, f32[7,8,256]{2,1,0:T(8,128)S(1)}, u32[]{:S(2)}, u32[]{:S(2)}) collective-permute-start(f32[7,8,256]{2,1,0:T(8,128)S(1)} %get-tuple-element.31), channel_id=1, source_target_pairs={{0,256},{256,0},{512,768},{768,512},{1,257},{257,1},{513,769},{769... | collective-permute-start | bytes 172040 | tf_op jit(solution)/shard_map/ppermute | solution.py:497
  9.3 0.7 collective-permute-start.1
  9.9 1.1 %collective-permute-done.one_ref = f32[7,8,256]{2,1,0:T(8,128)S(1)} collective-permute-done((f32[7,8,256]{2,1,0:T(8,128)S(1)}, f32[7,8,256]{2,1,0:T(8,128)S(1)}, u32[]{:S(2)}, u32[]{:S(2)}) %collective-permute-start) | collective-permute-done | bytes 57376 | tf_op jit(solution)/shard_map/ppermute | solution.py:497
  11.1 0.0 collective-permute-done.1.two_ref
  11.1 13.3 %collective-permute-start.2 = (f32[70,8,256]{2,1,0:T(8,128)S(1)}, f32[70,8,256]{2,1,0:T(8,128)S(1)}, u32[]{:S(2)}, u32[]{:S(2)}) collective-permute-start(f32[70,8,256]{2,1,0:T(8,128)S(1)} %get-tuple-element.34), channel_id=1, source_target_pairs={{0,1},{1,0},{2,3},{3,2},{4,5},{5,4},{6,7},{7,6},{8,9},{9,8},{10,11... | collective-permute-start | bytes 1720328 | tf_op jit(solution)/shard_map/ppermute | solution.py:507
  24.4 1.9 %collective-permute-start.3 = (f32[6,8,256]{2,1,0:T(8,128)S(1)}, f32[6,8,256]{2,1,0:T(8,128)S(1)}, u32[]{:S(2)}, u32[]{:S(2)}) collective-permute-start(f32[6,8,256]{2,1,0:T(8,128)S(1)} %get-tuple-element.35), channel_id=1, source_target_pairs={{1,2},{2,1},{3,4},{4,3},{5,6},{6,5},{7,8},{8,7},{9,10},{10,9},{11,... | collective-permute-start | bytes 147464 | tf_op jit(solution)/shard_map/ppermute | solution.py:508
  26.4 0.0 collective-permute-done.2.near_ref
  26.4 0.0 collective-permute-done.4.far_ref
  26.4 3.7 %middle.1 = (f32[32,256]{1,0:T(8,128)S(1)}, f32[72,16,256]{2,1,0:T(8,128)S(1)}, f32[72,16,256]{2,1,0:T(8,128)S(1)}, f32[72,16,256]{2,1,0:T(8,128)S(1)}, f32[72,1...) custom-call(f32[64,8,256]{2,1,0:T(8,128)S(1)} %get-tuple-element.29., ...), custom_call_target="tpu_custom_call" | custom-call | tf_op jit(solution)/shard_map/middle/pallas_call | solution.py:510
  30.1 0.0 collective-permute-done.3.corner_ref
  30.1 0.5 edges.1
  30.5 13.8 %all_to_all.10.part_ref = f32[32,1,128]{2,1,0:T(1,128)S(1)} all-to-all(f32[32,1,128]{2,1,0:T(1,128)S(1)} %get-tuple-element.46), channel_id=1, replica_groups=mesh['group'=4,'z'=16,'y'=8,'core'=2] {'group','y'}, dimensions={0} | all-to-all | bytes 32768 | tf_op jit(solution)/shard_map/all_to_all | solution.py:469
  44.4 29.4 %all_to_all.11.sums_ref = f32[32,1,128]{2,1,0:T(1,128)S(1)} all-to-all(f32[32,1,128]{2,1,0:T(1,128)S(1)} %merge.1), channel_id=1, replica_groups=mesh['group'=4,'z'=16,'y'=8,'core'=2] {'z','core'}, dimensions={0} | all-to-all | bytes 32768 | tf_op jit(solution)/shard_map/all_to_all | solution.py:469
  73.8 3.8 %last.1 = f32[64,8,256]{2,1,0:T(8,128)} custom-call(f32[32,1,128]{2,1,0:T(1,128)S(1)} %all_to_all.11.sums_ref, f32[72,16,256]{2,1,0:T(8,128)S(1)} %get-tuple-element.47.v_ref, f32[72,16,256]{2,1,0:T(8,128)S(1)} %get-tuple-element.48.tx_ref, f32[72,16,256]{2,1,0:T(8,128)S(1)} %get-tuple-element.49.ty_ref, f32[72,16,256]{2,1,0:T(8,128)S(1)} %get-tuple-element.50.tz_ref, ...), custom_call_target="tpu_custom_call" | custom-call | tf_op jit(solution)/shard_map/last/pallas_call | solution.py:529
  (3 shorter events, 0.1 us)
Async XLA Ops:
  1.5 24.9 %collective-permute-start.4 = (f32[80,8,256]{2,1,0:T(8,128)S(1)}, f32[80,8,256]{2,1,0:T(8,128)S(1)}, u32[]{:S(2)}, u32[]{:S(2)}) collective-permute-start(f32[80,8,256]{2,1,0:T(8,128)S(1)} %get-tuple-element.36), channel_id=1, source_target_pairs={{1,2},{2,1},{3,4},{4,3},{5,6},{6,5},{7,8},{8,7},{9,10},{10,9},{11,... | collective-permute-start | bytes 1966088 | tf_op jit(solution)/shard_map/ppermute | solution.py:493
  6.1 4.9 %collective-permute-start = (f32[7,8,256]{2,1,0:T(8,128)S(1)}, f32[7,8,256]{2,1,0:T(8,128)S(1)}, u32[]{:S(2)}, u32[]{:S(2)}) collective-permute-start(f32[7,8,256]{2,1,0:T(8,128)S(1)} %get-tuple-element.31), channel_id=1, source_target_pairs={{0,256},{256,0},{512,768},{768,512},{1,257},{257,1},{513,769},{769... | collective-permute-start | bytes 172040 | tf_op jit(solution)/shard_map/ppermute | solution.py:497
  9.3 1.8 %collective-permute-start.1 = (f32[7,8,256]{2,1,0:T(8,128)S(1)}, f32[7,8,256]{2,1,0:T(8,128)S(1)}, u32[]{:S(2)}, u32[]{:S(2)}) collective-permute-start(f32[7,8,256]{2,1,0:T(8,128)S(1)} %get-tuple-element.32), channel_id=1, source_target_pairs={{256,512},{512,256},{257,513},{513,257},{258,514},{514,258},{259,5... | collective-permute-start | bytes 172040 | tf_op jit(solution)/shard_map/ppermute | solution.py:497
  11.1 15.3 %collective-permute-start.2 = (f32[70,8,256]{2,1,0:T(8,128)S(1)}, f32[70,8,256]{2,1,0:T(8,128)S(1)}, u32[]{:S(2)}, u32[]{:S(2)}) collective-permute-start(f32[70,8,256]{2,1,0:T(8,128)S(1)} %get-tuple-element.34), channel_id=1, source_target_pairs={{0,1},{1,0},{2,3},{3,2},{4,5},{5,4},{6,7},{7,6},{8,9},{9,8},{10,11... | collective-permute-start | bytes 1720328 | tf_op jit(solution)/shard_map/ppermute | solution.py:507
  24.4 5.6 %collective-permute-start.3 = (f32[6,8,256]{2,1,0:T(8,128)S(1)}, f32[6,8,256]{2,1,0:T(8,128)S(1)}, u32[]{:S(2)}, u32[]{:S(2)}) collective-permute-start(f32[6,8,256]{2,1,0:T(8,128)S(1)} %get-tuple-element.35), channel_id=1, source_target_pairs={{1,2},{2,1},{3,4},{4,3},{5,6},{6,5},{7,8},{8,7},{9,10},{10,9},{11,... | collective-permute-start | bytes 147464 | tf_op jit(solution)/shard_map/ppermute | solution.py:508

commit v9 on v7

--- a/solution.py
+++ b/solution.py
@@ -164,9 +164,30 @@
         return tx
 
 
+def own_kernel(storage, r_ref, tx_ref, tz_ref, w_ref):
+    planes, rows, depth = r_ref.shape
+    wall = lax.broadcasted_iota(jnp.int32, (rows, depth), 1) == depth - 1
+
+    def faces(x, before):
+        r = r_ref[x]
+        over_x = r + r_ref[x + 1]
+        over_z = r + pltpu.roll(r, depth - 1, 1)
+        share = 2.0 / (over_x * over_z)
+        tx = share * over_z
+        tz = jnp.where(wall, 0.0, share * over_x)
+        tx_ref[HALO + x, 0:rows] = tx
+        tz_ref[HALO + x, 0:rows] = tz
+        w_ref[HALO + x, 0:rows] = storage + tx + before + tz + pltpu.roll(tz, 1, 1)
+        return tx
+
+    start = 2.0 / (r_ref[0] + r_ref[1])
+    tx_ref[HALO, 0:rows] = start
+    lax.fori_loop(1, planes - 1, faces, start, unroll=31)
+
+
 def middle_kernel(
     storage,
-    r_ref, source_ref, near_ref, far_ref,
+    r_ref, source_ref, near_ref, far_ref, tx_in, tz_in, w_in,
     part_ref, v_ref, tx_ref, ty_ref, tz_ref, w_ref, ws_ref, rr_ref, ss_ref,
 ):
     planes, rows, depth = r_ref.shape
@@ -182,13 +203,33 @@
         return carry
 
     lax.fori_loop(0, planes, gather_rows, 0, unroll=16)
-    refs = tx_ref, ty_ref, tz_ref, w_ref, ws_ref
+    own, beside = pl.ds(0, rows), pl.ds(rows, ROWS - rows)
+    in_z = walls.in_z[rows:ROWS]
 
     def faces(x, before):
-        return walls.faces(storage, x, before, rr_ref, ss_ref, refs)
-
-    start = 2.0 / (rr_ref[first] + rr_ref[first + 1])
-    tx_ref[first] = start
+        r = rr_ref[x]
+        over_y = r + pltpu.roll(r, ROWS - 1, 0)
+        r_side = r[rows:ROWS]
+        over_x = r_side + rr_ref[x + 1, beside]
+        over_z = r_side + pltpu.roll(r_side, depth - 1, 1)
+        over_xz = over_x * over_z
+        share = 2.0 / (over_xz * over_y[rows:ROWS])
+        rest = share * over_y[rows:ROWS]
+        tx = rest * over_z
+        tz = jnp.where(in_z, 0.0, rest * over_x)
+        ty = jnp.concatenate([2.0 / over_y[0:rows], share * over_xz], axis=0)
+        ty = jnp.where(walls.in_y, 0.0, ty)
+        side = storage + tx + before + tz + pltpu.roll(tz, 1, 1)
+        w = RELAX / (jnp.concatenate([w_in[x, own], side], axis=0) + ty + pltpu.roll(ty, 1, 0))
+        tx_ref[x, beside] = tx
+        ty_ref[x] = ty
+        tz_ref[x, beside] = tz
+        w_ref[x] = w
+        ws_ref[x] = w * ss_ref[x]
+        return tx
+
+    start = 2.0 / (rr_ref[first, beside] + rr_ref[first + 1, beside])
+    tx_ref[first, beside] = start
     lax.fori_loop(first + 1, last, faces, start, unroll=31)
 
     def second(x, carry):
@@ -476,6 +517,9 @@
     begin, end = call(planes_kernel, (slab, slab), [VMEM] * 2, name="planes")(r, source)
     end = lax.ppermute(end, "group", [(i, i + 1) for i in range(groups - 1)])
     begin = lax.ppermute(begin, "group", [(i + 1, i) for i in range(groups - 1)])
+    wide = f32(planes + 2 * HALO, ROWS, depth)
+    tx, tz, w = call(functools.partial(own_kernel, storage), (wide,) * 3, [VMEM], name="own")(r)
+    near, tx, tz, w = lax.optimization_barrier((near, tx, tz, w))
     near, corner = call(
         corners_kernel,
         (f32(*near.shape), f32(2 * (HALO - 1), rows, depth)),
@@ -485,13 +529,13 @@
     )(begin, end, near)
     near = lax.ppermute(near, "core", [(0, 1), (1, 0)])
     corner = lax.ppermute(corner, TILE_AXES, pairs)
-    wide = f32(planes + 2 * HALO, ROWS, depth)
     part, *fields = call(
         functools.partial(middle_kernel, storage),
         (f32(2 * rows + ROWS, depth),) + (wide,) * 8,
-        [VMEM] * 4,
+        [VMEM] * 7,
         name="middle",
-    )(r, source, near, far)
+        aliases={4: 2, 5: 4, 6: 5},
+    )(r, source, near, far, tx, tz, w)
     sums, *fields = call(
         functools.partial(edges_kernel, storage),
         (f32(groups * y_size, 1, 128),) + (wide,) * 8,

time: 77.3 us -> 76.8 us (level)
    pallas_call x1, Pallas kernels: 3.67 us -> 2.73 us  [on_device(): call(functools.partial(middle_kernel, storage), (f32(2 * rows + ROWS, dep...]
  transfers between devices with their start and end apart: 5 -> 5, of which waited for: 1 -> 2; matrix products, arithmetic and copies ran while one was open for 0% -> 0% of each run, Pallas kernels for 5% -> 4%
where the time goes in v9:
time: 76.8 us; the launch traced here: 76.5 us
  blocking collectives  40.9 us (53%)
  starting transfers between devices  25.1 us (33%)
  Pallas kernels  9.05 us (12%)
  waiting for transfers between devices  1.41 us (2%)
    all_to_all x2, blocking collectives, spread(): return lax.all_to_all(block, axes, 0, 0)  40.9 us
    ppermute x1, starting transfers between devices, on_device(): near = lax.ppermute(near, 'core', [(0, 1), (1, 0)])  13.3 us
    ppermute x1, starting transfers between devices, on_device(): far = lax.ppermute(far, TILE_AXES, pairs)  4.59 us
    ppermute x1, starting transfers between devices, on_device(): end = lax.ppermute(end, 'group', [(i, i + 1) for i in range(groups - 1)])  3.99 us
    pallas_call x1, Pallas kernels, on_device(): call(functools.partial(last_kernel, storage * planes * rows * depth, tile...  3.75 us
    pallas_call x1, Pallas kernels, on_device(): call(functools.partial(middle_kernel, storage), (f32(2 * rows + ROWS, dep...  2.73 us
    ppermute x1, starting transfers between devices, on_device(): corner = lax.ppermute(corner, TILE_AXES, pairs)  1.92 us
  transfers between devices with their start and end apart: 5, of which 2 were waited for; matrix products, arithmetic and copies ran while one was open for 0% of the time, Pallas kernels for 4%

profile of v9, /device:TPU:1, one launch (start us, length us, event | category | flops | bytes accessed | tf_op | source)
XLA Modules:
  0.0 76.5 jit_solution(17163646043429606352)
XLA Ops:
  0.0 1.5 %rows.1 = (f32[64,8,256]{2,1,0:T(8,128)S(1)}, f32[64,8,256]{2,1,0:T(8,128)S(1)}, f32[70,8,256]{2,1,0:T(8,128)S(1)}, f32[80,8,256]{2,1,0:T(8,128)S(1)}) custom-call(f32[8]{0:T(128)} %table_hbm.1, s32[64,8,256]{2,1,0:T(8,128)} %facies_hbm.1, f32[64,8,256]{2,1,0:T(8,128)} %source_hbm.1), custom_call_target="tpu_custom_call" | custom-call | tf_op jit(solution)/shard_map/rows/pallas_call | solution.py:502
  1.5 4.6 %collective-permute-start.4 = (f32[80,8,256]{2,1,0:T(8,128)S(1)}, f32[80,8,256]{2,1,0:T(8,128)S(1)}, u32[]{:S(2)}, u32[]{:S(2)}) collective-permute-start(f32[80,8,256]{2,1,0:T(8,128)S(1)} %get-tuple-element.47), channel_id=1, source_target_pairs={{1,2},{2,1},{3,4},{4,3},{5,6},{6,5},{7,8},{8,7},{9,10},{10,9},{11,... | collective-permute-start | bytes 1966088 | tf_op jit(solution)/shard_map/ppermute | solution.py:515
  6.1 1.3 %collective-permute-start = (f32[7,8,256]{2,1,0:T(8,128)S(1)}, f32[7,8,256]{2,1,0:T(8,128)S(1)}, u32[]{:S(2)}, u32[]{:S(2)}) collective-permute-start(f32[7,8,256]{2,1,0:T(8,128)S(1)} %get-tuple-element.38), channel_id=1, source_target_pairs={{256,0},{512,256},{768,512},{257,1},{513,257},{769,513},{258,2},{5... | collective-permute-start | bytes 172040 | tf_op jit(solution)/shard_map/ppermute | solution.py:519
  7.4 4.0 %collective-permute-start.1 = (f32[7,8,256]{2,1,0:T(8,128)S(1)}, f32[7,8,256]{2,1,0:T(8,128)S(1)}, u32[]{:S(2)}, u32[]{:S(2)}) collective-permute-start(f32[7,8,256]{2,1,0:T(8,128)S(1)} %get-tuple-element.39), channel_id=1, source_target_pairs={{0,256},{256,512},{512,768},{1,257},{257,513},{513,769},{2,258},{2... | collective-permute-start | bytes 172040 | tf_op jit(solution)/shard_map/ppermute | solution.py:518
  11.4 0.5 own.1
  12.0 0.0 collective-permute-done.begin_ref
  12.0 0.7 collective-permute-done.1.end_ref
  12.7 13.3 %collective-permute-start.2 = (f32[70,8,256]{2,1,0:T(8,128)S(1)}, f32[70,8,256]{2,1,0:T(8,128)S(1)}, u32[]{:S(2)}, u32[]{:S(2)}) collective-permute-start(f32[70,8,256]{2,1,0:T(8,128)S(1)} %get-tuple-element.45), channel_id=1, source_target_pairs={{0,1},{1,0},{2,3},{3,2},{4,5},{5,4},{6,7},{7,6},{8,9},{9,8},{10,11... | collective-permute-start | bytes 1720328 | tf_op jit(solution)/shard_map/ppermute | solution.py:530
  26.0 1.9 %collective-permute-start.3 = (f32[6,8,256]{2,1,0:T(8,128)S(1)}, f32[6,8,256]{2,1,0:T(8,128)S(1)}, u32[]{:S(2)}, u32[]{:S(2)}) collective-permute-start(f32[6,8,256]{2,1,0:T(8,128)S(1)} %get-tuple-element.46), channel_id=1, source_target_pairs={{1,2},{2,1},{3,4},{4,3},{5,6},{6,5},{7,8},{8,7},{9,10},{10,9},{11,... | collective-permute-start | bytes 147464 | tf_op jit(solution)/shard_map/ppermute | solution.py:531
  27.9 0.0 collective-permute-done.2.near_ref
  27.9 0.0 collective-permute-done.4.far_ref
  27.9 2.7 %middle.1 = (f32[32,256]{1,0:T(8,128)S(1)}, f32[72,16,256]{2,1,0:T(8,128)S(1)}, f32[72,16,256]{2,1,0:T(8,128)S(1)}, f32[72,16,256]{2,1,0:T(8,128)S(1)}, f32[72,1...) custom-call(f32[64,8,256]{2,1,0:T(8,128)S(1)} %get-tuple-element.36., ...), custom_call_target="tpu_custom_call", output_to_operand_aliasing={{2}: (4, {}), {4}: (5, {}), {5}: (6, {})} | custom-call | tf_op jit(solution)/shard_map/middle/pallas_call | solution.py:532
  30.7 0.7 collective-permute-done.3.corner_ref
  31.4 0.5 edges.1
  31.9 12.2 %all_to_all.10.part_ref = f32[32,1,128]{2,1,0:T(1,128)S(1)} all-to-all(f32[32,1,128]{2,1,0:T(1,128)S(1)} %get-tuple-element.60), channel_id=1, replica_groups=mesh['group'=4,'z'=16,'y'=8,'core'=2] {'group','y'}, dimensions={0} | all-to-all | bytes 32768 | tf_op jit(solution)/shard_map/all_to_all | solution.py:491
  44.1 28.6 %all_to_all.11.sums_ref = f32[32,1,128]{2,1,0:T(1,128)S(1)} all-to-all(f32[32,1,128]{2,1,0:T(1,128)S(1)} %merge.1), channel_id=1, replica_groups=mesh['group'=4,'z'=16,'y'=8,'core'=2] {'z','core'}, dimensions={0} | all-to-all | bytes 32768 | tf_op jit(solution)/shard_map/all_to_all | solution.py:491
  72.8 3.8 %last.1 = f32[64,8,256]{2,1,0:T(8,128)} custom-call(f32[32,1,128]{2,1,0:T(1,128)S(1)} %all_to_all.11.sums_ref, f32[72,16,256]{2,1,0:T(8,128)S(1)} %get-tuple-element.61.v_ref, f32[72,16,256]{2,1,0:T(8,128)S(1)} %get-tuple-element.62.tx_ref, f32[72,16,256]{2,1,0:T(8,128)S(1)} %get-tuple-element.63.ty_ref, f32[72,16,256]{2,1,0:T(8,128)S(1)} %get-tuple-element.64.tz_ref, ...), custom_call_target="tpu_custom_call" | custom-call | tf_op jit(solution)/shard_map/last/pallas_call | solution.py:552
  (3 shorter events, 0.1 us)
Async XLA Ops:
  1.5 26.4 %collective-permute-start.4 = (f32[80,8,256]{2,1,0:T(8,128)S(1)}, f32[80,8,256]{2,1,0:T(8,128)S(1)}, u32[]{:S(2)}, u32[]{:S(2)}) collective-permute-start(f32[80,8,256]{2,1,0:T(8,128)S(1)} %get-tuple-element.47), channel_id=1, source_target_pairs={{1,2},{2,1},{3,4},{4,3},{5,6},{6,5},{7,8},{8,7},{9,10},{10,9},{11,... | collective-permute-start | bytes 1966088 | tf_op jit(solution)/shard_map/ppermute | solution.py:515
  6.1 5.8 %collective-permute-start = (f32[7,8,256]{2,1,0:T(8,128)S(1)}, f32[7,8,256]{2,1,0:T(8,128)S(1)}, u32[]{:S(2)}, u32[]{:S(2)}) collective-permute-start(f32[7,8,256]{2,1,0:T(8,128)S(1)} %get-tuple-element.38), channel_id=1, source_target_pairs={{256,0},{512,256},{768,512},{257,1},{513,257},{769,513},{258,2},{5... | collective-permute-start | bytes 172040 | tf_op jit(solution)/shard_map/ppermute | solution.py:519
  7.4 5.2 %collective-permute-start.1 = (f32[7,8,256]{2,1,0:T(8,128)S(1)}, f32[7,8,256]{2,1,0:T(8,128)S(1)}, u32[]{:S(2)}, u32[]{:S(2)}) collective-permute-start(f32[7,8,256]{2,1,0:T(8,128)S(1)} %get-tuple-element.39), channel_id=1, source_target_pairs={{0,256},{256,512},{512,768},{1,257},{257,513},{513,769},{2,258},{2... | collective-permute-start | bytes 172040 | tf_op jit(solution)/shard_map/ppermute | solution.py:518
  12.7 15.2 %collective-permute-start.2 = (f32[70,8,256]{2,1,0:T(8,128)S(1)}, f32[70,8,256]{2,1,0:T(8,128)S(1)}, u32[]{:S(2)}, u32[]{:S(2)}) collective-permute-start(f32[70,8,256]{2,1,0:T(8,128)S(1)} %get-tuple-element.45), channel_id=1, source_target_pairs={{0,1},{1,0},{2,3},{3,2},{4,5},{5,4},{6,7},{7,6},{8,9},{9,8},{10,11... | collective-permute-start | bytes 1720328 | tf_op jit(solution)/shard_map/ppermute | solution.py:530
  26.0 5.4 %collective-permute-start.3 = (f32[6,8,256]{2,1,0:T(8,128)S(1)}, f32[6,8,256]{2,1,0:T(8,128)S(1)}, u32[]{:S(2)}, u32[]{:S(2)}) collective-permute-start(f32[6,8,256]{2,1,0:T(8,128)S(1)} %get-tuple-element.46), channel_id=1, source_target_pairs={{1,2},{2,1},{3,4},{4,3},{5,6},{6,5},{7,8},{8,7},{9,10},{10,9},{11,... | collective-permute-start | bytes 147464 | tf_op jit(solution)/shard_map/ppermute | solution.py:531
